TPU v7x, 32 devices: a whole 2x2x4 slice. The times are simulated.
32 devices in a mesh: slab: 2 (over y), ma: 4 (over z), freq: 2 (over x), pol: 2 (over core).
Axes of the slice: x: 2, y: 2, z: 4, core: 2. Of those that a mesh axis runs over, the one named last changes fastest.
Arguments:
- visibility: bfloat16 [16, 2, 64, 8192], P(('slab', 'freq'), None, 'pol', 'ma'), parts along dimension 0, may hold values from -6 to 6
- beam_rows: bfloat16 [16, 64, 768], P(('slab', 'freq'), 'pol'), parts along dimension 0, may hold values from -0.4375 to 0.4375
- mode_gain: float32 [192, 768], P('ma'), may hold values from 0.7 to 1.5
- harmonic_basis: bfloat16 [768, 768], replicated, may hold values from -0.21875 to 0.21875
- step_size: float32 [16], P(('slab', 'freq')), parts along dimension 0, may hold values from 0.15 to 0.25
- kl_matrix: bfloat16 [4, 8], P('slab'), parts along dimension 0, may hold values from -2 to 2
Outputs:
- filtered: bfloat16 [192, 4, 2, 768], P('ma', ('slab', 'freq'), 'pol'), parts along dimension 1
There are 2 independent parts, one for each index of `slab`. A program takes and returns all parts, laid end to end along the dimension named above; an argument that names none is the same for every part. Nothing has to cross between parts.
All inputs are finite; a program needn't handle non-finite values.
Results may differ from a plain program's by a relative error of at most 0.0088.
Values may be sent and summed in bfloat16 or wider, within the bound.
No kernel may reach another device: no remote copies, remote signals or barrier semaphores. Data moves between devices by JAX's collectives and lax.ppermute only.
A program may use at most 64 MiB of HBM per device.

v0:
```python
import jax
import jax.numpy as jnp
from jax import lax
from jax.sharding import PartitionSpec as P

NT = 8192
ITERS = 2


def spectral_tables(time_index, mode_index, total):
    phase = time_index[:, None] * mode_index[None, :] % total
    angle = phase.astype(jnp.float32) * (2.0 * jnp.pi / total)
    return (jnp.cos(angle).astype(jnp.bfloat16), jnp.sin(angle).astype(jnp.bfloat16))


def transform_block(samples, cosine, sine):
    nfreq, nparts, nbase, ntime = samples.shape
    flat = samples.reshape(nfreq * nparts * nbase, ntime)
    width = cosine.shape[1]
    first = jnp.dot(flat, cosine, preferred_element_type=jnp.float32).reshape(
        nfreq, 2, nbase, width
    )
    second = jnp.dot(flat, sine, preferred_element_type=jnp.float32).reshape(nfreq, 2, nbase, width)
    return jnp.stack([first[:, 0] + second[:, 1], first[:, 1] - second[:, 0]], axis=1)


def on_device(visibility, beam_rows, mode_gain, harmonic_basis, step_size, kl_matrix):
    local_modes = mode_gain.shape[0]
    local_time = visibility.shape[3]
    degrees = harmonic_basis.shape[1]
    norm_scale = NT ** (-0.5)
    time_index = lax.axis_index("ma") * local_time + jnp.arange(local_time, dtype=jnp.int32)
    mode_index = jnp.arange(local_modes * lax.axis_size("ma"), dtype=jnp.int32)
    cosine, sine = spectral_tables(time_index, mode_index, NT)
    spectrum = lax.psum_scatter(
        transform_block(visibility, cosine, sine).transpose(3, 0, 1, 2),
        "ma",
        scatter_dimension=0,
        tiled=True,
    )
    modes = (spectrum * norm_scale).astype(jnp.bfloat16)
    mode_ids = lax.axis_index("ma") * local_modes + jnp.arange(local_modes, dtype=jnp.int32)
    mask = (jnp.arange(degrees, dtype=jnp.int32)[None, :] >= mode_ids[:, None]).astype(jnp.float32)
    gain = mode_gain[:, None, None, :]

    def back(signal, rows):
        total = jnp.einsum("mfpb,fbk->mfpk", signal, rows, preferred_element_type=jnp.float32)
        scaled = (total * gain).astype(jnp.bfloat16)
        result = jnp.dot(
            scaled.reshape(-1, degrees), harmonic_basis, preferred_element_type=jnp.float32
        )
        return result.reshape(scaled.shape) * mask[:, None, None, :]

    rows = lax.all_gather(beam_rows, "pol", axis=1, tiled=True)
    signal = lax.all_to_all(modes, "pol", split_axis=2, concat_axis=3, tiled=True)
    dirty = back(signal, rows)
    stepping = step_size[None, :, None, None]
    estimate = stepping * dirty
    for counter in range(ITERS):
        rounded = estimate.astype(jnp.bfloat16)
        sampled = jnp.einsum(
            "mfpl,kl->mfpk", rounded, harmonic_basis, preferred_element_type=jnp.float32
        )
        fore_scaled = (sampled * gain).astype(jnp.bfloat16)
        estimate = estimate + stepping * (
            dirty
            - back(
                jnp.einsum(
                    "mfpk,fbk->mfpb", fore_scaled, rows, preferred_element_type=jnp.float32
                ).astype(jnp.bfloat16),
                rows,
            )
        )
    rounded = estimate.astype(jnp.bfloat16)
    local_freqs = step_size.shape[0]
    columns = lax.dynamic_slice_in_dim(
        kl_matrix, lax.axis_index("freq") * local_freqs, local_freqs, 1
    )
    terms = jnp.einsum("jf,mfpl->mjpl", columns, rounded, preferred_element_type=jnp.float32)
    filtered = lax.psum_scatter(terms, "freq", scatter_dimension=1, tiled=True).astype(jnp.bfloat16)
    return filtered


def solution(mesh):
    placed = (
        P(("slab", "freq"), None, "pol", "ma"),
        P(("slab", "freq"), "pol", None),
        P("ma", None),
        P(),
        P(("slab", "freq")),
        P("slab", None),
    )
    return jax.shard_map(
        on_device,
        mesh=mesh,
        in_specs=placed,
        out_specs=P("ma", ("slab", "freq"), "pol", None),
        check_vma=False,
    )
```

profile of v0, /device:TPU:0, one launch (start us, length us, event | category | flops | bytes accessed | tf_op | source)
XLA Modules:
  0.0 77.7 jit_solution(14288232921664229300)
XLA Ops:
  6.5 0.0 copy-start
  6.5 0.0 reduce-scatter.7.cloned.1.call-start
  6.6 11.0 %convolution_bitcast_fusion.4 = f32[256,192]{0,1:T(8,128)S(1)} fusion(bf16[256,2048]{1,0:T(8,128)(2,1)} %bitcast.132, s32[2048]{0:T(1024)S(1)} %iota_add_fusion), kind=kOutput, calls=%fused_computation.45 | convolution fusion | flops 207224832 | bytes 1253376 | tf_op jit(solution)/shard_map/dot_general | solution.py:23
  17.5 7.9 %convolution_bitcast_fusion.5 = f32[256,192]{0,1:T(8,128)S(1)} fusion(bf16[256,2048]{1,0:T(8,128)(2,1)S(1)} %bitcast.133, s32[2048]{0:T(1024)S(1)} %iota_add_fusion), kind=kOutput, calls=%fused_computation.46 | convolution fusion | flops 207224832 | bytes 1253376 | tf_op jit(solution)/shard_map/dot_general | solution.py:20
  25.5 0.1 copy.16
  25.6 0.0 copy-start.2
  25.6 0.1 copy.15
  25.8 0.0 copy-start.1
  25.9 0.8 %copy.25 = f32[192,256]{1,0:T(8,128)} copy(f32[192,256]{0,1:T(8,128)S(1)} %bitcast.128) | data formatting | bytes 393216
  26.6 0.0 reduce-scatter.7.cloned.1.call-update
  26.7 0.0 reduce-scatter.5.cloned.1.call-start
  26.7 2.2 %all_gather.3 = bf16[4,64,768]{2,1,0:T(8,128)(2,1)S(1)} all-gather(bf16[4,32,768]{2,1,0:T(8,128)(2,1)S(1)} %copy-done.2), channel_id=1, replica_groups=mesh['slab'=2,'ma'=4,'freq'=2,'pol'=2] {'pol'}, dimensions={1}, use_global_device_ids=true | all-gather | bytes 589824 | tf_op jit(solution)/shard_map/all_gather | solution.py:54
  28.9 0.1 fusion.59
  29.0 20.1 %reduce-scatter.7.cloned.1.call-done = f32[48,256]{1,0:T(8,128)} async-done(((f32[192,256]{1,0:T(8,128)}), f32[48,256]{1,0:T(8,128)}) %reduce-scatter.7.cloned.1.call-update) | async-done | bytes 49168
  49.1 0.9 %copy.26 = f32[48,256]{0,1:T(8,128)S(1)} copy(f32[48,256]{1,0:T(8,128)} %reduce-scatter.7.cloned.1.call-done) | data formatting | bytes 98304
  50.1 0.1 reshape.118
  50.2 3.7 %all_to_all.4 = bf16[2,2,3072]{2,1,0:T(2,128)(2,1)S(1)} all-to-all(bf16[2,2,3072]{2,1,0:T(2,128)(2,1)S(1)} %reshape.118), channel_id=1, replica_groups=mesh['slab'=2,'ma'=4,'freq'=2,'pol'=2] {'pol'}, dimensions={0} | all-to-all | bytes 49152 | tf_op jit(solution)/shard_map/all_to_all | solution.py:55
  53.9 0.1 reshape.119
  54.1 0.0 copy-start.3
  54.1 0.6 convolution_multiply_fusion.4
  54.7 0.0 copy-done.3
  54.7 0.8 %fusion.44 = bf16[48,4,64]{2,0,1:T(8,128)(2,1)S(1)} fusion(bf16[4,64,768]{2,1,0:T(8,128)(2,1)S(1)} %all_gather.3, bf16[768,768]{1,0:T(8,128)(2,1)S(1)} %copy-done, f32[48,4,768]{2,0,1:T(8,128)S(1)} %convolution_multiply_fusion.4, f32[48,768]{1,0:T(8,128)S(1)} %copy-done.1, f32[4]{0:T(128)S(1)} %copy-done.3), kind=kOutput, calls=%fused_computation.50 | convolution fusion | flops 245968896 | bytes 2334736 | tf_op jit(solution)/shard_map/mfpk,fbk->mfpb/dot_general | solution.py:68
  55.6 0.5 fusion.8
  56.1 0.8 %fusion.41 = bf16[48,4,64]{2,0,1:T(8,128)(2,1)S(1)} fusion(bf16[4,64,768]{2,1,0:T(8,128)(2,1)S(1)} %all_gather.3, bf16[768,768]{1,0:T(8,128)(2,1)S(1)} %copy-done, f32[48,4,768]{2,0,1:T(8,128)S(1)} %fusion.8, f32[48,768]{1,0:T(8,128)S(1)} %copy-done.1), kind=kOutput, calls=%fused_computation.49 | convolution fusion | flops 245821440 | bytes 2334720 | tf_op jit(solution)/shard_map/mfpk,fbk->mfpb/dot_general | solution.py:68
  57.0 0.0 copy-start.4
  57.0 0.5 fusion.15
  57.5 0.1 copy-done.4
  57.6 0.4 convolution_bitcast_fusion.3
  58.0 0.7 copy.21
  58.7 0.0 reduce-scatter.5.cloned.1.call-update
  58.8 10.5 %reduce-scatter.5.cloned.1.call-done = f32[48,1,1,768]{3,0,2,1:T(8,128)} async-done(((f32[48,2,1,768]{3,0,2,1:T(8,128)}), f32[48,1,1,768]{3,0,2,1:T(8,128)}) %reduce-scatter.5.cloned.1.call-update) | async-done | bytes 147472 | tf_op jit(solution)/shard_map/reduce_scatter | solution.py:80
  69.3 1.6 %convert_element_type.96 = bf16[48,1,1,768]{3,0,2,1:T(8,128)(2,1)} convert(f32[48,1,1,768]{3,0,2,1:T(8,128)} %reduce-scatter.5.cloned.1.call-done) | non-fusion elementwise | flops 36864 | bytes 221184 | tf_op jit(solution)/shard_map/convert_element_type | solution.py:80
  (11 shorter events, 0.1 us)
Async XLA Ops:
  6.5 47.5 %copy-start = (bf16[768,768]{1,0:T(8,128)(2,1)S(1)}, bf16[768,768]{1,0:T(8,128)(2,1)}, u32[]{:S(2)}) copy-start(bf16[768,768]{1,0:T(8,128)(2,1)} %param.9) | copy-start | bytes 3538948
  6.5 42.6 %reduce-scatter.7.cloned.1.call-start = ((), (), s32[]{:S(2)}) async-start(), calls=%async_computation.4 | async-start | bytes 245760
  6.5 11.0 %copy-start.5 = (bf16[4,2,32,2048]{3,2,1,0:T(8,128)(2,1)S(1)}, bf16[4,2,32,2048]{3,2,1,0:T(8,128)(2,1)}, u32[]{:S(2)}) copy-start(bf16[4,2,32,2048]{3,2,1,0:T(8,128)(2,1)} %param.6) | copy-start | bytes 3145732
  25.6 1.1 %copy-start.2 = (bf16[4,32,768]{2,1,0:T(8,128)(2,1)S(1)}, bf16[4,32,768]{2,1,0:T(8,128)(2,1)}, u32[]{:S(2)}) copy-start(bf16[4,32,768]{2,1,0:T(8,128)(2,1)} %param.7) | copy-start | bytes 589828
  25.8 28.2 %copy-start.1 = (f32[48,768]{1,0:T(8,128)S(1)}, f32[48,768]{1,0:T(8,128)}, u32[]{:S(2)}) copy-start(f32[48,768]{1,0:T(8,128)} %param.8) | copy-start | bytes 442372
  26.7 42.6 %reduce-scatter.5.cloned.1.call-start = ((), (), s32[]{:S(2)}) async-start(), calls=%async_computation.3 | async-start | bytes 442368 | tf_op jit(solution)/shard_map/reduce_scatter | solution.py:80
  54.1 0.7 copy-start.3
  57.0 0.7 copy-start.4
Sparse Core Ops, SparseCore 0:
  26.8 22.3 reduce-scatter.6
  58.9 10.3 reduce-scatter.4
where the time goes:
time: 77.9 us; the launch traced here: 77.7 us
  waiting for transfers between devices  30.7 us (39%)
  matrix products  22.6 us (29%)
  between operations  13.6 us (17%)
  blocking collectives  5.94 us (8%)
  local copies, waits for them, and re-layouts  3.12 us (4%)
  other arithmetic  1.71 us (2%)
    unnamed x3, waiting for transfers between devices  20.1 us
    dot_general x1, matrix products, transform_block(): jnp.dot(flat, sine, preferred_element_type=jnp.float32)  11 us
    reduce_scatter x1, waiting for transfers between devices, on_device(): lax.psum_scatter(terms, 'freq', scatter_dimension=1, tiled=True)  10.5 us
    dot_general x1, matrix products, transform_block(): jnp.dot(flat, cosine, preferred_element_type=jnp.float32)  7.93 us
    all_to_all x1, blocking collectives, on_device(): lax.all_to_all(modes, 'pol', split_axis=2, concat_axis=3, tiled=True)  3.74 us
    all_gather x1, blocking collectives, on_device(): rows = lax.all_gather(beam_rows, 'pol', axis=1, tiled=True)  2.21 us
    unnamed x16, local copies, waits for them, and re-layouts  2.13 us
    dot_general x2, matrix products, on_device(): jnp.einsum('mfpk,fbk->mfpb', fore_scaled, rows, preferred_element_type=jn...  1.68 us
  transfers between devices with their start and end apart: 2, of which 2 were waited for; matrix products, arithmetic and copies ran while one was open for 0% of the time, Pallas kernels for 0%

commit v1 on v0

v1 whole, which is shorter than its diff:
```python
import functools
import math

import jax
import jax.numpy as jnp
import numpy as np
from jax import lax
from jax.experimental import pallas as pl
from jax.experimental.pallas import tpu as pltpu
from jax.sharding import PartitionSpec as P

NT = 8192
ITERS = 2
LANES = 128
NT_DIMS = (((1,), (1,)), ((), ()))
VMEM = pl.BlockSpec(memory_space=pltpu.VMEM)
SMEM = pl.BlockSpec(memory_space=pltpu.SMEM)


def partner_of(index, step, size):
    if size & (size - 1) == 0:
        return index ^ step, index ^ step
    return (index + step) % size, (index + size - step) % size


def exchange(array, axis, size, step):
    pairs = [(i, partner_of(i, step, size)[0]) for i in range(size)]
    return lax.ppermute(array, axis, pairs)


def phase_tables(modes, local_time, blocks):
    m = np.arange(modes, dtype=np.int64)[:, None]
    groups = local_time // LANES
    coarse = (m * np.arange(groups) * LANES) % NT
    origin = (m * np.arange(blocks) * local_time) % NT
    fine = (m * np.arange(LANES)) % NT
    unit = 2.0 * np.pi / NT
    columns = np.concatenate(
        [np.cos(coarse * unit), np.sin(coarse * unit), np.cos(origin * unit), np.sin(origin * unit)], axis=1
    )
    columns = np.pad(columns, ((0, 0), (0, -columns.shape[1] % LANES)))
    tables = (columns, np.cos(fine * unit), np.sin(fine * unit))
    return tuple(jnp.asarray(t.astype(np.float32)) for t in tables)


def transform_kernel(blocks, vis_ref, col_ref, fc_ref, fs_ref, own_ref, other_ref, cos_ref, sin_ref):
    nfreq, _, nbase, ntime = vis_ref.shape
    groups = ntime // LANES
    modes = col_ref.shape[0]
    block, part = lax.axis_index("ma"), lax.axis_index("pol")
    lane = lax.broadcasted_iota(jnp.int32, col_ref.shape, 1)
    columns = col_ref[...]
    oc = jnp.sum(jnp.where(lane == 2 * groups + block, columns, 0.0), axis=1, keepdims=True)
    os = jnp.sum(jnp.where(lane == 2 * groups + blocks + block, columns, 0.0), axis=1, keepdims=True)
    fc = fc_ref[...] * oc - fs_ref[...] * os
    fs = fs_ref[...] * oc + fc_ref[...] * os
    for u in range(groups):
        cc = columns[:, u : u + 1]
        cs = columns[:, groups + u : groups + u + 1]
        cos_ref[:, u * LANES : (u + 1) * LANES] = (cc * fc - cs * fs).astype(jnp.bfloat16)
        sin_ref[:, u * LANES : (u + 1) * LANES] = (cs * fc + cc * fs).astype(jnp.bfloat16)
    mine = vis_ref[:, part].reshape(nfreq * nbase, ntime)
    theirs = vis_ref[:, 1 - part].reshape(nfreq * nbase, ntime)
    both = jnp.concatenate([mine, theirs], axis=0)
    c = lax.dot_general(cos_ref[...], both, NT_DIMS, preferred_element_type=jnp.float32)
    s = lax.dot_general(sin_ref[...], both, NT_DIMS, preferred_element_type=jnp.float32)
    sign = (1 - 2 * part).astype(jnp.float32)
    scale = NT ** (-0.5)
    n = nfreq * nbase
    own_ref[...] = ((c[:, :n] + sign * s[:, n:]) * scale).astype(own_ref.dtype)
    other_ref[...] = ((c[:, n:] - sign * s[:, :n]) * scale).astype(other_ref.dtype)


def merge_kernel(blocks, own_ref, other_ref, *out_refs):
    rows, n = out_refs[0].shape[0], own_ref.shape[1]
    me = lax.axis_index("ma")
    for step, out_ref in enumerate(out_refs):
        to = partner_of(me, step, blocks)[0]
        at = pl.ds(pl.multiple_of(to * rows, 16), rows)
        out_ref[:, :n] = own_ref[at, :]
        out_ref[:, n:] = other_ref[at, :]


def solve_kernel(blocks, nf_blocks, *refs):
    parts = refs[:blocks]
    rows_own, rows_other, gain_ref, basis_ref, step_ref, kl_ref = refs[blocks : blocks + 6]
    terms = refs[blocks + 6 : blocks + 6 + nf_blocks]
    beam, dirty, estimate = refs[blocks + 6 + nf_blocks :]
    nfreq, nbase, degrees = rows_own.shape
    modes = gain_ref.shape[0]
    n = nfreq * nbase
    beam[:n, :] = rows_own[...].reshape(n, degrees)
    beam[n:, :] = rows_other[...].reshape(n, degrees)
    total = parts[0][...].astype(jnp.float32)
    for part in parts[1:]:
        total = total + part[...].astype(jnp.float32)
    base = (lax.broadcasted_iota(jnp.int32, (modes, 2 * n), 1) % n) // nbase
    keep = jnp.concatenate([base == f for f in range(nfreq)], axis=0)
    signal = jnp.where(keep, jnp.concatenate([total] * nfreq, axis=0), 0.0).astype(jnp.bfloat16)
    ids = lax.axis_index("ma") * modes + lax.broadcasted_iota(jnp.int32, (modes, degrees), 0)
    mask = lax.broadcasted_iota(jnp.int32, (modes, degrees), 1) >= ids

    def scaled(values):
        return jnp.concatenate(
            [(values[f * modes : (f + 1) * modes] * gain_ref[...]).astype(jnp.bfloat16) for f in range(nfreq)], axis=0
        )

    def back(signal):
        h = scaled(jnp.dot(signal, beam[...], preferred_element_type=jnp.float32))
        return jnp.dot(h, basis_ref[...], preferred_element_type=jnp.float32)

    def fore(coeffs):
        e = lax.dot_general(coeffs, basis_ref[...], NT_DIMS, preferred_element_type=jnp.float32)
        s = lax.dot_general(scaled(e), beam[...], NT_DIMS, preferred_element_type=jnp.float32)
        return jnp.where(keep, s, 0.0).astype(jnp.bfloat16)

    def rounded():
        return jnp.concatenate(
            [estimate[f * modes : (f + 1) * modes].astype(jnp.bfloat16) for f in range(nfreq)], axis=0
        )

    first = back(signal)
    for f in range(nfreq):
        at = slice(f * modes, (f + 1) * modes)
        d = jnp.where(mask, first[at], 0.0)
        dirty[at] = d
        estimate[at] = step_ref[f] * d
    for _ in range(ITERS):
        again = back(fore(rounded()))
        for f in range(nfreq):
            at = slice(f * modes, (f + 1) * modes)
            estimate[at] = estimate[at] + step_ref[f] * (dirty[at] - jnp.where(mask, again[at], 0.0))
    here = lax.axis_index("freq")
    kl = kl_ref[...].astype(jnp.float32)
    kl_row = lax.broadcasted_iota(jnp.int32, kl.shape, 0)
    kl_col = lax.broadcasted_iota(jnp.int32, kl.shape, 1)
    kept = kl.shape[0] // nf_blocks
    final = rounded().astype(jnp.float32)
    for step, out_ref in enumerate(terms):
        to = partner_of(here, step, nf_blocks)[0]
        for j in range(kept):
            acc = None
            for f in range(nfreq):
                hit = (kl_row == to * kept + j) & (kl_col == here * nfreq + f)
                weight = jnp.sum(jnp.where(hit, kl, 0.0), keepdims=True)
                term = weight * final[f * modes : (f + 1) * modes]
                acc = term if acc is None else acc + term
            out_ref[j] = acc.astype(out_ref.dtype)


def on_device(sizes, visibility, beam_rows, mode_gain, harmonic_basis, step_size, kl_matrix):
    blocks, nf_blocks = sizes["ma"], sizes["freq"]
    nfreq, _, nbase, ntime = visibility.shape
    local_modes, degrees = mode_gain.shape
    modes = local_modes * blocks
    n = nfreq * nbase
    shape = jax.ShapeDtypeStruct
    other_rows = exchange(beam_rows, "pol", 2, 1)
    columns, fc, fs = phase_tables(modes, ntime, blocks)
    own, other = pl.pallas_call(
        functools.partial(transform_kernel, blocks),
        out_shape=[shape((modes, n), jnp.bfloat16)] * 2,
        in_specs=[VMEM] * 4,
        out_specs=[VMEM] * 2,
        scratch_shapes=[pltpu.VMEM((modes, ntime), jnp.bfloat16)] * 2,
        compiler_params=pltpu.CompilerParams(vmem_limit_bytes=20 << 20),
        name="transform",
    )(visibility, columns, fc, fs)
    other = exchange(other, "pol", 2, 1)
    mine = pl.pallas_call(
        functools.partial(merge_kernel, blocks),
        out_shape=[shape((local_modes, 2 * n), jnp.bfloat16)] * blocks,
        in_specs=[VMEM] * 2,
        out_specs=[VMEM] * blocks,
        compiler_params=pltpu.CompilerParams(vmem_limit_bytes=16 << 20),
        name="merge",
    )(own, other)
    parts = [mine[0]] + [exchange(mine[k], "ma", blocks, k) for k in range(1, blocks)]
    kept = kl_matrix.shape[0] // nf_blocks
    terms = pl.pallas_call(
        functools.partial(solve_kernel, blocks, nf_blocks),
        out_shape=[shape((kept, local_modes, degrees), jnp.float32)]
        + [shape((kept, local_modes, degrees), jnp.bfloat16)] * (nf_blocks - 1),
        in_specs=[VMEM] * (blocks + 4) + [SMEM, VMEM],
        out_specs=[VMEM] * nf_blocks,
        scratch_shapes=[
            pltpu.VMEM((2 * n, degrees), jnp.bfloat16),
            pltpu.VMEM((nfreq * local_modes, degrees), jnp.float32),
            pltpu.VMEM((nfreq * local_modes, degrees), jnp.float32),
        ],
        compiler_params=pltpu.CompilerParams(vmem_limit_bytes=24 << 20),
        name="solve",
    )(*parts, beam_rows, other_rows, mode_gain, harmonic_basis, step_size, kl_matrix)
    total = terms[0]
    for k in range(1, nf_blocks):
        total = total + exchange(terms[k], "freq", nf_blocks, k).astype(jnp.float32)
    return total.astype(jnp.bfloat16).transpose(1, 0, 2)[:, :, None, :]


def solution(mesh):
    placed = (
        P(("slab", "freq"), None, "pol", "ma"),
        P(("slab", "freq"), "pol", None),
        P("ma", None),
        P(),
        P(("slab", "freq")),
        P("slab", None),
    )
    return jax.shard_map(
        functools.partial(on_device, dict(mesh.shape)),
        mesh=mesh,
        in_specs=placed,
        out_specs=P("ma", ("slab", "freq"), "pol", None),
        check_vma=False,
    )
```

time: 77.9 us -> 27.5 us (0.35)
  matrix products: 22.6 us -> 0 us
  waiting for transfers between devices: 30.7 us -> 9.6 us
  between operations: 13.6 us -> 0.06 us
  starting transfers between devices: 0.04 us -> 7.6 us
  blocking collectives: 5.94 us -> 0 us
  Pallas kernels: 0 us -> 4.49 us
  local copies, waits for them, and re-layouts: 3.12 us -> 4.82 us
  other arithmetic: 1.71 us -> 0.65 us
    dot_general x8 -> x0, matrix products: 22.6 us -> none  [the longest x1 11 us: transform_block(): jnp.dot(flat, sine, preferred_element_type=jnp.float32)]
    unnamed x3 -> x0, waiting for transfers between devices: 20.1 us -> none
    reduce_scatter x1 -> x0, waiting for transfers between devices: 10.5 us -> none  [on_device(): lax.psum_scatter(terms, 'freq', scatter_dimension=1, tiled=True)]
    ppermute x0 -> x6, waiting for transfers between devices: none -> 9.6 us  [exchange(): return lax.ppermute(array, axis, pairs)]
    ppermute x0 -> x6, starting transfers between devices: none -> 7.6 us  [exchange(): return lax.ppermute(array, axis, pairs)]
    pallas_call x0 -> x3, Pallas kernels: none -> 4.49 us  [the longest x1 3.06 us: on_device(): pl.pallas_call(functools.partial(solve_kernel, blocks, nf_blocks), out_sh...]
    all_to_all x1 -> x0, blocking collectives: 3.74 us -> none  [on_device(): lax.all_to_all(modes, 'pol', split_axis=2, concat_axis=3, tiled=True)]
    unnamed x16 -> x18, local copies, waits for them, and re-layouts: 2.13 us -> 4.82 us
  transfers between devices with their start and end apart: 2 -> 6, of which waited for: 2 -> 4; matrix products, arithmetic and copies ran while one was open for 0% -> 0% of each run, Pallas kernels for 0% -> 5%
where the time goes in v1:
time: 27.5 us; the launch traced here: 27.2 us
  waiting for transfers between devices  9.6 us (35%)
  starting transfers between devices  7.6 us (28%)
  local copies, waits for them, and re-layouts  4.82 us (18%)
  Pallas kernels  4.49 us (16%)
  other arithmetic  0.65 us (2%)
    ppermute x6, waiting for transfers between devices, exchange(): return lax.ppermute(array, axis, pairs)  9.6 us
    ppermute x6, starting transfers between devices, exchange(): return lax.ppermute(array, axis, pairs)  7.6 us
    unnamed x18, local copies, waits for them, and re-layouts  4.82 us
    pallas_call x1, Pallas kernels, on_device(): pl.pallas_call(functools.partial(solve_kernel, blocks, nf_blocks), out_sh...  3.06 us
    pallas_call x1, Pallas kernels, on_device(): pl.pallas_call(functools.partial(transform_kernel, blocks), out_shape=[sh...  1.41 us
    another operation x1, other arithmetic, on_device(): return total.astype(jnp.bfloat16).transpose(1, 0, 2)[:, :, None, :]  0.65 us
  transfers between devices with their start and end apart: 6, of which 4 were waited for; matrix products, arithmetic and copies ran while one was open for 0% of the time, Pallas kernels for 5%

profile of v1, /device:TPU:0, one launch (start us, length us, event | category | flops | bytes accessed | tf_op | source)
XLA Modules:
  0.0 27.2 jit_solution(14823244171609633143)
XLA Ops:
  0.0 0.0 copy-start
  0.0 0.5 %collective-permute-start.4 = (bf16[4,32,768]{2,1,0:T(8,128)(2,1)}, bf16[4,32,768]{2,1,0:T(8,128)(2,1)S(1)}, u32[]{:S(2)}, u32[]{:S(2)}) collective-permute-start(bf16[4,32,768]{2,1,0:T(8,128)(2,1)} %refs_4_.1), channel_id=1, source_target_pairs={{0,1},{1,0},{2,3},{3,2},{4,5},{5,4},{6,7},{7,6},{8,9},{9,8},{10,11... | collective-permute-start | bytes 589832 | tf_op jit(solution)/shard_map/ppermute | solution.py:28
  0.5 0.0 copy-start.1
  0.5 1.2 %copy-done.1 = bf16[4,2,32,2048]{3,2,1,0:T(8,128)(2,1)S(1)} copy-done((bf16[4,2,32,2048]{3,2,1,0:T(8,128)(2,1)S(1)}, bf16[4,2,32,2048]{3,2,1,0:T(8,128)(2,1)}, u32[]{:S(2)}) %copy-start.1) | copy-done | bytes 1048600
  1.7 0.0 copy-start.4
  1.7 0.9 %copy-done.4 = f32[192,128]{1,0:T(8,128)S(1)} copy-done((f32[192,128]{1,0:T(8,128)S(1)}, f32[192,128]{1,0:T(8,128)}, u32[]{:S(2)}) %copy-start.4) | copy-done | bytes 98328
  2.6 0.0 copy-start.5
  2.6 0.9 %copy-done.5 = f32[192,128]{1,0:T(8,128)S(1)} copy-done((f32[192,128]{1,0:T(8,128)S(1)}, f32[192,128]{1,0:T(8,128)}, u32[]{:S(2)}) %copy-start.5) | copy-done | bytes 98328
  3.5 0.0 copy-start.6
  3.5 0.9 %copy-done.6 = f32[192,128]{1,0:T(8,128)S(1)} copy-done((f32[192,128]{1,0:T(8,128)S(1)}, f32[192,128]{1,0:T(8,128)}, u32[]{:S(2)}) %copy-start.6) | copy-done | bytes 98328
  4.4 0.0 copy-start.2
  4.4 0.0 copy-start.7
  4.4 1.4 %transform.1 = (bf16[192,128]{1,0:T(8,128)(2,1)S(1)}, bf16[192,128]{1,0:T(8,128)(2,1)S(1)}) custom-call(bf16[4,2,32,2048]{3,2,1,0:T(8,128)(2,1)S(1)} %copy-done.1, f32[192,128]{1,0:T(8,128)S(1)} %copy-done.6, f32[192,128]{1,0:T(8,128)S(1)} %copy-done.5, f32[192,128]{1,0:T(8,128)S(1)} %copy-done.4), custom_call_target="tpu_custom_call" | custom-call | tf_op jit(solution)/shard_map/transform/pallas_call | solution.py:160
  5.8 0.2 collective-permute-start
  6.0 1.1 %collective-permute-done.other_ref = bf16[192,128]{1,0:T(8,128)(2,1)S(1)} collective-permute-done((bf16[192,128]{1,0:T(8,128)(2,1)S(1)}, bf16[192,128]{1,0:T(8,128)(2,1)S(1)}, u32[]{:S(2)}, u32[]{:S(2)}) %collective-permute-start) | collective-permute-done | bytes 49184 | tf_op jit(solution)/shard_map/ppermute | solution.py:28
  7.1 2.8 %collective-permute-start.1 = (bf16[48,256]{1,0:T(8,128)(2,1)S(1)}, bf16[48,256]{1,0:T(8,128)(2,1)S(1)}, u32[]{:S(2)}, u32[]{:S(2)}) collective-permute-start(bf16[48,256]{1,0:T(8,128)(2,1)S(1)} %get-tuple-element.16), channel_id=1, source_target_pairs={{0,4},{4,0},{8,12},{12,8},{1,5},{5,1},{9,13},{13,9},{2,6},{6,2},{1... | collective-permute-start | bytes 73736 | tf_op jit(solution)/shard_map/ppermute | solution.py:28
  9.9 2.6 %collective-permute-start.2 = (bf16[48,256]{1,0:T(8,128)(2,1)S(1)}, bf16[48,256]{1,0:T(8,128)(2,1)S(1)}, u32[]{:S(2)}, u32[]{:S(2)}) collective-permute-start(bf16[48,256]{1,0:T(8,128)(2,1)S(1)} %get-tuple-element.17), channel_id=1, source_target_pairs={{0,8},{4,12},{8,0},{12,4},{1,9},{5,13},{9,1},{13,5},{2,10},{6,14},... | collective-permute-start | bytes 73736 | tf_op jit(solution)/shard_map/ppermute | solution.py:28
  12.5 0.0 collective-permute-start.3
  12.5 0.0 collective-permute-done.1.refs_1_
  12.5 2.2 %collective-permute-done.2.refs_2_ = bf16[48,256]{1,0:T(8,128)(2,1)S(1)} collective-permute-done((bf16[48,256]{1,0:T(8,128)(2,1)S(1)}, bf16[48,256]{1,0:T(8,128)(2,1)S(1)}, u32[]{:S(2)}, u32[]{:S(2)}) %collective-permute-start.2) | collective-permute-done | bytes 24608 | tf_op jit(solution)/shard_map/ppermute | solution.py:28
  14.7 3.4 %collective-permute-done.3.refs_3_ = bf16[48,256]{1,0:T(8,128)(2,1)S(1)} collective-permute-done((bf16[48,256]{1,0:T(8,128)(2,1)S(1)}, bf16[48,256]{1,0:T(8,128)(2,1)S(1)}, u32[]{:S(2)}, u32[]{:S(2)}) %collective-permute-start.3) | collective-permute-done | bytes 24608 | tf_op jit(solution)/shard_map/ppermute | solution.py:28
  18.1 0.0 collective-permute-done.4.refs_5_
  18.1 0.0 copy-done
  18.1 0.0 copy-done.2
  18.2 0.0 copy-done.7
  18.2 0.0 copy-done.8
  18.2 0.0 copy-start.3
  18.2 0.9 %copy-done.3 = f32[48,768]{1,0:T(8,128)S(1)} copy-done((f32[48,768]{1,0:T(8,128)S(1)}, f32[48,768]{1,0:T(8,128)}, u32[]{:S(2)}) %copy-start.3) | copy-done | bytes 147480
  19.1 3.1 %solve.1 = (f32[1,48,768]{2,1,0:T(8,128)S(1)}, bf16[1,48,768]{2,1,0:T(8,128)(2,1)S(1)}) custom-call(bf16[48,256]{1,0:T(8,128)(2,1)S(1)} %get-tuple-element.15.refs_0_, bf16[48,256]{1,0:T(8,128)(2,1)S(1)} %collective-permute-done.1.refs_1_, bf16[48,256]{1,0:T(8,128)(2,1)S(1)} %collective-permute-done.2.refs_2_, ...), custom_call_target="tpu_custom_call" | custom-call | tf_op jit(solution)/shard_map/solve/pallas_call | solution.py:180
  22.2 1.6 %collective-permute-start.5 = (bf16[1,48,768]{2,1,0:T(8,128)(2,1)S(1)}, bf16[1,48,768]{2,1,0:T(8,128)(2,1)S(1)}, u32[]{:S(2)}, u32[]{:S(2)}) collective-permute-start(bf16[1,48,768]{2,1,0:T(8,128)(2,1)S(1)} %get-tuple-element.20), channel_id=1, source_target_pairs={{0,2},{2,0},{1,3},{3,1},{4,6},{6,4},{5,7},{7,5},{8,10},{10,8},{9,1... | collective-permute-start | bytes 221192 | tf_op jit(solution)/shard_map/ppermute | solution.py:28
  23.7 2.9 %collective-permute-done.5 = bf16[1,48,768]{2,1,0:T(8,128)(2,1)S(1)} collective-permute-done((bf16[1,48,768]{2,1,0:T(8,128)(2,1)S(1)}, bf16[1,48,768]{2,1,0:T(8,128)(2,1)S(1)}, u32[]{:S(2)}, u32[]{:S(2)}) %collective-permute-start.5) | collective-permute-done | bytes 73760 | tf_op jit(solution)/shard_map/ppermute | solution.py:28
  26.6 0.7 %fusion = bf16[48,1,1,768]{3,0,2,1:T(8,128)(2,1)} fusion(f32[1,48,768]{2,1,0:T(8,128)S(1)} %get-tuple-element.19, bf16[1,48,768]{2,1,0:T(8,128)(2,1)S(1)} %collective-permute-done.5), kind=kLoop, calls=%fused_computation.1 | loop fusion | flops 110592 | bytes 294912 | tf_op jit(solution)/shard_map/broadcast_in_dim;transpose | solution.py:197
  (2 shorter events, 0.0 us)
Async XLA Ops:
  0.0 18.1 %copy-start = (bf16[768,768]{1,0:T(8,128)(2,1)S(1)}, bf16[768,768]{1,0:T(8,128)(2,1)}, u32[]{:S(2)}) copy-start(bf16[768,768]{1,0:T(8,128)(2,1)} %refs_7_.1) | copy-start | bytes 3538948
  0.0 18.1 %collective-permute-start.4 = (bf16[4,32,768]{2,1,0:T(8,128)(2,1)}, bf16[4,32,768]{2,1,0:T(8,128)(2,1)S(1)}, u32[]{:S(2)}, u32[]{:S(2)}) collective-permute-start(bf16[4,32,768]{2,1,0:T(8,128)(2,1)} %refs_4_.1), channel_id=1, source_target_pairs={{0,1},{1,0},{2,3},{3,2},{4,5},{5,4},{6,7},{7,6},{8,9},{9,8},{10,11... | collective-permute-start | bytes 589832 | tf_op jit(solution)/shard_map/ppermute | solution.py:28
  0.5 1.2 %copy-start.1 = (bf16[4,2,32,2048]{3,2,1,0:T(8,128)(2,1)S(1)}, bf16[4,2,32,2048]{3,2,1,0:T(8,128)(2,1)}, u32[]{:S(2)}) copy-start(bf16[4,2,32,2048]{3,2,1,0:T(8,128)(2,1)} %vis_ref.1) | copy-start | bytes 3145732
  1.7 0.9 %copy-start.4 = (f32[192,128]{1,0:T(8,128)S(1)}, f32[192,128]{1,0:T(8,128)}, u32[]{:S(2)}) copy-start(f32[192,128]{1,0:T(8,128)} %constant.8.clone.fs_ref) | copy-start | bytes 294916
  2.6 0.9 %copy-start.5 = (f32[192,128]{1,0:T(8,128)S(1)}, f32[192,128]{1,0:T(8,128)}, u32[]{:S(2)}) copy-start(f32[192,128]{1,0:T(8,128)} %constant.7.clone.fc_ref) | copy-start | bytes 294916
  3.5 0.9 %copy-start.6 = (f32[192,128]{1,0:T(8,128)S(1)}, f32[192,128]{1,0:T(8,128)}, u32[]{:S(2)}) copy-start(f32[192,128]{1,0:T(8,128)} %constant.6.clone.col_ref) | copy-start | bytes 294916
  4.4 13.7 %copy-start.2 = (bf16[4,32,768]{2,1,0:T(8,128)(2,1)S(1)}, bf16[4,32,768]{2,1,0:T(8,128)(2,1)}, u32[]{:S(2)}) copy-start(bf16[4,32,768]{2,1,0:T(8,128)(2,1)} %refs_4_.1) | copy-start | bytes 589828
  4.4 13.8 %copy-start.7 = (f32[4]{0:T(128)S(1)}, f32[4]{0:T(128)}, u32[]{:S(2)}) copy-start(f32[4]{0:T(128)} %refs_8_.1) | copy-start | bytes 52
  4.4 13.8 %copy-start.8 = (bf16[2,8]{1,0:T(2,128)(2,1)S(1)}, bf16[2,8]{1,0:T(2,128)(2,1)}, u32[]{:S(2)}) copy-start(bf16[2,8]{1,0:T(2,128)(2,1)} %refs_9_.1) | copy-start | bytes 100
  5.8 1.3 %collective-permute-start = (bf16[192,128]{1,0:T(8,128)(2,1)S(1)}, bf16[192,128]{1,0:T(8,128)(2,1)S(1)}, u32[]{:S(2)}, u32[]{:S(2)}) collective-permute-start(bf16[192,128]{1,0:T(8,128)(2,1)S(1)} %get-tuple-element.14), channel_id=1, source_target_pairs={{0,1},{1,0},{2,3},{3,2},{4,5},{5,4},{6,7},{7,6},{8,9},{9,8},{10,11... | collective-permute-start | bytes 147464 | tf_op jit(solution)/shard_map/ppermute | solution.py:28
  7.1 5.4 %collective-permute-start.1 = (bf16[48,256]{1,0:T(8,128)(2,1)S(1)}, bf16[48,256]{1,0:T(8,128)(2,1)S(1)}, u32[]{:S(2)}, u32[]{:S(2)}) collective-permute-start(bf16[48,256]{1,0:T(8,128)(2,1)S(1)} %get-tuple-element.16), channel_id=1, source_target_pairs={{0,4},{4,0},{8,12},{12,8},{1,5},{5,1},{9,13},{13,9},{2,6},{6,2},{1... | collective-permute-start | bytes 73736 | tf_op jit(solution)/shard_map/ppermute | solution.py:28
  9.9 4.8 %collective-permute-start.2 = (bf16[48,256]{1,0:T(8,128)(2,1)S(1)}, bf16[48,256]{1,0:T(8,128)(2,1)S(1)}, u32[]{:S(2)}, u32[]{:S(2)}) collective-permute-start(bf16[48,256]{1,0:T(8,128)(2,1)S(1)} %get-tuple-element.17), channel_id=1, source_target_pairs={{0,8},{4,12},{8,0},{12,4},{1,9},{5,13},{9,1},{13,5},{2,10},{6,14},... | collective-permute-start | bytes 73736 | tf_op jit(solution)/shard_map/ppermute | solution.py:28
  12.5 5.6 %collective-permute-start.3 = (bf16[48,256]{1,0:T(8,128)(2,1)S(1)}, bf16[48,256]{1,0:T(8,128)(2,1)S(1)}, u32[]{:S(2)}, u32[]{:S(2)}) collective-permute-start(bf16[48,256]{1,0:T(8,128)(2,1)S(1)} %get-tuple-element.18), channel_id=1, source_target_pairs={{0,12},{4,8},{8,4},{12,0},{1,13},{5,9},{9,5},{13,1},{2,14},{6,10},... | collective-permute-start | bytes 73736 | tf_op jit(solution)/shard_map/ppermute | solution.py:28
  18.2 0.9 %copy-start.3 = (f32[48,768]{1,0:T(8,128)S(1)}, f32[48,768]{1,0:T(8,128)}, u32[]{:S(2)}) copy-start(f32[48,768]{1,0:T(8,128)} %refs_6_.1) | copy-start | bytes 442372
  22.2 4.4 %collective-permute-start.5 = (bf16[1,48,768]{2,1,0:T(8,128)(2,1)S(1)}, bf16[1,48,768]{2,1,0:T(8,128)(2,1)S(1)}, u32[]{:S(2)}, u32[]{:S(2)}) collective-permute-start(bf16[1,48,768]{2,1,0:T(8,128)(2,1)S(1)} %get-tuple-element.20), channel_id=1, source_target_pairs={{0,2},{2,0},{1,3},{3,1},{4,6},{6,4},{5,7},{7,5},{8,10},{10,8},{9,1... | collective-permute-start | bytes 221192 | tf_op jit(solution)/shard_map/ppermute | solution.py:28

commit v2 on v1

--- a/solution.py
+++ b/solution.py
@@ -3,7 +3,6 @@
 
 import jax
 import jax.numpy as jnp
-import numpy as np
 from jax import lax
 from jax.experimental import pallas as pl
 from jax.experimental.pallas import tpu as pltpu
@@ -14,7 +13,10 @@
 LANES = 128
 NT_DIMS = (((1,), (1,)), ((), ()))
 VMEM = pl.BlockSpec(memory_space=pltpu.VMEM)
-SMEM = pl.BlockSpec(memory_space=pltpu.SMEM)
+
+
+def work(microseconds):
+    return pl.CostEstimate(flops=int(1e9 * microseconds), bytes_accessed=1 << 18, transcendentals=0)
 
 
 def partner_of(index, step, size):
@@ -28,45 +30,50 @@
     return lax.ppermute(array, axis, pairs)
 
 
-def phase_tables(modes, local_time, blocks):
-    m = np.arange(modes, dtype=np.int64)[:, None]
-    groups = local_time // LANES
-    coarse = (m * np.arange(groups) * LANES) % NT
-    origin = (m * np.arange(blocks) * local_time) % NT
-    fine = (m * np.arange(LANES)) % NT
-    unit = 2.0 * np.pi / NT
-    columns = np.concatenate(
-        [np.cos(coarse * unit), np.sin(coarse * unit), np.cos(origin * unit), np.sin(origin * unit)], axis=1
-    )
-    columns = np.pad(columns, ((0, 0), (0, -columns.shape[1] % LANES)))
-    tables = (columns, np.cos(fine * unit), np.sin(fine * unit))
-    return tuple(jnp.asarray(t.astype(np.float32)) for t in tables)
-
-
-def transform_kernel(blocks, vis_ref, col_ref, fc_ref, fs_ref, own_ref, other_ref, cos_ref, sin_ref):
+def turn(phase):
+    quarter = NT // 4
+    quadrant = (phase + quarter // 2) // quarter
+    angle = (phase - quadrant * quarter).astype(jnp.float32) * (2.0 * math.pi / NT)
+    sq = angle * angle
+    c, s = jnp.full_like(sq, 1.0 / 40320), jnp.full_like(sq, 1.0 / 362880)
+    for k in (720, 24, 2):
+        c = sq * -c + 1.0 / k
+    c = 1.0 - sq * c
+    for k in (5040, 120, 6):
+        s = sq * -s + 1.0 / k
+    s = angle - angle * sq * s
+    swap = quadrant % 2 == 1
+    cos, sin = jnp.where(swap, s, c), jnp.where(swap, c, s)
+    cos = jnp.where((quadrant == 1) | (quadrant == 2), -cos, cos)
+    sin = jnp.where((quadrant == 2) | (quadrant == 3), -sin, sin)
+    return cos, sin
+
+
+def table_kernel(ntime, cos_ref, sin_ref):
+    modes = cos_ref.shape[0]
+    block = lax.axis_index("ma")
+    mode = lax.broadcasted_iota(jnp.int32, (modes, LANES), 0)
+    lane = lax.broadcasted_iota(jnp.int32, (modes, LANES), 1)
+    fc, fs = turn((mode * lane) % NT)
+    cc, cs = turn((mode * (block * ntime + lane * LANES)) % NT)
+    for u in range(ntime // LANES):
+        at = slice(u * LANES, (u + 1) * LANES)
+        c, s = cc[:, u : u + 1], cs[:, u : u + 1]
+        cos_ref[:, at] = (c * fc - s * fs).astype(jnp.bfloat16)
+        sin_ref[:, at] = (s * fc + c * fs).astype(jnp.bfloat16)
+
+
+def transform_kernel(vis_ref, cos_ref, sin_ref, own_ref, other_ref):
     nfreq, _, nbase, ntime = vis_ref.shape
-    groups = ntime // LANES
-    modes = col_ref.shape[0]
-    block, part = lax.axis_index("ma"), lax.axis_index("pol")
-    lane = lax.broadcasted_iota(jnp.int32, col_ref.shape, 1)
-    columns = col_ref[...]
-    oc = jnp.sum(jnp.where(lane == 2 * groups + block, columns, 0.0), axis=1, keepdims=True)
-    os = jnp.sum(jnp.where(lane == 2 * groups + blocks + block, columns, 0.0), axis=1, keepdims=True)
-    fc = fc_ref[...] * oc - fs_ref[...] * os
-    fs = fs_ref[...] * oc + fc_ref[...] * os
-    for u in range(groups):
-        cc = columns[:, u : u + 1]
-        cs = columns[:, groups + u : groups + u + 1]
-        cos_ref[:, u * LANES : (u + 1) * LANES] = (cc * fc - cs * fs).astype(jnp.bfloat16)
-        sin_ref[:, u * LANES : (u + 1) * LANES] = (cs * fc + cc * fs).astype(jnp.bfloat16)
-    mine = vis_ref[:, part].reshape(nfreq * nbase, ntime)
-    theirs = vis_ref[:, 1 - part].reshape(nfreq * nbase, ntime)
+    n = nfreq * nbase
+    part = lax.axis_index("pol")
+    mine = vis_ref[:, part].reshape(n, ntime)
+    theirs = vis_ref[:, 1 - part].reshape(n, ntime)
     both = jnp.concatenate([mine, theirs], axis=0)
     c = lax.dot_general(cos_ref[...], both, NT_DIMS, preferred_element_type=jnp.float32)
     s = lax.dot_general(sin_ref[...], both, NT_DIMS, preferred_element_type=jnp.float32)
     sign = (1 - 2 * part).astype(jnp.float32)
     scale = NT ** (-0.5)
-    n = nfreq * nbase
     own_ref[...] = ((c[:, :n] + sign * s[:, n:]) * scale).astype(own_ref.dtype)
     other_ref[...] = ((c[:, n:] - sign * s[:, :n]) * scale).astype(other_ref.dtype)
 
@@ -124,12 +131,12 @@
         at = slice(f * modes, (f + 1) * modes)
         d = jnp.where(mask, first[at], 0.0)
         dirty[at] = d
-        estimate[at] = step_ref[f] * d
+        estimate[at] = step_ref[:, f : f + 1] * d
     for _ in range(ITERS):
         again = back(fore(rounded()))
         for f in range(nfreq):
             at = slice(f * modes, (f + 1) * modes)
-            estimate[at] = estimate[at] + step_ref[f] * (dirty[at] - jnp.where(mask, again[at], 0.0))
+            estimate[at] = estimate[at] + step_ref[:, f : f + 1] * (dirty[at] - jnp.where(mask, again[at], 0.0))
     here = lax.axis_index("freq")
     kl = kl_ref[...].astype(jnp.float32)
     kl_row = lax.broadcasted_iota(jnp.int32, kl.shape, 0)
@@ -156,16 +163,23 @@
     n = nfreq * nbase
     shape = jax.ShapeDtypeStruct
     other_rows = exchange(beam_rows, "pol", 2, 1)
-    columns, fc, fs = phase_tables(modes, ntime, blocks)
+    cos, sin = pl.pallas_call(
+        functools.partial(table_kernel, ntime),
+        out_shape=[shape((modes, ntime), jnp.bfloat16)] * 2,
+        out_specs=[VMEM] * 2,
+        compiler_params=pltpu.CompilerParams(vmem_limit_bytes=16 << 20),
+        cost_estimate=work(1.0),
+        name="tables",
+    )()
     own, other = pl.pallas_call(
-        functools.partial(transform_kernel, blocks),
+        transform_kernel,
         out_shape=[shape((modes, n), jnp.bfloat16)] * 2,
-        in_specs=[VMEM] * 4,
+        in_specs=[VMEM] * 3,
         out_specs=[VMEM] * 2,
-        scratch_shapes=[pltpu.VMEM((modes, ntime), jnp.bfloat16)] * 2,
-        compiler_params=pltpu.CompilerParams(vmem_limit_bytes=20 << 20),
+        compiler_params=pltpu.CompilerParams(vmem_limit_bytes=16 << 20),
+        cost_estimate=work(1.0),
         name="transform",
-    )(visibility, columns, fc, fs)
+    )(visibility, cos, sin)
     other = exchange(other, "pol", 2, 1)
     mine = pl.pallas_call(
         functools.partial(merge_kernel, blocks),
@@ -173,6 +187,7 @@
         in_specs=[VMEM] * 2,
         out_specs=[VMEM] * blocks,
         compiler_params=pltpu.CompilerParams(vmem_limit_bytes=16 << 20),
+        cost_estimate=work(0.1),
         name="merge",
     )(own, other)
     parts = [mine[0]] + [exchange(mine[k], "ma", blocks, k) for k in range(1, blocks)]
@@ -181,7 +196,7 @@
         functools.partial(solve_kernel, blocks, nf_blocks),
         out_shape=[shape((kept, local_modes, degrees), jnp.float32)]
         + [shape((kept, local_modes, degrees), jnp.bfloat16)] * (nf_blocks - 1),
-        in_specs=[VMEM] * (blocks + 4) + [SMEM, VMEM],
+        in_specs=[VMEM] * (blocks + 6),
         out_specs=[VMEM] * nf_blocks,
         scratch_shapes=[
             pltpu.VMEM((2 * n, degrees), jnp.bfloat16),
@@ -189,8 +204,9 @@
             pltpu.VMEM((nfreq * local_modes, degrees), jnp.float32),
         ],
         compiler_params=pltpu.CompilerParams(vmem_limit_bytes=24 << 20),
+        cost_estimate=work(2.5),
         name="solve",
-    )(*parts, beam_rows, other_rows, mode_gain, harmonic_basis, step_size, kl_matrix)
+    )(*parts, beam_rows, other_rows, mode_gain, harmonic_basis, step_size[None, :], kl_matrix)
     total = terms[0]
     for k in range(1, nf_blocks):
         total = total + exchange(terms[k], "freq", nf_blocks, k).astype(jnp.float32)

time: 27.5 us -> 22.9 us (0.83)
  local copies, waits for them, and re-layouts: 4.82 us -> 0.04 us
    unnamed x18 -> x12, local copies, waits for them, and re-layouts: 4.82 us -> 0.04 us
    pallas_call x1 -> x2, Pallas kernels: 1.41 us -> 2.22 us  [the longest x1 1.37 us: on_device(): pl.pallas_call(functools.partial(table_kernel, ntime), out_shape=[shape((...]
    pallas_call x1, Pallas kernels: 3.06 us -> 2.52 us  [on_device(): pl.pallas_call(functools.partial(solve_kernel, blocks, nf_blocks), out_sh...]
  transfers between devices with their start and end apart: 6 -> 6, of which waited for: 4 -> 4; matrix products, arithmetic and copies ran while one was open for 0% -> 0% of each run, Pallas kernels for 5% -> 10%
where the time goes in v2:
time: 22.9 us; the launch traced here: 22.8 us
  waiting for transfers between devices  9.7 us (42%)
  starting transfers between devices  7.51 us (33%)
  Pallas kernels  4.76 us (21%)
  other arithmetic  0.65 us (3%)
    ppermute x6, waiting for transfers between devices, exchange(): return lax.ppermute(array, axis, pairs)  9.7 us
    ppermute x6, starting transfers between devices, exchange(): return lax.ppermute(array, axis, pairs)  7.51 us
    pallas_call x1, Pallas kernels, on_device(): pl.pallas_call(functools.partial(solve_kernel, blocks, nf_blocks), out_sh...  2.52 us
    pallas_call x1, Pallas kernels, on_device(): pl.pallas_call(functools.partial(table_kernel, ntime), out_shape=[shape((...  1.37 us
    pallas_call x1, Pallas kernels, on_device(): pl.pallas_call(transform_kernel, out_shape=[shape((modes, n), jnp.bfloat1...  0.86 us
    another operation x1, other arithmetic, on_device(): return total.astype(jnp.bfloat16).transpose(1, 0, 2)[:, :, None, :]  0.65 us
  transfers between devices with their start and end apart: 6, of which 4 were waited for; matrix products, arithmetic and copies ran while one was open for 0% of the time, Pallas kernels for 10%

profile of v2, /device:TPU:0, one launch (start us, length us, event | category | flops | bytes accessed | tf_op | source)
XLA Modules:
  0.0 22.8 jit_solution(11611213196805584304)
XLA Ops:
  0.0 0.0 copy-start.1
  0.0 0.5 %collective-permute-start.4 = (bf16[4,32,768]{2,1,0:T(8,128)(2,1)}, bf16[4,32,768]{2,1,0:T(8,128)(2,1)S(1)}, u32[]{:S(2)}, u32[]{:S(2)}) collective-permute-start(bf16[4,32,768]{2,1,0:T(8,128)(2,1)} %refs_4_.1), channel_id=1, source_target_pairs={{0,1},{1,0},{2,3},{3,2},{4,5},{5,4},{6,7},{7,6},{8,9},{9,8},{10,11... | collective-permute-start | bytes 589832 | tf_op jit(solution)/shard_map/ppermute | solution.py:30
  0.5 1.4 %tables.1 = (bf16[192,2048]{1,0:T(8,128)(2,1)S(1)}, bf16[192,2048]{1,0:T(8,128)(2,1)S(1)}) custom-call(), custom_call_target="tpu_custom_call" | custom-call | flops 1000000000 | bytes 262144 | tf_op jit(solution)/shard_map/tables/pallas_call | solution.py:166
  1.9 0.0 copy-done.1
  1.9 0.0 copy-start
  1.9 0.0 copy-start.2
  1.9 0.0 copy-start.3
  1.9 0.0 copy-start.4
  1.9 0.0 copy-start.5
  1.9 0.9 %transform.1 = (bf16[192,128]{1,0:T(8,128)(2,1)S(1)}, bf16[192,128]{1,0:T(8,128)(2,1)S(1)}) custom-call(bf16[4,2,32,2048]{3,2,1,0:T(8,128)(2,1)S(1)} %copy-done.1, bf16[192,2048]{1,0:T(8,128)(2,1)S(1)} %get-tuple-element.15.cos_ref, bf16[192,2048]{1,0:T(8,128)(2,1)S(1)} %get-tuple-element.16.sin_ref), custom_call_target="tpu_custom_call" | custom-call | flops 1000000000 | bytes 262144 | tf_op jit(solution)/shard_map/transform/pallas_call | solution.py:174
  2.8 0.1 collective-permute-start
  2.9 1.2 %collective-permute-done.other_ref = bf16[192,128]{1,0:T(8,128)(2,1)S(1)} collective-permute-done((bf16[192,128]{1,0:T(8,128)(2,1)S(1)}, bf16[192,128]{1,0:T(8,128)(2,1)S(1)}, u32[]{:S(2)}, u32[]{:S(2)}) %collective-permute-start) | collective-permute-done | bytes 49184 | tf_op jit(solution)/shard_map/ppermute | solution.py:30
  4.1 2.8 %collective-permute-start.1 = (bf16[48,256]{1,0:T(8,128)(2,1)S(1)}, bf16[48,256]{1,0:T(8,128)(2,1)S(1)}, u32[]{:S(2)}, u32[]{:S(2)}) collective-permute-start(bf16[48,256]{1,0:T(8,128)(2,1)S(1)} %get-tuple-element.20), channel_id=1, source_target_pairs={{0,4},{4,0},{8,12},{12,8},{1,5},{5,1},{9,13},{13,9},{2,6},{6,2},{1... | collective-permute-start | bytes 73736 | tf_op jit(solution)/shard_map/ppermute | solution.py:30
  6.9 2.6 %collective-permute-start.2 = (bf16[48,256]{1,0:T(8,128)(2,1)S(1)}, bf16[48,256]{1,0:T(8,128)(2,1)S(1)}, u32[]{:S(2)}, u32[]{:S(2)}) collective-permute-start(bf16[48,256]{1,0:T(8,128)(2,1)S(1)} %get-tuple-element.21), channel_id=1, source_target_pairs={{0,8},{4,12},{8,0},{12,4},{1,9},{5,13},{9,1},{13,5},{2,10},{6,14},... | collective-permute-start | bytes 73736 | tf_op jit(solution)/shard_map/ppermute | solution.py:30
  9.5 0.0 collective-permute-start.3
  9.5 0.0 collective-permute-done.1.refs_1_
  9.5 2.2 %collective-permute-done.2.refs_2_ = bf16[48,256]{1,0:T(8,128)(2,1)S(1)} collective-permute-done((bf16[48,256]{1,0:T(8,128)(2,1)S(1)}, bf16[48,256]{1,0:T(8,128)(2,1)S(1)}, u32[]{:S(2)}, u32[]{:S(2)}) %collective-permute-start.2) | collective-permute-done | bytes 24608 | tf_op jit(solution)/shard_map/ppermute | solution.py:30
  11.7 3.4 %collective-permute-done.3.refs_3_ = bf16[48,256]{1,0:T(8,128)(2,1)S(1)} collective-permute-done((bf16[48,256]{1,0:T(8,128)(2,1)S(1)}, bf16[48,256]{1,0:T(8,128)(2,1)S(1)}, u32[]{:S(2)}, u32[]{:S(2)}) %collective-permute-start.3) | collective-permute-done | bytes 24608 | tf_op jit(solution)/shard_map/ppermute | solution.py:30
  15.1 0.0 collective-permute-done.4.refs_5_
  15.1 0.0 copy-done
  15.1 0.0 copy-done.2
  15.1 0.0 copy-done.3
  15.1 0.0 copy-done.4
  15.1 0.0 copy-done.5
  15.2 2.5 %solve.1 = (f32[1,48,768]{2,1,0:T(8,128)S(1)}, bf16[1,48,768]{2,1,0:T(8,128)(2,1)S(1)}) custom-call(bf16[48,256]{1,0:T(8,128)(2,1)S(1)} %get-tuple-element.19.refs_0_, bf16[48,256]{1,0:T(8,128)(2,1)S(1)} %collective-permute-done.1.refs_1_, bf16[48,256]{1,0:T(8,128)(2,1)S(1)} %collective-permute-done.2.refs_2_, ...), custom_call_target="tpu_custom_call" | custom-call | flops 2500000000 | bytes 262144 | tf_op jit(solution)/shard_map/solve/pallas_call | solution.py:195
  17.7 1.6 %collective-permute-start.5 = (bf16[1,48,768]{2,1,0:T(8,128)(2,1)S(1)}, bf16[1,48,768]{2,1,0:T(8,128)(2,1)S(1)}, u32[]{:S(2)}, u32[]{:S(2)}) collective-permute-start(bf16[1,48,768]{2,1,0:T(8,128)(2,1)S(1)} %get-tuple-element.24), channel_id=1, source_target_pairs={{0,2},{2,0},{1,3},{3,1},{4,6},{6,4},{5,7},{7,5},{8,10},{10,8},{9,1... | collective-permute-start | bytes 221192 | tf_op jit(solution)/shard_map/ppermute | solution.py:30
  19.2 2.9 %collective-permute-done.5 = bf16[1,48,768]{2,1,0:T(8,128)(2,1)S(1)} collective-permute-done((bf16[1,48,768]{2,1,0:T(8,128)(2,1)S(1)}, bf16[1,48,768]{2,1,0:T(8,128)(2,1)S(1)}, u32[]{:S(2)}, u32[]{:S(2)}) %collective-permute-start.5) | collective-permute-done | bytes 73760 | tf_op jit(solution)/shard_map/ppermute | solution.py:30
  22.1 0.7 %fusion = bf16[48,1,1,768]{3,0,2,1:T(8,128)(2,1)} fusion(f32[1,48,768]{2,1,0:T(8,128)S(1)} %get-tuple-element.23, bf16[1,48,768]{2,1,0:T(8,128)(2,1)S(1)} %collective-permute-done.5), kind=kLoop, calls=%fused_computation.1 | loop fusion | flops 110592 | bytes 294912 | tf_op jit(solution)/shard_map/broadcast_in_dim;transpose | solution.py:213
  (1 shorter events, 0.0 us)
Async XLA Ops:
  0.0 1.9 %copy-start.1 = (bf16[4,2,32,2048]{3,2,1,0:T(8,128)(2,1)S(1)}, bf16[4,2,32,2048]{3,2,1,0:T(8,128)(2,1)}, u32[]{:S(2)}) copy-start(bf16[4,2,32,2048]{3,2,1,0:T(8,128)(2,1)} %vis_ref.1) | copy-start | bytes 3145732
  0.0 15.1 %collective-permute-start.4 = (bf16[4,32,768]{2,1,0:T(8,128)(2,1)}, bf16[4,32,768]{2,1,0:T(8,128)(2,1)S(1)}, u32[]{:S(2)}, u32[]{:S(2)}) collective-permute-start(bf16[4,32,768]{2,1,0:T(8,128)(2,1)} %refs_4_.1), channel_id=1, source_target_pairs={{0,1},{1,0},{2,3},{3,2},{4,5},{5,4},{6,7},{7,6},{8,9},{9,8},{10,11... | collective-permute-start | bytes 589832 | tf_op jit(solution)/shard_map/ppermute | solution.py:30
  1.9 13.2 %copy-start = (bf16[768,768]{1,0:T(8,128)(2,1)S(1)}, bf16[768,768]{1,0:T(8,128)(2,1)}, u32[]{:S(2)}) copy-start(bf16[768,768]{1,0:T(8,128)(2,1)} %refs_7_.1) | copy-start | bytes 3538948
  1.9 13.2 %copy-start.2 = (bf16[4,32,768]{2,1,0:T(8,128)(2,1)S(1)}, bf16[4,32,768]{2,1,0:T(8,128)(2,1)}, u32[]{:S(2)}) copy-start(bf16[4,32,768]{2,1,0:T(8,128)(2,1)} %refs_4_.1) | copy-start | bytes 589828
  1.9 13.2 %copy-start.3 = (f32[48,768]{1,0:T(8,128)S(1)}, f32[48,768]{1,0:T(8,128)}, u32[]{:S(2)}) copy-start(f32[48,768]{1,0:T(8,128)} %refs_6_.1) | copy-start | bytes 442372
  1.9 13.2 %copy-start.4 = (f32[4]{0:T(128)S(1)}, f32[4]{0:T(128)}, u32[]{:S(2)}) copy-start(f32[4]{0:T(128)} %param.10) | copy-start | bytes 52
  1.9 13.2 %copy-start.5 = (bf16[2,8]{1,0:T(2,128)(2,1)S(1)}, bf16[2,8]{1,0:T(2,128)(2,1)}, u32[]{:S(2)}) copy-start(bf16[2,8]{1,0:T(2,128)(2,1)} %refs_9_.1) | copy-start | bytes 100
  2.8 1.3 %collective-permute-start = (bf16[192,128]{1,0:T(8,128)(2,1)S(1)}, bf16[192,128]{1,0:T(8,128)(2,1)S(1)}, u32[]{:S(2)}, u32[]{:S(2)}) collective-permute-start(bf16[192,128]{1,0:T(8,128)(2,1)S(1)} %get-tuple-element.18), channel_id=1, source_target_pairs={{0,1},{1,0},{2,3},{3,2},{4,5},{5,4},{6,7},{7,6},{8,9},{9,8},{10,11... | collective-permute-start | bytes 147464 | tf_op jit(solution)/shard_map/ppermute | solution.py:30
  4.1 5.4 %collective-permute-start.1 = (bf16[48,256]{1,0:T(8,128)(2,1)S(1)}, bf16[48,256]{1,0:T(8,128)(2,1)S(1)}, u32[]{:S(2)}, u32[]{:S(2)}) collective-permute-start(bf16[48,256]{1,0:T(8,128)(2,1)S(1)} %get-tuple-element.20), channel_id=1, source_target_pairs={{0,4},{4,0},{8,12},{12,8},{1,5},{5,1},{9,13},{13,9},{2,6},{6,2},{1... | collective-permute-start | bytes 73736 | tf_op jit(solution)/shard_map/ppermute | solution.py:30
  6.9 4.8 %collective-permute-start.2 = (bf16[48,256]{1,0:T(8,128)(2,1)S(1)}, bf16[48,256]{1,0:T(8,128)(2,1)S(1)}, u32[]{:S(2)}, u32[]{:S(2)}) collective-permute-start(bf16[48,256]{1,0:T(8,128)(2,1)S(1)} %get-tuple-element.21), channel_id=1, source_target_pairs={{0,8},{4,12},{8,0},{12,4},{1,9},{5,13},{9,1},{13,5},{2,10},{6,14},... | collective-permute-start | bytes 73736 | tf_op jit(solution)/shard_map/ppermute | solution.py:30
  9.5 5.6 %collective-permute-start.3 = (bf16[48,256]{1,0:T(8,128)(2,1)S(1)}, bf16[48,256]{1,0:T(8,128)(2,1)S(1)}, u32[]{:S(2)}, u32[]{:S(2)}) collective-permute-start(bf16[48,256]{1,0:T(8,128)(2,1)S(1)} %get-tuple-element.22), channel_id=1, source_target_pairs={{0,12},{4,8},{8,4},{12,0},{1,13},{5,9},{9,5},{13,1},{2,14},{6,10},... | collective-permute-start | bytes 73736 | tf_op jit(solution)/shard_map/ppermute | solution.py:30
  17.7 4.4 %collective-permute-start.5 = (bf16[1,48,768]{2,1,0:T(8,128)(2,1)S(1)}, bf16[1,48,768]{2,1,0:T(8,128)(2,1)S(1)}, u32[]{:S(2)}, u32[]{:S(2)}) collective-permute-start(bf16[1,48,768]{2,1,0:T(8,128)(2,1)S(1)} %get-tuple-element.24), channel_id=1, source_target_pairs={{0,2},{2,0},{1,3},{3,1},{4,6},{6,4},{5,7},{7,5},{8,10},{10,8},{9,1... | collective-permute-start | bytes 221192 | tf_op jit(solution)/shard_map/ppermute | solution.py:30

commit v3 on v2

--- a/solution.py
+++ b/solution.py
@@ -8,9 +8,11 @@
 from jax.experimental.pallas import tpu as pltpu
 from jax.sharding import PartitionSpec as P
 
+
 NT = 8192
 ITERS = 2
 LANES = 128
+LINE_OF_FOUR = (((0, 2), (1, 3), (2, 1), (3, 0)), ((0, 3), (1, 2), (2, 0), (3, 1)), ((0, 1), (1, 0), (2, 3), (3, 2)))
 NT_DIMS = (((1,), (1,)), ((), ()))
 VMEM = pl.BlockSpec(memory_space=pltpu.VMEM)
 
@@ -28,6 +30,12 @@
 def exchange(array, axis, size, step):
     pairs = [(i, partner_of(i, step, size)[0]) for i in range(size)]
     return lax.ppermute(array, axis, pairs)
+
+
+def scatter_plan(size):
+    if size == 4:
+        return LINE_OF_FOUR
+    return tuple(tuple((i, partner_of(i, k, size)[0]) for i in range(size)) for k in range(1, size))
 
 
 def turn(phase):
@@ -63,32 +71,36 @@
         sin_ref[:, at] = (s * fc + c * fs).astype(jnp.bfloat16)
 
 
-def transform_kernel(vis_ref, cos_ref, sin_ref, own_ref, other_ref):
+def half_of_modes(vis_ref, cos_ref, sin_ref):
     nfreq, _, nbase, ntime = vis_ref.shape
-    n = nfreq * nbase
     part = lax.axis_index("pol")
-    mine = vis_ref[:, part].reshape(n, ntime)
-    theirs = vis_ref[:, 1 - part].reshape(n, ntime)
-    both = jnp.concatenate([mine, theirs], axis=0)
-    c = lax.dot_general(cos_ref[...], both, NT_DIMS, preferred_element_type=jnp.float32)
-    s = lax.dot_general(sin_ref[...], both, NT_DIMS, preferred_element_type=jnp.float32)
-    sign = (1 - 2 * part).astype(jnp.float32)
-    scale = NT ** (-0.5)
-    own_ref[...] = ((c[:, :n] + sign * s[:, n:]) * scale).astype(own_ref.dtype)
-    other_ref[...] = ((c[:, n:] - sign * s[:, :n]) * scale).astype(other_ref.dtype)
-
-
-def merge_kernel(blocks, own_ref, other_ref, *out_refs):
-    rows, n = out_refs[0].shape[0], own_ref.shape[1]
+    mine = vis_ref[:, part].reshape(nfreq * nbase, ntime)
+    theirs = vis_ref[:, 1 - part].reshape(nfreq * nbase, ntime)
+    c = lax.dot_general(cos_ref[...], mine, NT_DIMS, preferred_element_type=jnp.float32)
+    s = lax.dot_general(sin_ref[...], theirs, NT_DIMS, preferred_element_type=jnp.float32)
+    return (c + (1 - 2 * part).astype(jnp.float32) * s) * NT ** (-0.5)
+
+
+def near_kernel(vis_ref, cos_ref, sin_ref, out_ref):
+    out_ref[...] = half_of_modes(vis_ref, cos_ref, sin_ref).astype(out_ref.dtype)
+
+
+def far_kernel(plan, vis_ref, cos_ref, sin_ref, near_ref, *refs):
+    out_refs, far_ref = refs[:-1], refs[-1]
+    far_ref[...] = half_of_modes(vis_ref, cos_ref, sin_ref).astype(far_ref.dtype)
+    rows, n = out_refs[0].shape[0], near_ref.shape[1]
     me = lax.axis_index("ma")
-    for step, out_ref in enumerate(out_refs):
-        to = partner_of(me, step, blocks)[0]
+    for pairs, out_ref in zip(((),) + plan, out_refs):
+        to = me
+        for source, target in pairs:
+            to = jnp.where(me == source, target, to)
         at = pl.ds(pl.multiple_of(to * rows, 16), rows)
-        out_ref[:, :n] = own_ref[at, :]
-        out_ref[:, n:] = other_ref[at, :]
-
-
-def solve_kernel(blocks, nf_blocks, *refs):
+        out_ref[:, :n] = near_ref[at, :]
+        out_ref[:, n:] = far_ref[at, :]
+
+
+def solve_kernel(received, nf_blocks, *refs):
+    blocks = received + 1
     parts = refs[:blocks]
     rows_own, rows_other, gain_ref, basis_ref, step_ref, kl_ref = refs[blocks : blocks + 6]
     terms = refs[blocks + 6 : blocks + 6 + nf_blocks]
@@ -162,7 +174,7 @@
     modes = local_modes * blocks
     n = nfreq * nbase
     shape = jax.ShapeDtypeStruct
-    other_rows = exchange(beam_rows, "pol", 2, 1)
+    far_visibility = exchange(visibility, "pol", 2, 1)
     cos, sin = pl.pallas_call(
         functools.partial(table_kernel, ntime),
         out_shape=[shape((modes, ntime), jnp.bfloat16)] * 2,
@@ -171,32 +183,36 @@
         cost_estimate=work(1.0),
         name="tables",
     )()
-    own, other = pl.pallas_call(
-        transform_kernel,
-        out_shape=[shape((modes, n), jnp.bfloat16)] * 2,
+    near = pl.pallas_call(
+        near_kernel,
+        out_shape=shape((modes, n), jnp.bfloat16),
         in_specs=[VMEM] * 3,
-        out_specs=[VMEM] * 2,
+        out_specs=VMEM,
         compiler_params=pltpu.CompilerParams(vmem_limit_bytes=16 << 20),
-        cost_estimate=work(1.0),
-        name="transform",
+        cost_estimate=work(0.5),
+        name="near",
     )(visibility, cos, sin)
-    other = exchange(other, "pol", 2, 1)
+    plan = scatter_plan(blocks)
     mine = pl.pallas_call(
-        functools.partial(merge_kernel, blocks),
-        out_shape=[shape((local_modes, 2 * n), jnp.bfloat16)] * blocks,
-        in_specs=[VMEM] * 2,
-        out_specs=[VMEM] * blocks,
+        functools.partial(far_kernel, plan),
+        out_shape=[shape((local_modes, 2 * n), jnp.bfloat16)] * (len(plan) + 1),
+        in_specs=[VMEM] * 4,
+        out_specs=[VMEM] * (len(plan) + 1),
+        scratch_shapes=[pltpu.VMEM((modes, n), jnp.bfloat16)],
         compiler_params=pltpu.CompilerParams(vmem_limit_bytes=16 << 20),
-        cost_estimate=work(0.1),
-        name="merge",
-    )(own, other)
-    parts = [mine[0]] + [exchange(mine[k], "ma", blocks, k) for k in range(1, blocks)]
+        cost_estimate=work(0.5),
+        name="far",
+    )(far_visibility, cos, sin, near)
+    parts = [mine[0]]
+    for k, pairs in enumerate(plan):
+        parts.append(lax.ppermute(mine[k + 1], "ma", pairs))
+    other_rows = exchange(beam_rows, "pol", 2, 1)
     kept = kl_matrix.shape[0] // nf_blocks
     terms = pl.pallas_call(
-        functools.partial(solve_kernel, blocks, nf_blocks),
+        functools.partial(solve_kernel, len(plan), nf_blocks),
         out_shape=[shape((kept, local_modes, degrees), jnp.float32)]
         + [shape((kept, local_modes, degrees), jnp.bfloat16)] * (nf_blocks - 1),
-        in_specs=[VMEM] * (blocks + 6),
+        in_specs=[VMEM] * (len(plan) + 7),
         out_specs=[VMEM] * nf_blocks,
         scratch_shapes=[
             pltpu.VMEM((2 * n, degrees), jnp.bfloat16),

time: 22.9 us -> 20.5 us (0.90)
  waiting for transfers between devices: 9.7 us -> 6.84 us
  Pallas kernels: 4.76 us -> 5.06 us
    ppermute x6 -> x3, waiting for transfers between devices: 9.7 us -> 3.27 us  [exchange(): return lax.ppermute(array, axis, pairs)]
    ppermute x0 -> x3, starting transfers between devices: none -> 5.58 us  [on_device(): parts.append(lax.ppermute(mine[k + 1], 'ma', pairs))]
    ppermute x6 -> x3, starting transfers between devices: 7.51 us -> 2.11 us  [exchange(): return lax.ppermute(array, axis, pairs)]
    ppermute x0 -> x3, waiting for transfers between devices: none -> 3.57 us  [on_device(): parts.append(lax.ppermute(mine[k + 1], 'ma', pairs))]
    pallas_call x3, Pallas kernels: 3.4 us -> 3.69 us  [the longest x1 2.53 us: on_device(): pl.pallas_call(functools.partial(solve_kernel, len(plan), nf_blocks), out...]
  transfers between devices with their start and end apart: 6 -> 6, of which waited for: 4 -> 5; matrix products, arithmetic and copies ran while one was open for 0% -> 0% of each run, Pallas kernels for 10% -> 12%
where the time goes in v3:
time: 20.5 us; the launch traced here: 20.4 us
  starting transfers between devices  7.69 us (38%)
  waiting for transfers between devices  6.84 us (33%)
  Pallas kernels  5.06 us (25%)
  other arithmetic  0.65 us (3%)
    ppermute x3, starting transfers between devices, on_device(): parts.append(lax.ppermute(mine[k + 1], 'ma', pairs))  5.58 us
    ppermute x3, waiting for transfers between devices, on_device(): parts.append(lax.ppermute(mine[k + 1], 'ma', pairs))  3.57 us
    ppermute x3, waiting for transfers between devices, exchange(): return lax.ppermute(array, axis, pairs)  3.27 us
    pallas_call x1, Pallas kernels, on_device(): pl.pallas_call(functools.partial(solve_kernel, len(plan), nf_blocks), out...  2.53 us
    ppermute x3, starting transfers between devices, exchange(): return lax.ppermute(array, axis, pairs)  2.11 us
    pallas_call x1, Pallas kernels, on_device(): pl.pallas_call(functools.partial(table_kernel, ntime), out_shape=[shape((...  1.36 us
    another operation x1, other arithmetic, on_device(): return total.astype(jnp.bfloat16).transpose(1, 0, 2)[:, :, None, :]  0.65 us
    pallas_call x1, Pallas kernels, on_device(): pl.pallas_call(functools.partial(far_kernel, plan), out_shape=[shape((loc...  0.59 us
  transfers between devices with their start and end apart: 6, of which 5 were waited for; matrix products, arithmetic and copies ran while one was open for 0% of the time, Pallas kernels for 12%

profile of v3, /device:TPU:0, one launch (start us, length us, event | category | flops | bytes accessed | tf_op | source)
XLA Modules:
  0.0 20.4 jit_solution(14525740127934702745)
XLA Ops:
  0.0 0.0 copy-start
  0.0 0.5 %collective-permute-start = (bf16[4,2,32,2048]{3,2,1,0:T(8,128)(2,1)}, bf16[4,2,32,2048]{3,2,1,0:T(8,128)(2,1)S(1)}, u32[]{:S(2)}, u32[]{:S(2)}) collective-permute-start(bf16[4,2,32,2048]{3,2,1,0:T(8,128)(2,1)} %vis_ref.1), channel_id=1, source_target_pairs={{0,1},{1,0},{2,3},{3,2},{4,5},{5,4},{6,7},{7,6},{8,9},{9,8},{10,11... | collective-permute-start | bytes 3145736 | tf_op jit(solution)/shard_map/ppermute | solution.py:32
  0.5 0.1 collective-permute-start.4
  0.6 1.4 %tables.1 = (bf16[192,2048]{1,0:T(8,128)(2,1)S(1)}, bf16[192,2048]{1,0:T(8,128)(2,1)S(1)}) custom-call(), custom_call_target="tpu_custom_call" | custom-call | flops 1000000000 | bytes 262144 | tf_op jit(solution)/shard_map/tables/pallas_call | solution.py:178
  1.9 0.0 copy-done
  1.9 0.6 %near.1.near_ref = bf16[192,128]{1,0:T(8,128)(2,1)S(1)} custom-call(bf16[4,2,32,2048]{3,2,1,0:T(8,128)(2,1)S(1)} %copy-done, bf16[192,2048]{1,0:T(8,128)(2,1)S(1)} %get-tuple-element.13.cos_ref, bf16[192,2048]{1,0:T(8,128)(2,1)S(1)} %get-tuple-element.14.sin_ref), custom_call_target="tpu_custom_call" | custom-call | flops 500000000 | bytes 262144 | tf_op jit(solution)/shard_map/near/pallas_call | solution.py:186
  2.5 0.0 copy-start.1
  2.5 0.0 copy-start.2
  2.5 0.0 copy-start.3
  2.6 0.0 copy-start.4
  2.6 0.0 copy-start.5
  2.6 0.4 %collective-permute-done.vis_ref = bf16[4,2,32,2048]{3,2,1,0:T(8,128)(2,1)S(1)} collective-permute-done((bf16[4,2,32,2048]{3,2,1,0:T(8,128)(2,1)}, bf16[4,2,32,2048]{3,2,1,0:T(8,128)(2,1)S(1)}, u32[]{:S(2)}, u32[]{:S(2)}) %collective-permute-start) | collective-permute-done | bytes 1048608 | tf_op jit(solution)/shard_map/ppermute | solution.py:32
  3.0 0.6 %far.1 = (bf16[48,256]{1,0:T(8,128)(2,1)S(1)}, bf16[48,256]{1,0:T(8,128)(2,1)S(1)}, bf16[48,256]{1,0:T(8,128)(2,1)S(1)}, bf16[48,256]{1,0:T(8,128)(2,1)S(1)}) custom-call(bf16[4,2,32,2048]{3,2,1,0:T(8,128)(2,1)S(1)} %collective-permute-done.vis_ref, bf16[192,2048]{1,0:T(8,128)(2,1)S(1)} %get-tuple-element.13.cos_ref, ...), custom_call_target="tpu_custom_call" | custom-call | flops 500000000 | bytes 262144 | tf_op jit(solution)/shard_map/far/pallas_call | solution.py:196
  3.6 4.0 %collective-permute-start.1 = (bf16[48,256]{1,0:T(8,128)(2,1)S(1)}, bf16[48,256]{1,0:T(8,128)(2,1)S(1)}, u32[]{:S(2)}, u32[]{:S(2)}) collective-permute-start(bf16[48,256]{1,0:T(8,128)(2,1)S(1)} %get-tuple-element.16), channel_id=1, source_target_pairs={{0,8},{4,12},{8,4},{12,0},{1,9},{5,13},{9,5},{13,1},{2,10},{6,14},... | collective-permute-start | bytes 73736 | tf_op jit(solution)/shard_map/ppermute | solution.py:208
  7.6 1.1 %collective-permute-start.2 = (bf16[48,256]{1,0:T(8,128)(2,1)S(1)}, bf16[48,256]{1,0:T(8,128)(2,1)S(1)}, u32[]{:S(2)}, u32[]{:S(2)}) collective-permute-start(bf16[48,256]{1,0:T(8,128)(2,1)S(1)} %get-tuple-element.17), channel_id=1, source_target_pairs={{0,12},{4,8},{8,0},{12,4},{1,13},{5,9},{9,1},{13,5},{2,14},{6,10},... | collective-permute-start | bytes 73736 | tf_op jit(solution)/shard_map/ppermute | solution.py:208
  8.7 0.5 %collective-permute-start.3 = (bf16[48,256]{1,0:T(8,128)(2,1)S(1)}, bf16[48,256]{1,0:T(8,128)(2,1)S(1)}, u32[]{:S(2)}, u32[]{:S(2)}) collective-permute-start(bf16[48,256]{1,0:T(8,128)(2,1)S(1)} %get-tuple-element.18), channel_id=1, source_target_pairs={{0,4},{4,0},{8,12},{12,8},{1,5},{5,1},{9,13},{13,9},{2,6},{6,2},{1... | collective-permute-start | bytes 73736 | tf_op jit(solution)/shard_map/ppermute | solution.py:208
  9.2 0.0 collective-permute-done.4.refs_5_
  9.2 1.2 %collective-permute-done.1.refs_1_ = bf16[48,256]{1,0:T(8,128)(2,1)S(1)} collective-permute-done((bf16[48,256]{1,0:T(8,128)(2,1)S(1)}, bf16[48,256]{1,0:T(8,128)(2,1)S(1)}, u32[]{:S(2)}, u32[]{:S(2)}) %collective-permute-start.1) | collective-permute-done | bytes 24608 | tf_op jit(solution)/shard_map/ppermute | solution.py:208
  10.4 2.2 %collective-permute-done.2.refs_2_ = bf16[48,256]{1,0:T(8,128)(2,1)S(1)} collective-permute-done((bf16[48,256]{1,0:T(8,128)(2,1)S(1)}, bf16[48,256]{1,0:T(8,128)(2,1)S(1)}, u32[]{:S(2)}, u32[]{:S(2)}) %collective-permute-start.2) | collective-permute-done | bytes 24608 | tf_op jit(solution)/shard_map/ppermute | solution.py:208
  12.6 0.2 collective-permute-done.3.refs_3_
  12.7 0.0 copy-done.1
  12.7 0.0 copy-done.2
  12.7 0.0 copy-done.3
  12.7 0.0 copy-done.4
  12.8 0.0 copy-done.5
  12.8 2.5 %solve.1 = (f32[1,48,768]{2,1,0:T(8,128)S(1)}, bf16[1,48,768]{2,1,0:T(8,128)(2,1)S(1)}) custom-call(bf16[48,256]{1,0:T(8,128)(2,1)S(1)} %get-tuple-element.15.refs_0_, bf16[48,256]{1,0:T(8,128)(2,1)S(1)} %collective-permute-done.1.refs_1_, bf16[48,256]{1,0:T(8,128)(2,1)S(1)} %collective-permute-done.2.refs_2_, ...), custom_call_target="tpu_custom_call" | custom-call | flops 2500000000 | bytes 262144 | tf_op jit(solution)/shard_map/solve/pallas_call | solution.py:211
  15.3 1.6 %collective-permute-start.5 = (bf16[1,48,768]{2,1,0:T(8,128)(2,1)S(1)}, bf16[1,48,768]{2,1,0:T(8,128)(2,1)S(1)}, u32[]{:S(2)}, u32[]{:S(2)}) collective-permute-start(bf16[1,48,768]{2,1,0:T(8,128)(2,1)S(1)} %get-tuple-element.20), channel_id=1, source_target_pairs={{0,2},{2,0},{1,3},{3,1},{4,6},{6,4},{5,7},{7,5},{8,10},{10,8},{9,1... | collective-permute-start | bytes 221192 | tf_op jit(solution)/shard_map/ppermute | solution.py:32
  16.9 2.9 %collective-permute-done.5 = bf16[1,48,768]{2,1,0:T(8,128)(2,1)S(1)} collective-permute-done((bf16[1,48,768]{2,1,0:T(8,128)(2,1)S(1)}, bf16[1,48,768]{2,1,0:T(8,128)(2,1)S(1)}, u32[]{:S(2)}, u32[]{:S(2)}) %collective-permute-start.5) | collective-permute-done | bytes 73760 | tf_op jit(solution)/shard_map/ppermute | solution.py:32
  19.7 0.7 %fusion = bf16[48,1,1,768]{3,0,2,1:T(8,128)(2,1)} fusion(f32[1,48,768]{2,1,0:T(8,128)S(1)} %get-tuple-element.19, bf16[1,48,768]{2,1,0:T(8,128)(2,1)S(1)} %collective-permute-done.5), kind=kLoop, calls=%fused_computation.1 | loop fusion | flops 110592 | bytes 294912 | tf_op jit(solution)/shard_map/broadcast_in_dim;transpose | solution.py:229
Async XLA Ops:
  0.0 1.9 %copy-start = (bf16[4,2,32,2048]{3,2,1,0:T(8,128)(2,1)S(1)}, bf16[4,2,32,2048]{3,2,1,0:T(8,128)(2,1)}, u32[]{:S(2)}) copy-start(bf16[4,2,32,2048]{3,2,1,0:T(8,128)(2,1)} %vis_ref.1) | copy-start | bytes 3145732
  0.0 3.0 %collective-permute-start = (bf16[4,2,32,2048]{3,2,1,0:T(8,128)(2,1)}, bf16[4,2,32,2048]{3,2,1,0:T(8,128)(2,1)S(1)}, u32[]{:S(2)}, u32[]{:S(2)}) collective-permute-start(bf16[4,2,32,2048]{3,2,1,0:T(8,128)(2,1)} %vis_ref.1), channel_id=1, source_target_pairs={{0,1},{1,0},{2,3},{3,2},{4,5},{5,4},{6,7},{7,6},{8,9},{9,8},{10,11... | collective-permute-start | bytes 3145736 | tf_op jit(solution)/shard_map/ppermute | solution.py:32
  0.5 8.7 %collective-permute-start.4 = (bf16[4,32,768]{2,1,0:T(8,128)(2,1)}, bf16[4,32,768]{2,1,0:T(8,128)(2,1)S(1)}, u32[]{:S(2)}, u32[]{:S(2)}) collective-permute-start(bf16[4,32,768]{2,1,0:T(8,128)(2,1)} %refs_4_.1), channel_id=1, source_target_pairs={{0,1},{1,0},{2,3},{3,2},{4,5},{5,4},{6,7},{7,6},{8,9},{9,8},{10,11... | collective-permute-start | bytes 589832 | tf_op jit(solution)/shard_map/ppermute | solution.py:32
  2.5 10.2 %copy-start.1 = (bf16[768,768]{1,0:T(8,128)(2,1)S(1)}, bf16[768,768]{1,0:T(8,128)(2,1)}, u32[]{:S(2)}) copy-start(bf16[768,768]{1,0:T(8,128)(2,1)} %refs_7_.1) | copy-start | bytes 3538948
  2.5 10.2 %copy-start.2 = (bf16[4,32,768]{2,1,0:T(8,128)(2,1)S(1)}, bf16[4,32,768]{2,1,0:T(8,128)(2,1)}, u32[]{:S(2)}) copy-start(bf16[4,32,768]{2,1,0:T(8,128)(2,1)} %refs_4_.1) | copy-start | bytes 589828
  2.5 10.2 %copy-start.3 = (f32[48,768]{1,0:T(8,128)S(1)}, f32[48,768]{1,0:T(8,128)}, u32[]{:S(2)}) copy-start(f32[48,768]{1,0:T(8,128)} %refs_6_.1) | copy-start | bytes 442372
  2.6 10.2 %copy-start.4 = (f32[4]{0:T(128)S(1)}, f32[4]{0:T(128)}, u32[]{:S(2)}) copy-start(f32[4]{0:T(128)} %param.10) | copy-start | bytes 52
  2.6 10.2 %copy-start.5 = (bf16[2,8]{1,0:T(2,128)(2,1)S(1)}, bf16[2,8]{1,0:T(2,128)(2,1)}, u32[]{:S(2)}) copy-start(bf16[2,8]{1,0:T(2,128)(2,1)} %refs_9_.1) | copy-start | bytes 100
  3.6 6.8 %collective-permute-start.1 = (bf16[48,256]{1,0:T(8,128)(2,1)S(1)}, bf16[48,256]{1,0:T(8,128)(2,1)S(1)}, u32[]{:S(2)}, u32[]{:S(2)}) collective-permute-start(bf16[48,256]{1,0:T(8,128)(2,1)S(1)} %get-tuple-element.16), channel_id=1, source_target_pairs={{0,8},{4,12},{8,4},{12,0},{1,9},{5,13},{9,5},{13,1},{2,10},{6,14},... | collective-permute-start | bytes 73736 | tf_op jit(solution)/shard_map/ppermute | solution.py:208
  7.6 5.0 %collective-permute-start.2 = (bf16[48,256]{1,0:T(8,128)(2,1)S(1)}, bf16[48,256]{1,0:T(8,128)(2,1)S(1)}, u32[]{:S(2)}, u32[]{:S(2)}) collective-permute-start(bf16[48,256]{1,0:T(8,128)(2,1)S(1)} %get-tuple-element.17), channel_id=1, source_target_pairs={{0,12},{4,8},{8,0},{12,4},{1,13},{5,9},{9,1},{13,5},{2,14},{6,10},... | collective-permute-start | bytes 73736 | tf_op jit(solution)/shard_map/ppermute | solution.py:208
  8.7 4.1 %collective-permute-start.3 = (bf16[48,256]{1,0:T(8,128)(2,1)S(1)}, bf16[48,256]{1,0:T(8,128)(2,1)S(1)}, u32[]{:S(2)}, u32[]{:S(2)}) collective-permute-start(bf16[48,256]{1,0:T(8,128)(2,1)S(1)} %get-tuple-element.18), channel_id=1, source_target_pairs={{0,4},{4,0},{8,12},{12,8},{1,5},{5,1},{9,13},{13,9},{2,6},{6,2},{1... | collective-permute-start | bytes 73736 | tf_op jit(solution)/shard_map/ppermute | solution.py:208
  15.3 4.4 %collective-permute-start.5 = (bf16[1,48,768]{2,1,0:T(8,128)(2,1)S(1)}, bf16[1,48,768]{2,1,0:T(8,128)(2,1)S(1)}, u32[]{:S(2)}, u32[]{:S(2)}) collective-permute-start(bf16[1,48,768]{2,1,0:T(8,128)(2,1)S(1)} %get-tuple-element.20), channel_id=1, source_target_pairs={{0,2},{2,0},{1,3},{3,1},{4,6},{6,4},{5,7},{7,5},{8,10},{10,8},{9,1... | collective-permute-start | bytes 221192 | tf_op jit(solution)/shard_map/ppermute | solution.py:32

commit v4 on v3

--- a/solution.py
+++ b/solution.py
@@ -12,7 +12,12 @@
 NT = 8192
 ITERS = 2
 LANES = 128
-LINE_OF_FOUR = (((0, 2), (1, 3), (2, 1), (3, 0)), ((0, 3), (1, 2), (2, 0), (3, 1)), ((0, 1), (1, 0), (2, 3), (3, 2)))
+LINE_OF_FOUR = (
+    (1, 5, 3, 7, 0, 4, 2, 6),
+    (2, 7, 4, 5, 6, 3, 0, 1),
+    (6, 3, 0, 1, 2, 7, 4, 5),
+    (4, 0, 6, 2, 5, 1, 7, 3),
+)
 NT_DIMS = (((1,), (1,)), ((), ()))
 VMEM = pl.BlockSpec(memory_space=pltpu.VMEM)
 
@@ -35,7 +40,13 @@
 def scatter_plan(size):
     if size == 4:
         return LINE_OF_FOUR
-    return tuple(tuple((i, partner_of(i, k, size)[0]) for i in range(size)) for k in range(1, size))
+    return tuple(tuple(2 * partner_of(i // 2, k, size)[0] + i % 2 for i in range(2 * size)) for k in range(1, size))
+
+
+def lookup(index, values):
+    if len(values) * 2 > 30 or max(values) > 3:
+        return sum(jnp.where(index == i, v, 0) for i, v in enumerate(values))
+    return (sum(v << (2 * i) for i, v in enumerate(values)) >> (2 * index)) & 3
 
 
 def turn(phase):
@@ -89,30 +100,39 @@
     out_refs, far_ref = refs[:-1], refs[-1]
     far_ref[...] = half_of_modes(vis_ref, cos_ref, sin_ref).astype(far_ref.dtype)
     rows, n = out_refs[0].shape[0], near_ref.shape[1]
-    me = lax.axis_index("ma")
-    for pairs, out_ref in zip(((),) + plan, out_refs):
-        to = me
-        for source, target in pairs:
-            to = jnp.where(me == source, target, to)
+    me = 2 * lax.axis_index("ma") + lax.axis_index("pol")
+    for targets, out_ref in zip(((),) + plan, out_refs):
+        to = lookup(me, [target // 2 for target in targets]) if targets else lax.axis_index("ma")
         at = pl.ds(pl.multiple_of(to * rows, 16), rows)
         out_ref[:, :n] = near_ref[at, :]
         out_ref[:, n:] = far_ref[at, :]
 
 
-def solve_kernel(received, nf_blocks, *refs):
-    blocks = received + 1
+def prepare_kernel(rows_own, rows_other, basis_ref, beam_ref, beam_turned_ref, basis_turned_ref):
+    nfreq, nbase, degrees = rows_own.shape
+    n = nfreq * nbase
+    beam_ref[:n, :] = rows_own[...].reshape(n, degrees)
+    beam_ref[n:, :] = rows_other[...].reshape(n, degrees)
+    beam_turned_ref[...] = beam_ref[...].T
+    basis_turned_ref[...] = basis_ref[...].T
+
+
+def solve_kernel(plan, nf_blocks, *refs):
+    blocks = len(plan) + 1
     parts = refs[:blocks]
-    rows_own, rows_other, gain_ref, basis_ref, step_ref, kl_ref = refs[blocks : blocks + 6]
-    terms = refs[blocks + 6 : blocks + 6 + nf_blocks]
-    beam, dirty, estimate = refs[blocks + 6 + nf_blocks :]
-    nfreq, nbase, degrees = rows_own.shape
-    modes = gain_ref.shape[0]
-    n = nfreq * nbase
-    beam[:n, :] = rows_own[...].reshape(n, degrees)
-    beam[n:, :] = rows_other[...].reshape(n, degrees)
+    beam, beam_turned, basis_ref, basis_turned, gain_ref, step_ref, kl_ref = refs[blocks : blocks + 7]
+    terms = refs[blocks + 7 : blocks + 7 + nf_blocks]
+    dirty, estimate = refs[blocks + 7 + nf_blocks :]
+    modes, degrees = gain_ref.shape
+    nfreq = step_ref.shape[1]
+    n = beam.shape[0] // 2
+    nbase = n // nfreq
     total = parts[0][...].astype(jnp.float32)
-    for part in parts[1:]:
-        total = total + part[...].astype(jnp.float32)
+    me = 2 * lax.axis_index("ma") + lax.axis_index("pol")
+    for targets, part in zip(plan, parts[1:]):
+        real = [int(targets.index(i) // 2 != i // 2) for i in range(len(targets))]
+        values = part[...].astype(jnp.float32)
+        total = total + (values if all(real) else jnp.where(lookup(me, real) == 1, values, 0.0))
     base = (lax.broadcasted_iota(jnp.int32, (modes, 2 * n), 1) % n) // nbase
     keep = jnp.concatenate([base == f for f in range(nfreq)], axis=0)
     signal = jnp.where(keep, jnp.concatenate([total] * nfreq, axis=0), 0.0).astype(jnp.bfloat16)
@@ -129,8 +149,8 @@
         return jnp.dot(h, basis_ref[...], preferred_element_type=jnp.float32)
 
     def fore(coeffs):
-        e = lax.dot_general(coeffs, basis_ref[...], NT_DIMS, preferred_element_type=jnp.float32)
-        s = lax.dot_general(scaled(e), beam[...], NT_DIMS, preferred_element_type=jnp.float32)
+        e = jnp.dot(coeffs, basis_turned[...], preferred_element_type=jnp.float32)
+        s = jnp.dot(scaled(e), beam_turned[...], preferred_element_type=jnp.float32)
         return jnp.where(keep, s, 0.0).astype(jnp.bfloat16)
 
     def rounded():
@@ -192,6 +212,8 @@
         cost_estimate=work(0.5),
         name="near",
     )(visibility, cos, sin)
+    near, late_rows = lax.optimization_barrier((near, beam_rows))
+    other_rows = exchange(late_rows, "pol", 2, 1)
     plan = scatter_plan(blocks)
     mine = pl.pallas_call(
         functools.partial(far_kernel, plan),
@@ -204,25 +226,37 @@
         name="far",
     )(far_visibility, cos, sin, near)
     parts = [mine[0]]
-    for k, pairs in enumerate(plan):
-        parts.append(lax.ppermute(mine[k + 1], "ma", pairs))
-    other_rows = exchange(beam_rows, "pol", 2, 1)
+    for k, targets in enumerate(plan):
+        parts.append(lax.ppermute(mine[k + 1], ("ma", "pol"), list(enumerate(targets))))
+    tables = pl.pallas_call(
+        prepare_kernel,
+        out_shape=[
+            shape((2 * n, degrees), jnp.bfloat16),
+            shape((degrees, 2 * n), jnp.bfloat16),
+            shape((degrees, degrees), jnp.bfloat16),
+        ],
+        in_specs=[VMEM] * 3,
+        out_specs=[VMEM] * 3,
+        compiler_params=pltpu.CompilerParams(vmem_limit_bytes=16 << 20),
+        cost_estimate=work(0.7),
+        name="prepare",
+    )(beam_rows, other_rows, harmonic_basis)
+    beam, beam_turned, basis_turned = tables
     kept = kl_matrix.shape[0] // nf_blocks
     terms = pl.pallas_call(
-        functools.partial(solve_kernel, len(plan), nf_blocks),
+        functools.partial(solve_kernel, plan, nf_blocks),
         out_shape=[shape((kept, local_modes, degrees), jnp.float32)]
         + [shape((kept, local_modes, degrees), jnp.bfloat16)] * (nf_blocks - 1),
-        in_specs=[VMEM] * (len(plan) + 7),
+        in_specs=[VMEM] * (len(plan) + 8),
         out_specs=[VMEM] * nf_blocks,
         scratch_shapes=[
-            pltpu.VMEM((2 * n, degrees), jnp.bfloat16),
             pltpu.VMEM((nfreq * local_modes, degrees), jnp.float32),
             pltpu.VMEM((nfreq * local_modes, degrees), jnp.float32),
         ],
         compiler_params=pltpu.CompilerParams(vmem_limit_bytes=24 << 20),
         cost_estimate=work(2.5),
         name="solve",
-    )(*parts, beam_rows, other_rows, mode_gain, harmonic_basis, step_size[None, :], kl_matrix)
+    )(*parts, beam, beam_turned, harmonic_basis, basis_turned, mode_gain, step_size[None, :], kl_matrix)
     total = terms[0]
     for k in range(1, nf_blocks):
         total = total + exchange(terms[k], "freq", nf_blocks, k).astype(jnp.float32)

time: 20.5 us -> 19.4 us (0.946)
  waiting for transfers between devices: 6.84 us -> 4.3 us
  starting transfers between devices: 7.69 us -> 8.44 us
  Pallas kernels: 5.06 us -> 5.42 us
  local copies, waits for them, and re-layouts: 0.04 us -> 0.36 us
    ppermute x3 -> x4, waiting for transfers between devices: 3.57 us -> 1.04 us  [on_device(): lax.ppermute(mine[k + 1], ('ma', 'pol'), list(enumerate(targets)))]
    ppermute x3 -> x4, starting transfers between devices: 5.58 us -> 6.1 us  [on_device(): lax.ppermute(mine[k + 1], ('ma', 'pol'), list(enumerate(targets)))]
    pallas_call x1 -> x2, Pallas kernels: 2.53 us -> 2.92 us  [the longest x1 2.46 us: on_device(): pl.pallas_call(functools.partial(solve_kernel, plan, nf_blocks), out_shap...]
    unnamed x12, local copies, waits for them, and re-layouts: 0.04 us -> 0.36 us
    ppermute x3, starting transfers between devices: 2.11 us -> 2.33 us  [exchange(): return lax.ppermute(array, axis, pairs)]
  transfers between devices with their start and end apart: 6 -> 7, of which waited for: 5 -> 4; matrix products, arithmetic and copies ran while one was open for 0% -> 0% of each run, Pallas kernels for 12% -> 15%
where the time goes in v4:
time: 19.4 us; the launch traced here: 19.2 us
  starting transfers between devices  8.44 us (44%)
  Pallas kernels  5.42 us (28%)
  waiting for transfers between devices  4.3 us (22%)
  other arithmetic  0.65 us (3%)
  local copies, waits for them, and re-layouts  0.36 us (2%)
    ppermute x4, starting transfers between devices, on_device(): lax.ppermute(mine[k + 1], ('ma', 'pol'), list(enumerate(targets)))  6.1 us
    ppermute x3, waiting for transfers between devices, exchange(): return lax.ppermute(array, axis, pairs)  3.26 us
    pallas_call x1, Pallas kernels, on_device(): pl.pallas_call(functools.partial(solve_kernel, plan, nf_blocks), out_shap...  2.46 us
    ppermute x3, starting transfers between devices, exchange(): return lax.ppermute(array, axis, pairs)  2.33 us
    pallas_call x1, Pallas kernels, on_device(): pl.pallas_call(functools.partial(table_kernel, ntime), out_shape=[shape((...  1.34 us
    ppermute x4, waiting for transfers between devices, on_device(): lax.ppermute(mine[k + 1], ('ma', 'pol'), list(enumerate(targets)))  1.04 us
    another operation x1, other arithmetic, on_device(): return total.astype(jnp.bfloat16).transpose(1, 0, 2)[:, :, None, :]  0.65 us
    pallas_call x1, Pallas kernels, on_device(): pl.pallas_call(functools.partial(far_kernel, plan), out_shape=[shape((loc...  0.59 us
  transfers between devices with their start and end apart: 7, of which 4 were waited for; matrix products, arithmetic and copies ran while one was open for 0% of the time, Pallas kernels for 15%

profile of v4, /device:TPU:0, one launch (start us, length us, event | category | flops | bytes accessed | tf_op | source)
XLA Modules:
  0.0 19.2 jit_solution(14987068193149872585)
XLA Ops:
  0.0 0.0 copy-start
  0.0 0.5 %collective-permute-start = (bf16[4,2,32,2048]{3,2,1,0:T(8,128)(2,1)}, bf16[4,2,32,2048]{3,2,1,0:T(8,128)(2,1)S(1)}, u32[]{:S(2)}, u32[]{:S(2)}) collective-permute-start(bf16[4,2,32,2048]{3,2,1,0:T(8,128)(2,1)} %vis_ref.1), channel_id=1, source_target_pairs={{0,1},{1,0},{2,3},{3,2},{4,5},{5,4},{6,7},{7,6},{8,9},{9,8},{10,11... | collective-permute-start | bytes 3145736 | tf_op jit(solution)/shard_map/ppermute | solution.py:37
  0.5 1.3 %tables.1 = (bf16[192,2048]{1,0:T(8,128)(2,1)S(1)}, bf16[192,2048]{1,0:T(8,128)(2,1)S(1)}) custom-call(), custom_call_target="tpu_custom_call" | custom-call | flops 1000000000 | bytes 262144 | tf_op jit(solution)/shard_map/tables/pallas_call | solution.py:198
  1.8 0.0 copy-done
  1.8 0.0 copy-start.2
  1.9 0.6 %near.1.near_ref = bf16[192,128]{1,0:T(8,128)(2,1)S(1)} custom-call(bf16[4,2,32,2048]{3,2,1,0:T(8,128)(2,1)S(1)} %copy-done, bf16[192,2048]{1,0:T(8,128)(2,1)S(1)} %get-tuple-element.19.cos_ref, bf16[192,2048]{1,0:T(8,128)(2,1)S(1)} %get-tuple-element.20.sin_ref), custom_call_target="tpu_custom_call" | custom-call | flops 500000000 | bytes 262144 | tf_op jit(solution)/shard_map/near/pallas_call | solution.py:206
  2.4 0.3 %copy-done.2 = bf16[4,32,768]{2,1,0:T(8,128)(2,1)S(1)} copy-done((bf16[4,32,768]{2,1,0:T(8,128)(2,1)S(1)}, bf16[4,32,768]{2,1,0:T(8,128)(2,1)}, u32[]{:S(2)}) %copy-start.2) | copy-done | bytes 196632
  2.8 0.0 copy-start.1
  2.8 0.0 collective-permute-start.5
  2.8 0.2 %collective-permute-done.vis_ref = bf16[4,2,32,2048]{3,2,1,0:T(8,128)(2,1)S(1)} collective-permute-done((bf16[4,2,32,2048]{3,2,1,0:T(8,128)(2,1)}, bf16[4,2,32,2048]{3,2,1,0:T(8,128)(2,1)S(1)}, u32[]{:S(2)}, u32[]{:S(2)}) %collective-permute-start) | collective-permute-done | bytes 1048608 | tf_op jit(solution)/shard_map/ppermute | solution.py:37
  3.0 0.6 %far.1 = (bf16[48,256]{1,0:T(8,128)(2,1)S(1)}, bf16[48,256]{1,0:T(8,128)(2,1)S(1)}, bf16[48,256]{1,0:T(8,128)(2,1)S(1)}, bf16[48,256]{1,0:T(8,128)(2,1)S(1)}, bf16[48,256]{1,0:T(8,128)(2,1)S(1)}) custom-call(bf16[4,2,32,2048]{3,2,1,0:T(8,128)(2,1)S(1)} %collective-permute-done.vis_ref, bf16[192,2048]{1,0:T(8,128)(2,1)S(1)} %get-tuple-element.19.cos_ref, ...), custom_call_target="tpu_custom_call" | custom-call | flops 500000000 | bytes 262144 | tf_op jit(solution)/shard_map/far/pallas_call | solution.py:218
  3.6 0.4 %collective-permute-start.1 = (bf16[48,256]{1,0:T(8,128)(2,1)S(1)}, bf16[48,256]{1,0:T(8,128)(2,1)S(1)}, u32[]{:S(2)}, u32[]{:S(2)}) collective-permute-start(bf16[48,256]{1,0:T(8,128)(2,1)S(1)} %get-tuple-element.23), channel_id=1, source_target_pairs={{0,1},{1,9},{4,5},{5,13},{8,0},{9,8},{12,4},{13,12},{2,3},{3,11},{... | collective-permute-start | bytes 73736 | tf_op jit(solution)/shard_map/ppermute | solution.py:230
  4.0 2.7 %collective-permute-start.2 = (bf16[48,256]{1,0:T(8,128)(2,1)S(1)}, bf16[48,256]{1,0:T(8,128)(2,1)S(1)}, u32[]{:S(2)}, u32[]{:S(2)}) collective-permute-start(bf16[48,256]{1,0:T(8,128)(2,1)S(1)} %get-tuple-element.24), channel_id=1, source_target_pairs={{0,4},{1,13},{4,8},{5,9},{8,12},{9,5},{12,0},{13,1},{2,6},{3,15},{... | collective-permute-start | bytes 73736 | tf_op jit(solution)/shard_map/ppermute | solution.py:230
  6.7 2.2 %collective-permute-start.3 = (bf16[48,256]{1,0:T(8,128)(2,1)S(1)}, bf16[48,256]{1,0:T(8,128)(2,1)S(1)}, u32[]{:S(2)}, u32[]{:S(2)}) collective-permute-start(bf16[48,256]{1,0:T(8,128)(2,1)S(1)} %get-tuple-element.25), channel_id=1, source_target_pairs={{0,12},{1,5},{4,0},{5,1},{8,4},{9,13},{12,8},{13,9},{2,14},{3,7},{... | collective-permute-start | bytes 73736 | tf_op jit(solution)/shard_map/ppermute | solution.py:230
  8.9 0.0 copy-start.3
  9.0 0.0 copy-start.4
  9.0 0.0 copy-start.5
  9.0 0.7 %collective-permute-start.4 = (bf16[48,256]{1,0:T(8,128)(2,1)S(1)}, bf16[48,256]{1,0:T(8,128)(2,1)S(1)}, u32[]{:S(2)}, u32[]{:S(2)}) collective-permute-start(bf16[48,256]{1,0:T(8,128)(2,1)S(1)} %get-tuple-element.26), channel_id=1, source_target_pairs={{0,8},{1,0},{4,12},{5,4},{8,9},{9,1},{12,13},{13,5},{2,10},{3,2},{... | collective-permute-start | bytes 73736 | tf_op jit(solution)/shard_map/ppermute | solution.py:230
  9.7 0.0 collective-permute-done.5.rows_other
  9.7 0.0 copy-done.1
  9.7 0.5 %prepare.1 = (bf16[256,768]{1,0:T(8,128)(2,1)S(1)}, bf16[768,256]{1,0:T(8,128)(2,1)S(1)}, bf16[768,768]{1,0:T(8,128)(2,1)S(1)}) custom-call(bf16[4,32,768]{2,1,0:T(8,128)(2,1)S(1)} %copy-done.2, bf16[4,32,768]{2,1,0:T(8,128)(2,1)S(1)} %collective-permute-done.5.rows_other, bf16[768,768]{1,0:T(8,128)(2,1)S(1)} %copy-done.1), custom_call_target="tpu_custom_call" | custom-call | flops 700000000 | bytes 262144 | tf_op jit(solution)/shard_map/prepare/pallas_call | solution.py:231
  10.2 0.0 collective-permute-done.1.refs_1_
  10.2 0.8 %collective-permute-done.2.refs_2_ = bf16[48,256]{1,0:T(8,128)(2,1)S(1)} collective-permute-done((bf16[48,256]{1,0:T(8,128)(2,1)S(1)}, bf16[48,256]{1,0:T(8,128)(2,1)S(1)}, u32[]{:S(2)}, u32[]{:S(2)}) %collective-permute-start.2) | collective-permute-done | bytes 24608 | tf_op jit(solution)/shard_map/ppermute | solution.py:230
  11.0 0.0 collective-permute-done.3.refs_3_
  11.0 0.2 %collective-permute-done.4.refs_4_ = bf16[48,256]{1,0:T(8,128)(2,1)S(1)} collective-permute-done((bf16[48,256]{1,0:T(8,128)(2,1)S(1)}, bf16[48,256]{1,0:T(8,128)(2,1)S(1)}, u32[]{:S(2)}, u32[]{:S(2)}) %collective-permute-start.4) | collective-permute-done | bytes 24608 | tf_op jit(solution)/shard_map/ppermute | solution.py:230
  11.2 0.0 copy-done.3
  11.2 0.0 copy-done.4
  11.2 0.0 copy-done.5
  11.2 2.5 %solve.1 = (f32[1,48,768]{2,1,0:T(8,128)S(1)}, bf16[1,48,768]{2,1,0:T(8,128)(2,1)S(1)}) custom-call(bf16[48,256]{1,0:T(8,128)(2,1)S(1)} %get-tuple-element.22.refs_0_, bf16[48,256]{1,0:T(8,128)(2,1)S(1)} %collective-permute-done.1.refs_1_, bf16[48,256]{1,0:T(8,128)(2,1)S(1)} %collective-permute-done.2.refs_2_, ...), custom_call_target="tpu_custom_call" | custom-call | flops 2500000000 | bytes 262144 | tf_op jit(solution)/shard_map/solve/pallas_call | solution.py:246
  13.7 1.8 %collective-permute-start.6 = (bf16[1,48,768]{2,1,0:T(8,128)(2,1)S(1)}, bf16[1,48,768]{2,1,0:T(8,128)(2,1)S(1)}, u32[]{:S(2)}, u32[]{:S(2)}) collective-permute-start(bf16[1,48,768]{2,1,0:T(8,128)(2,1)S(1)} %get-tuple-element.32), channel_id=1, source_target_pairs={{0,2},{2,0},{1,3},{3,1},{4,6},{6,4},{5,7},{7,5},{8,10},{10,8},{9,1... | collective-permute-start | bytes 221192 | tf_op jit(solution)/shard_map/ppermute | solution.py:37
  15.5 3.1 %collective-permute-done.6 = bf16[1,48,768]{2,1,0:T(8,128)(2,1)S(1)} collective-permute-done((bf16[1,48,768]{2,1,0:T(8,128)(2,1)S(1)}, bf16[1,48,768]{2,1,0:T(8,128)(2,1)S(1)}, u32[]{:S(2)}, u32[]{:S(2)}) %collective-permute-start.6) | collective-permute-done | bytes 73760 | tf_op jit(solution)/shard_map/ppermute | solution.py:37
  18.6 0.7 %fusion = bf16[48,1,1,768]{3,0,2,1:T(8,128)(2,1)} fusion(f32[1,48,768]{2,1,0:T(8,128)S(1)} %get-tuple-element.31, bf16[1,48,768]{2,1,0:T(8,128)(2,1)S(1)} %collective-permute-done.6), kind=kLoop, calls=%fused_computation.1 | loop fusion | flops 110592 | bytes 294912 | tf_op jit(solution)/shard_map/broadcast_in_dim;transpose | solution.py:263
Async XLA Ops:
  0.0 1.8 %copy-start = (bf16[4,2,32,2048]{3,2,1,0:T(8,128)(2,1)S(1)}, bf16[4,2,32,2048]{3,2,1,0:T(8,128)(2,1)}, u32[]{:S(2)}) copy-start(bf16[4,2,32,2048]{3,2,1,0:T(8,128)(2,1)} %vis_ref.1) | copy-start | bytes 3145732
  0.0 3.0 %collective-permute-start = (bf16[4,2,32,2048]{3,2,1,0:T(8,128)(2,1)}, bf16[4,2,32,2048]{3,2,1,0:T(8,128)(2,1)S(1)}, u32[]{:S(2)}, u32[]{:S(2)}) collective-permute-start(bf16[4,2,32,2048]{3,2,1,0:T(8,128)(2,1)} %vis_ref.1), channel_id=1, source_target_pairs={{0,1},{1,0},{2,3},{3,2},{4,5},{5,4},{6,7},{7,6},{8,9},{9,8},{10,11... | collective-permute-start | bytes 3145736 | tf_op jit(solution)/shard_map/ppermute | solution.py:37
  1.8 0.9 %copy-start.2 = (bf16[4,32,768]{2,1,0:T(8,128)(2,1)S(1)}, bf16[4,32,768]{2,1,0:T(8,128)(2,1)}, u32[]{:S(2)}) copy-start(bf16[4,32,768]{2,1,0:T(8,128)(2,1)} %rows_own.1) | copy-start | bytes 589828
  2.8 6.9 %copy-start.1 = (bf16[768,768]{1,0:T(8,128)(2,1)S(1)}, bf16[768,768]{1,0:T(8,128)(2,1)}, u32[]{:S(2)}) copy-start(bf16[768,768]{1,0:T(8,128)(2,1)} %refs_7_.1) | copy-start | bytes 3538948
  2.8 6.9 %collective-permute-start.5 = (bf16[4,32,768]{2,1,0:T(8,128)(2,1)S(1)}, bf16[4,32,768]{2,1,0:T(8,128)(2,1)S(1)}, u32[]{:S(2)}, u32[]{:S(2)}) collective-permute-start(bf16[4,32,768]{2,1,0:T(8,128)(2,1)S(1)} %copy-done.2), channel_id=1, source_target_pairs={{0,1},{1,0},{2,3},{3,2},{4,5},{5,4},{6,7},{7,6},{8,9},{9,8},{10,11... | collective-permute-start | bytes 589832 | tf_op jit(solution)/shard_map/ppermute | solution.py:37
  3.6 6.6 %collective-permute-start.1 = (bf16[48,256]{1,0:T(8,128)(2,1)S(1)}, bf16[48,256]{1,0:T(8,128)(2,1)S(1)}, u32[]{:S(2)}, u32[]{:S(2)}) collective-permute-start(bf16[48,256]{1,0:T(8,128)(2,1)S(1)} %get-tuple-element.23), channel_id=1, source_target_pairs={{0,1},{1,9},{4,5},{5,13},{8,0},{9,8},{12,4},{13,12},{2,3},{3,11},{... | collective-permute-start | bytes 73736 | tf_op jit(solution)/shard_map/ppermute | solution.py:230
  4.0 7.0 %collective-permute-start.2 = (bf16[48,256]{1,0:T(8,128)(2,1)S(1)}, bf16[48,256]{1,0:T(8,128)(2,1)S(1)}, u32[]{:S(2)}, u32[]{:S(2)}) collective-permute-start(bf16[48,256]{1,0:T(8,128)(2,1)S(1)} %get-tuple-element.24), channel_id=1, source_target_pairs={{0,4},{1,13},{4,8},{5,9},{8,12},{9,5},{12,0},{13,1},{2,6},{3,15},{... | collective-permute-start | bytes 73736 | tf_op jit(solution)/shard_map/ppermute | solution.py:230
  6.7 4.3 %collective-permute-start.3 = (bf16[48,256]{1,0:T(8,128)(2,1)S(1)}, bf16[48,256]{1,0:T(8,128)(2,1)S(1)}, u32[]{:S(2)}, u32[]{:S(2)}) collective-permute-start(bf16[48,256]{1,0:T(8,128)(2,1)S(1)} %get-tuple-element.25), channel_id=1, source_target_pairs={{0,12},{1,5},{4,0},{5,1},{8,4},{9,13},{12,8},{13,9},{2,14},{3,7},{... | collective-permute-start | bytes 73736 | tf_op jit(solution)/shard_map/ppermute | solution.py:230
  8.9 2.3 %copy-start.3 = (f32[48,768]{1,0:T(8,128)S(1)}, f32[48,768]{1,0:T(8,128)}, u32[]{:S(2)}) copy-start(f32[48,768]{1,0:T(8,128)} %refs_9_.1) | copy-start | bytes 442372
  9.0 2.3 %copy-start.4 = (f32[4]{0:T(128)S(1)}, f32[4]{0:T(128)}, u32[]{:S(2)}) copy-start(f32[4]{0:T(128)} %param.10) | copy-start | bytes 52
  9.0 2.3 %copy-start.5 = (bf16[2,8]{1,0:T(2,128)(2,1)S(1)}, bf16[2,8]{1,0:T(2,128)(2,1)}, u32[]{:S(2)}) copy-start(bf16[2,8]{1,0:T(2,128)(2,1)} %refs_11_.1) | copy-start | bytes 100
  9.0 2.3 %collective-permute-start.4 = (bf16[48,256]{1,0:T(8,128)(2,1)S(1)}, bf16[48,256]{1,0:T(8,128)(2,1)S(1)}, u32[]{:S(2)}, u32[]{:S(2)}) collective-permute-start(bf16[48,256]{1,0:T(8,128)(2,1)S(1)} %get-tuple-element.26), channel_id=1, source_target_pairs={{0,8},{1,0},{4,12},{5,4},{8,9},{9,1},{12,13},{13,5},{2,10},{3,2},{... | collective-permute-start | bytes 73736 | tf_op jit(solution)/shard_map/ppermute | solution.py:230
  13.7 4.9 %collective-permute-start.6 = (bf16[1,48,768]{2,1,0:T(8,128)(2,1)S(1)}, bf16[1,48,768]{2,1,0:T(8,128)(2,1)S(1)}, u32[]{:S(2)}, u32[]{:S(2)}) collective-permute-start(bf16[1,48,768]{2,1,0:T(8,128)(2,1)S(1)} %get-tuple-element.32), channel_id=1, source_target_pairs={{0,2},{2,0},{1,3},{3,1},{4,6},{6,4},{5,7},{7,5},{8,10},{10,8},{9,1... | collective-permute-start | bytes 221192 | tf_op jit(solution)/shard_map/ppermute | solution.py:37

commit v5 on v4

--- a/solution.py
+++ b/solution.py
@@ -49,37 +49,38 @@
     return (sum(v << (2 * i) for i, v in enumerate(values)) >> (2 * index)) & 3
 
 
-def turn(phase):
+def turn(steps):
     quarter = NT // 4
-    quadrant = (phase + quarter // 2) // quarter
+    phase = steps & (NT - 1)
+    quadrant = (phase + quarter // 2) >> (quarter.bit_length() - 1)
     angle = (phase - quadrant * quarter).astype(jnp.float32) * (2.0 * math.pi / NT)
     sq = angle * angle
-    c, s = jnp.full_like(sq, 1.0 / 40320), jnp.full_like(sq, 1.0 / 362880)
-    for k in (720, 24, 2):
-        c = sq * -c + 1.0 / k
-    c = 1.0 - sq * c
-    for k in (5040, 120, 6):
-        s = sq * -s + 1.0 / k
-    s = angle - angle * sq * s
-    swap = quadrant % 2 == 1
+    c = 1.0 + sq * (-1.0 / 2 + sq * (1.0 / 24 + sq * (-1.0 / 720 + sq * (1.0 / 40320))))
+    s = angle + angle * sq * (-1.0 / 6 + sq * (1.0 / 120 + sq * (-1.0 / 5040 + sq * (1.0 / 362880))))
+    swap = (quadrant & 1) == 1
     cos, sin = jnp.where(swap, s, c), jnp.where(swap, c, s)
-    cos = jnp.where((quadrant == 1) | (quadrant == 2), -cos, cos)
-    sin = jnp.where((quadrant == 2) | (quadrant == 3), -sin, sin)
+    cos = jnp.where(((quadrant + 1) & 2) == 2, -cos, cos)
+    sin = jnp.where((quadrant & 2) == 2, -sin, sin)
     return cos, sin
 
 
 def table_kernel(ntime, cos_ref, sin_ref):
     modes = cos_ref.shape[0]
-    block = lax.axis_index("ma")
-    mode = lax.broadcasted_iota(jnp.int32, (modes, LANES), 0)
-    lane = lax.broadcasted_iota(jnp.int32, (modes, LANES), 1)
-    fc, fs = turn((mode * lane) % NT)
-    cc, cs = turn((mode * (block * ntime + lane * LANES)) % NT)
-    for u in range(ntime // LANES):
-        at = slice(u * LANES, (u + 1) * LANES)
-        c, s = cc[:, u : u + 1], cs[:, u : u + 1]
-        cos_ref[:, at] = (c * fc - s * fs).astype(jnp.bfloat16)
-        sin_ref[:, at] = (s * fc + c * fs).astype(jnp.bfloat16)
+    origin = lax.axis_index("ma") * ntime
+    chunk = math.gcd(modes, 48)
+    for top in range(0, modes, chunk):
+        at = slice(top, top + chunk)
+        mode = top + lax.broadcasted_iota(jnp.int32, (chunk, LANES), 0)
+        lane = lax.broadcasted_iota(jnp.int32, (chunk, LANES), 1)
+        dc, ds = turn(mode * LANES)
+        c, s = turn(mode * (origin + lane))
+        c_last, s_last = c * dc + s * ds, s * dc - c * ds
+        for u in range(ntime // LANES):
+            columns = slice(u * LANES, (u + 1) * LANES)
+            cos_ref[at, columns] = c.astype(jnp.bfloat16)
+            sin_ref[at, columns] = s.astype(jnp.bfloat16)
+            c, c_last = (2.0 * dc) * c - c_last, c
+            s, s_last = (2.0 * dc) * s - s_last, s
 
 
 def half_of_modes(vis_ref, cos_ref, sin_ref):
@@ -108,83 +109,80 @@
         out_ref[:, n:] = far_ref[at, :]
 
 
-def prepare_kernel(rows_own, rows_other, basis_ref, beam_ref, beam_turned_ref, basis_turned_ref):
+def prepare_kernel(nf_blocks, rows_own, rows_other, basis_ref, step_ref, kl_ref, *outs):
+    beam_ref, beam_turned_ref, basis_turned_ref, keep_ref, lanes_ref = outs
     nfreq, nbase, degrees = rows_own.shape
     n = nfreq * nbase
     beam_ref[:n, :] = rows_own[...].reshape(n, degrees)
     beam_ref[n:, :] = rows_other[...].reshape(n, degrees)
     beam_turned_ref[...] = beam_ref[...].T
     basis_turned_ref[...] = basis_ref[...].T
+    modes = keep_ref.shape[0] // nfreq
+    of_column = (lax.broadcasted_iota(jnp.int32, (modes, 2 * n), 1) % n) // nbase
+    for f in range(nfreq):
+        keep_ref[f * modes : (f + 1) * modes, :] = jnp.where(of_column == f, 1.0, 0.0)
+
+    def by_column(values):
+        return sum(jnp.where(of_column[:1] == f, value, 0.0) for f, value in enumerate(values))
+
+    here = lax.axis_index("freq")
+    kl = kl_ref[...].astype(jnp.float32)
+    kl_row = lax.broadcasted_iota(jnp.int32, kl.shape, 0)
+    kl_col = lax.broadcasted_iota(jnp.int32, kl.shape, 1)
+    kept = kl.shape[0] // nf_blocks
+
+    def weight(row, f):
+        hit = (kl_row == row) & (kl_col == here * nfreq + f)
+        return jnp.sum(jnp.where(hit, kl, 0.0), keepdims=True)
+
+    lanes_ref[0:1, :] = by_column([step_ref[:, f : f + 1] for f in range(nfreq)])
+    for step in range(nf_blocks):
+        for j in range(kept):
+            row = partner_of(here, step, nf_blocks)[0] * kept + j
+            at = 1 + step * kept + j
+            lanes_ref[at : at + 1, :] = by_column([weight(row, f) for f in range(nfreq)])
 
 
 def solve_kernel(plan, nf_blocks, *refs):
     blocks = len(plan) + 1
     parts = refs[:blocks]
-    beam, beam_turned, basis_ref, basis_turned, gain_ref, step_ref, kl_ref = refs[blocks : blocks + 7]
-    terms = refs[blocks + 7 : blocks + 7 + nf_blocks]
-    dirty, estimate = refs[blocks + 7 + nf_blocks :]
+    beam, beam_turned, basis_ref, basis_turned, keep, lanes, gain_ref = refs[blocks : blocks + 7]
+    terms = refs[blocks + 7 :]
     modes, degrees = gain_ref.shape
-    nfreq = step_ref.shape[1]
-    n = beam.shape[0] // 2
-    nbase = n // nfreq
+    nfreq = keep.shape[0] // modes
     total = parts[0][...].astype(jnp.float32)
     me = 2 * lax.axis_index("ma") + lax.axis_index("pol")
     for targets, part in zip(plan, parts[1:]):
         real = [int(targets.index(i) // 2 != i // 2) for i in range(len(targets))]
         values = part[...].astype(jnp.float32)
         total = total + (values if all(real) else jnp.where(lookup(me, real) == 1, values, 0.0))
-    base = (lax.broadcasted_iota(jnp.int32, (modes, 2 * n), 1) % n) // nbase
-    keep = jnp.concatenate([base == f for f in range(nfreq)], axis=0)
-    signal = jnp.where(keep, jnp.concatenate([total] * nfreq, axis=0), 0.0).astype(jnp.bfloat16)
     ids = lax.axis_index("ma") * modes + lax.broadcasted_iota(jnp.int32, (modes, degrees), 0)
     mask = lax.broadcasted_iota(jnp.int32, (modes, degrees), 1) >= ids
 
+    def groups(values):
+        return [values[at : at + modes] for at in range(0, values.shape[0], modes)]
+
     def scaled(values):
-        return jnp.concatenate(
-            [(values[f * modes : (f + 1) * modes] * gain_ref[...]).astype(jnp.bfloat16) for f in range(nfreq)], axis=0
-        )
+        return jnp.concatenate([(v * gain_ref[...]).astype(jnp.bfloat16) for v in groups(values)], axis=0)
 
     def back(signal):
         h = scaled(jnp.dot(signal, beam[...], preferred_element_type=jnp.float32))
-        return jnp.dot(h, basis_ref[...], preferred_element_type=jnp.float32)
-
-    def fore(coeffs):
+        return [jnp.where(mask, v, 0.0) for v in groups(jnp.dot(h, basis_ref[...], preferred_element_type=jnp.float32))]
+
+    step = lanes[0:1, :]
+    y = step * total
+    for _ in range(ITERS):
+        spread = (jnp.concatenate([y] * nfreq, axis=0) * keep[...]).astype(jnp.bfloat16)
+        coeffs = jnp.concatenate([v.astype(jnp.bfloat16) for v in back(spread)], axis=0)
         e = jnp.dot(coeffs, basis_turned[...], preferred_element_type=jnp.float32)
-        s = jnp.dot(scaled(e), beam_turned[...], preferred_element_type=jnp.float32)
-        return jnp.where(keep, s, 0.0).astype(jnp.bfloat16)
-
-    def rounded():
-        return jnp.concatenate(
-            [estimate[f * modes : (f + 1) * modes].astype(jnp.bfloat16) for f in range(nfreq)], axis=0
-        )
-
-    first = back(signal)
-    for f in range(nfreq):
-        at = slice(f * modes, (f + 1) * modes)
-        d = jnp.where(mask, first[at], 0.0)
-        dirty[at] = d
-        estimate[at] = step_ref[:, f : f + 1] * d
-    for _ in range(ITERS):
-        again = back(fore(rounded()))
-        for f in range(nfreq):
-            at = slice(f * modes, (f + 1) * modes)
-            estimate[at] = estimate[at] + step_ref[:, f : f + 1] * (dirty[at] - jnp.where(mask, again[at], 0.0))
-    here = lax.axis_index("freq")
-    kl = kl_ref[...].astype(jnp.float32)
-    kl_row = lax.broadcasted_iota(jnp.int32, kl.shape, 0)
-    kl_col = lax.broadcasted_iota(jnp.int32, kl.shape, 1)
-    kept = kl.shape[0] // nf_blocks
-    final = rounded().astype(jnp.float32)
-    for step, out_ref in enumerate(terms):
-        to = partner_of(here, step, nf_blocks)[0]
-        for j in range(kept):
-            acc = None
-            for f in range(nfreq):
-                hit = (kl_row == to * kept + j) & (kl_col == here * nfreq + f)
-                weight = jnp.sum(jnp.where(hit, kl, 0.0), keepdims=True)
-                term = weight * final[f * modes : (f + 1) * modes]
-                acc = term if acc is None else acc + term
-            out_ref[j] = acc.astype(out_ref.dtype)
+        again = jnp.dot(scaled(e), beam_turned[...], preferred_element_type=jnp.float32) * keep[...]
+        y = y + step * (total - sum(groups(again)))
+    rows = [lanes[row : row + 1, :] for row in range(1, 1 + nf_blocks * terms[0].shape[0])]
+    mixed = jnp.concatenate([(y * row).astype(jnp.bfloat16) for row in rows], axis=0)
+    values = back(mixed)
+    for out_ref in terms:
+        for j in range(out_ref.shape[0]):
+            out_ref[j] = values.pop(0).astype(out_ref.dtype)
 
 
 def on_device(sizes, visibility, beam_rows, mode_gain, harmonic_basis, step_size, kl_matrix):
@@ -229,19 +227,21 @@
     for k, targets in enumerate(plan):
         parts.append(lax.ppermute(mine[k + 1], ("ma", "pol"), list(enumerate(targets))))
     tables = pl.pallas_call(
-        prepare_kernel,
+        functools.partial(prepare_kernel, nf_blocks),
         out_shape=[
             shape((2 * n, degrees), jnp.bfloat16),
             shape((degrees, 2 * n), jnp.bfloat16),
             shape((degrees, degrees), jnp.bfloat16),
+            shape((nfreq * local_modes, 2 * n), jnp.float32),
+            shape((1 + kl_matrix.shape[0], 2 * n), jnp.float32),
         ],
-        in_specs=[VMEM] * 3,
-        out_specs=[VMEM] * 3,
+        in_specs=[VMEM] * 5,
+        out_specs=[VMEM] * 5,
         compiler_params=pltpu.CompilerParams(vmem_limit_bytes=16 << 20),
         cost_estimate=work(0.7),
         name="prepare",
-    )(beam_rows, other_rows, harmonic_basis)
-    beam, beam_turned, basis_turned = tables
+    )(beam_rows, other_rows, harmonic_basis, step_size[None, :], kl_matrix)
+    beam, beam_turned, basis_turned, keep, lanes = tables
     kept = kl_matrix.shape[0] // nf_blocks
     terms = pl.pallas_call(
         functools.partial(solve_kernel, plan, nf_blocks),
@@ -249,14 +249,10 @@
         + [shape((kept, local_modes, degrees), jnp.bfloat16)] * (nf_blocks - 1),
         in_specs=[VMEM] * (len(plan) + 8),
         out_specs=[VMEM] * nf_blocks,
-        scratch_shapes=[
-            pltpu.VMEM((nfreq * local_modes, degrees), jnp.float32),
-            pltpu.VMEM((nfreq * local_modes, degrees), jnp.float32),
-        ],
         compiler_params=pltpu.CompilerParams(vmem_limit_bytes=24 << 20),
         cost_estimate=work(2.5),
         name="solve",
-    )(*parts, beam, beam_turned, harmonic_basis, basis_turned, mode_gain, step_size[None, :], kl_matrix)
+    )(*parts, beam, beam_turned, harmonic_basis, basis_turned, keep, lanes, mode_gain)
     total = terms[0]
     for k in range(1, nf_blocks):
         total = total + exchange(terms[k], "freq", nf_blocks, k).astype(jnp.float32)

time: 19.4 us -> 19.4 us (level)
  Pallas kernels: 5.42 us -> 4.7 us
  starting transfers between devices: 8.44 us -> 8.91 us
    pallas_call x1, Pallas kernels: 1.34 us -> 0.61 us  [on_device(): pl.pallas_call(functools.partial(table_kernel, ntime), out_shape=[shape((...]
    ppermute x3, starting transfers between devices: 2.33 us -> 2.81 us  [exchange(): return lax.ppermute(array, axis, pairs)]
    ppermute x3, waiting for transfers between devices: 3.26 us -> 3.47 us  [exchange(): return lax.ppermute(array, axis, pairs)]
  transfers between devices with their start and end apart: 7 -> 7, of which waited for: 4 -> 4; matrix products, arithmetic and copies ran while one was open for 0% -> 0% of each run, Pallas kernels for 15% -> 12%
where the time goes in v5:
time: 19.4 us; the launch traced here: 19.2 us
  starting transfers between devices  8.91 us (46%)
  Pallas kernels  4.7 us (24%)
  waiting for transfers between devices  4.41 us (23%)
  other arithmetic  0.65 us (3%)
  local copies, waits for them, and re-layouts  0.49 us (3%)
    ppermute x4, starting transfers between devices, on_device(): lax.ppermute(mine[k + 1], ('ma', 'pol'), list(enumerate(targets)))  6.1 us
    ppermute x3, waiting for transfers between devices, exchange(): return lax.ppermute(array, axis, pairs)  3.47 us
    ppermute x3, starting transfers between devices, exchange(): return lax.ppermute(array, axis, pairs)  2.81 us
    pallas_call x1, Pallas kernels, on_device(): pl.pallas_call(functools.partial(solve_kernel, plan, nf_blocks), out_shap...  2.39 us
    ppermute x4, waiting for transfers between devices, on_device(): lax.ppermute(mine[k + 1], ('ma', 'pol'), list(enumerate(targets)))  0.94 us
    another operation x1, other arithmetic, on_device(): return total.astype(jnp.bfloat16).transpose(1, 0, 2)[:, :, None, :]  0.65 us
    pallas_call x1, Pallas kernels, on_device(): pl.pallas_call(functools.partial(table_kernel, ntime), out_shape=[shape((...  0.61 us
    pallas_call x1, Pallas kernels, on_device(): pl.pallas_call(functools.partial(far_kernel, plan), out_shape=[shape((loc...  0.59 us
  transfers between devices with their start and end apart: 7, of which 4 were waited for; matrix products, arithmetic and copies ran while one was open for 0% of the time, Pallas kernels for 12%

profile of v5, /device:TPU:0, one launch (start us, length us, event | category | flops | bytes accessed | tf_op | source)
XLA Modules:
  0.0 19.2 jit_solution(13906384498653263825)
XLA Ops:
  0.0 0.0 copy-start
  0.0 0.5 %collective-permute-start = (bf16[4,2,32,2048]{3,2,1,0:T(8,128)(2,1)}, bf16[4,2,32,2048]{3,2,1,0:T(8,128)(2,1)S(1)}, u32[]{:S(2)}, u32[]{:S(2)}) collective-permute-start(bf16[4,2,32,2048]{3,2,1,0:T(8,128)(2,1)} %vis_ref.1), channel_id=1, source_target_pairs={{0,1},{1,0},{2,3},{3,2},{4,5},{5,4},{6,7},{7,6},{8,9},{9,8},{10,11... | collective-permute-start | bytes 3145736 | tf_op jit(solution)/shard_map/ppermute | solution.py:37
  0.5 0.6 %tables.1 = (bf16[192,2048]{1,0:T(8,128)(2,1)S(1)}, bf16[192,2048]{1,0:T(8,128)(2,1)S(1)}) custom-call(), custom_call_target="tpu_custom_call" | custom-call | flops 1000000000 | bytes 262144 | tf_op jit(solution)/shard_map/tables/pallas_call | solution.py:196
  1.1 0.1 copy-done
  1.2 0.0 copy-start.2
  1.2 0.6 %near.1.near_ref = bf16[192,128]{1,0:T(8,128)(2,1)S(1)} custom-call(bf16[4,2,32,2048]{3,2,1,0:T(8,128)(2,1)S(1)} %copy-done, bf16[192,2048]{1,0:T(8,128)(2,1)S(1)} %get-tuple-element.21.cos_ref, bf16[192,2048]{1,0:T(8,128)(2,1)S(1)} %get-tuple-element.22.sin_ref), custom_call_target="tpu_custom_call" | custom-call | flops 500000000 | bytes 262144 | tf_op jit(solution)/shard_map/near/pallas_call | solution.py:204
  1.8 0.3 %copy-done.2 = bf16[4,32,768]{2,1,0:T(8,128)(2,1)S(1)} copy-done((bf16[4,32,768]{2,1,0:T(8,128)(2,1)S(1)}, bf16[4,32,768]{2,1,0:T(8,128)(2,1)}, u32[]{:S(2)}) %copy-start.2) | copy-done | bytes 196632
  2.2 0.0 copy-start.1
  2.2 0.0 copy-start.4
  2.2 0.0 copy-start.5
  2.2 0.5 %collective-permute-start.5 = (bf16[4,32,768]{2,1,0:T(8,128)(2,1)S(1)}, bf16[4,32,768]{2,1,0:T(8,128)(2,1)S(1)}, u32[]{:S(2)}, u32[]{:S(2)}) collective-permute-start(bf16[4,32,768]{2,1,0:T(8,128)(2,1)S(1)} %copy-done.2), channel_id=1, source_target_pairs={{0,1},{1,0},{2,3},{3,2},{4,5},{5,4},{6,7},{7,6},{8,9},{9,8},{10,11... | collective-permute-start | bytes 589832 | tf_op jit(solution)/shard_map/ppermute | solution.py:37
  2.7 0.3 %collective-permute-done.vis_ref = bf16[4,2,32,2048]{3,2,1,0:T(8,128)(2,1)S(1)} collective-permute-done((bf16[4,2,32,2048]{3,2,1,0:T(8,128)(2,1)}, bf16[4,2,32,2048]{3,2,1,0:T(8,128)(2,1)S(1)}, u32[]{:S(2)}, u32[]{:S(2)}) %collective-permute-start) | collective-permute-done | bytes 1048608 | tf_op jit(solution)/shard_map/ppermute | solution.py:37
  3.0 0.6 %far.1 = (bf16[48,256]{1,0:T(8,128)(2,1)S(1)}, bf16[48,256]{1,0:T(8,128)(2,1)S(1)}, bf16[48,256]{1,0:T(8,128)(2,1)S(1)}, bf16[48,256]{1,0:T(8,128)(2,1)S(1)}, bf16[48,256]{1,0:T(8,128)(2,1)S(1)}) custom-call(bf16[4,2,32,2048]{3,2,1,0:T(8,128)(2,1)S(1)} %collective-permute-done.vis_ref, bf16[192,2048]{1,0:T(8,128)(2,1)S(1)} %get-tuple-element.21.cos_ref, ...), custom_call_target="tpu_custom_call" | custom-call | flops 500000000 | bytes 262144 | tf_op jit(solution)/shard_map/far/pallas_call | solution.py:216
  3.6 0.4 %collective-permute-start.1 = (bf16[48,256]{1,0:T(8,128)(2,1)S(1)}, bf16[48,256]{1,0:T(8,128)(2,1)S(1)}, u32[]{:S(2)}, u32[]{:S(2)}) collective-permute-start(bf16[48,256]{1,0:T(8,128)(2,1)S(1)} %get-tuple-element.25), channel_id=1, source_target_pairs={{0,1},{1,9},{4,5},{5,13},{8,0},{9,8},{12,4},{13,12},{2,3},{3,11},{... | collective-permute-start | bytes 73736 | tf_op jit(solution)/shard_map/ppermute | solution.py:228
  4.0 2.7 %collective-permute-start.2 = (bf16[48,256]{1,0:T(8,128)(2,1)S(1)}, bf16[48,256]{1,0:T(8,128)(2,1)S(1)}, u32[]{:S(2)}, u32[]{:S(2)}) collective-permute-start(bf16[48,256]{1,0:T(8,128)(2,1)S(1)} %get-tuple-element.26), channel_id=1, source_target_pairs={{0,4},{1,13},{4,8},{5,9},{8,12},{9,5},{12,0},{13,1},{2,6},{3,15},{... | collective-permute-start | bytes 73736 | tf_op jit(solution)/shard_map/ppermute | solution.py:228
  6.7 2.2 %collective-permute-start.3 = (bf16[48,256]{1,0:T(8,128)(2,1)S(1)}, bf16[48,256]{1,0:T(8,128)(2,1)S(1)}, u32[]{:S(2)}, u32[]{:S(2)}) collective-permute-start(bf16[48,256]{1,0:T(8,128)(2,1)S(1)} %get-tuple-element.27), channel_id=1, source_target_pairs={{0,12},{1,5},{4,0},{5,1},{8,4},{9,13},{12,8},{13,9},{2,14},{3,7},{... | collective-permute-start | bytes 73736 | tf_op jit(solution)/shard_map/ppermute | solution.py:228
  8.9 0.7 %collective-permute-start.4 = (bf16[48,256]{1,0:T(8,128)(2,1)S(1)}, bf16[48,256]{1,0:T(8,128)(2,1)S(1)}, u32[]{:S(2)}, u32[]{:S(2)}) collective-permute-start(bf16[48,256]{1,0:T(8,128)(2,1)S(1)} %get-tuple-element.28), channel_id=1, source_target_pairs={{0,8},{1,0},{4,12},{5,4},{8,9},{9,1},{12,13},{13,5},{2,10},{3,2},{... | collective-permute-start | bytes 73736 | tf_op jit(solution)/shard_map/ppermute | solution.py:228
  9.7 0.0 collective-permute-done.5.rows_other
  9.7 0.0 copy-done.1
  9.7 0.0 copy-done.4
  9.7 0.0 copy-done.5
  9.7 0.0 copy-start.3
  9.7 0.5 %prepare.1 = (bf16[256,768]{1,0:T(8,128)(2,1)S(1)}, bf16[768,256]{1,0:T(8,128)(2,1)S(1)}, bf16[768,768]{1,0:T(8,128)(2,1)S(1)}, f32[192,256]{1,0:T(8,128)S(1)}, f32[3,256]{1,0:T(4,128)S(1)}) custom-call(bf16[4,32,768]{2,1,0:T(8,128)(2,1)S(1)} %copy-done.2, bf16[4,32,768]{2,1,0:T(8,128)(2,1)S(1)} %collective-permute-done.5.rows_other, ...), custom_call_target="tpu_custom_call" | custom-call | flops 700000000 | bytes 262144 | tf_op jit(solution)/shard_map/prepare/pallas_call | solution.py:229
  10.3 0.0 collective-permute-done.1.refs_1_
  10.3 0.7 %collective-permute-done.2.refs_2_ = bf16[48,256]{1,0:T(8,128)(2,1)S(1)} collective-permute-done((bf16[48,256]{1,0:T(8,128)(2,1)S(1)}, bf16[48,256]{1,0:T(8,128)(2,1)S(1)}, u32[]{:S(2)}, u32[]{:S(2)}) %collective-permute-start.2) | collective-permute-done | bytes 24608 | tf_op jit(solution)/shard_map/ppermute | solution.py:228
  11.0 0.0 collective-permute-done.3.refs_3_
  11.0 0.2 %collective-permute-done.4.refs_4_ = bf16[48,256]{1,0:T(8,128)(2,1)S(1)} collective-permute-done((bf16[48,256]{1,0:T(8,128)(2,1)S(1)}, bf16[48,256]{1,0:T(8,128)(2,1)S(1)}, u32[]{:S(2)}, u32[]{:S(2)}) %collective-permute-start.4) | collective-permute-done | bytes 24608 | tf_op jit(solution)/shard_map/ppermute | solution.py:228
  11.2 0.0 copy-done.3
  11.2 2.4 %solve.1 = (f32[1,48,768]{2,1,0:T(8,128)S(1)}, bf16[1,48,768]{2,1,0:T(8,128)(2,1)S(1)}) custom-call(bf16[48,256]{1,0:T(8,128)(2,1)S(1)} %get-tuple-element.24.refs_0_, bf16[48,256]{1,0:T(8,128)(2,1)S(1)} %collective-permute-done.1.refs_1_, bf16[48,256]{1,0:T(8,128)(2,1)S(1)} %collective-permute-done.2.refs_2_, ...), custom_call_target="tpu_custom_call" | custom-call | flops 2500000000 | bytes 262144 | tf_op jit(solution)/shard_map/solve/pallas_call | solution.py:246
  13.6 1.8 %collective-permute-start.6 = (bf16[1,48,768]{2,1,0:T(8,128)(2,1)S(1)}, bf16[1,48,768]{2,1,0:T(8,128)(2,1)S(1)}, u32[]{:S(2)}, u32[]{:S(2)}) collective-permute-start(bf16[1,48,768]{2,1,0:T(8,128)(2,1)S(1)} %get-tuple-element.36), channel_id=1, source_target_pairs={{0,2},{2,0},{1,3},{3,1},{4,6},{6,4},{5,7},{7,5},{8,10},{10,8},{9,1... | collective-permute-start | bytes 221192 | tf_op jit(solution)/shard_map/ppermute | solution.py:37
  15.4 3.1 %collective-permute-done.6 = bf16[1,48,768]{2,1,0:T(8,128)(2,1)S(1)} collective-permute-done((bf16[1,48,768]{2,1,0:T(8,128)(2,1)S(1)}, bf16[1,48,768]{2,1,0:T(8,128)(2,1)S(1)}, u32[]{:S(2)}, u32[]{:S(2)}) %collective-permute-start.6) | collective-permute-done | bytes 73760 | tf_op jit(solution)/shard_map/ppermute | solution.py:37
  18.6 0.7 %fusion = bf16[48,1,1,768]{3,0,2,1:T(8,128)(2,1)} fusion(f32[1,48,768]{2,1,0:T(8,128)S(1)} %get-tuple-element.35, bf16[1,48,768]{2,1,0:T(8,128)(2,1)S(1)} %collective-permute-done.6), kind=kLoop, calls=%fused_computation.1 | loop fusion | flops 110592 | bytes 294912 | tf_op jit(solution)/shard_map/broadcast_in_dim;transpose | solution.py:259
Async XLA Ops:
  0.0 1.2 %copy-start = (bf16[4,2,32,2048]{3,2,1,0:T(8,128)(2,1)S(1)}, bf16[4,2,32,2048]{3,2,1,0:T(8,128)(2,1)}, u32[]{:S(2)}) copy-start(bf16[4,2,32,2048]{3,2,1,0:T(8,128)(2,1)} %vis_ref.1) | copy-start | bytes 3145732
  0.0 3.0 %collective-permute-start = (bf16[4,2,32,2048]{3,2,1,0:T(8,128)(2,1)}, bf16[4,2,32,2048]{3,2,1,0:T(8,128)(2,1)S(1)}, u32[]{:S(2)}, u32[]{:S(2)}) collective-permute-start(bf16[4,2,32,2048]{3,2,1,0:T(8,128)(2,1)} %vis_ref.1), channel_id=1, source_target_pairs={{0,1},{1,0},{2,3},{3,2},{4,5},{5,4},{6,7},{7,6},{8,9},{9,8},{10,11... | collective-permute-start | bytes 3145736 | tf_op jit(solution)/shard_map/ppermute | solution.py:37
  1.2 0.9 %copy-start.2 = (bf16[4,32,768]{2,1,0:T(8,128)(2,1)S(1)}, bf16[4,32,768]{2,1,0:T(8,128)(2,1)}, u32[]{:S(2)}) copy-start(bf16[4,32,768]{2,1,0:T(8,128)(2,1)} %rows_own.1) | copy-start | bytes 589828
  2.2 7.5 %copy-start.1 = (bf16[768,768]{1,0:T(8,128)(2,1)S(1)}, bf16[768,768]{1,0:T(8,128)(2,1)}, u32[]{:S(2)}) copy-start(bf16[768,768]{1,0:T(8,128)(2,1)} %refs_7_.1) | copy-start | bytes 3538948
  2.2 7.5 %copy-start.4 = (f32[4]{0:T(128)S(1)}, f32[4]{0:T(128)}, u32[]{:S(2)}) copy-start(f32[4]{0:T(128)} %param.10) | copy-start | bytes 52
  2.2 7.5 %copy-start.5 = (bf16[2,8]{1,0:T(2,128)(2,1)S(1)}, bf16[2,8]{1,0:T(2,128)(2,1)}, u32[]{:S(2)}) copy-start(bf16[2,8]{1,0:T(2,128)(2,1)} %kl_ref.1) | copy-start | bytes 100
  2.2 7.5 %collective-permute-start.5 = (bf16[4,32,768]{2,1,0:T(8,128)(2,1)S(1)}, bf16[4,32,768]{2,1,0:T(8,128)(2,1)S(1)}, u32[]{:S(2)}, u32[]{:S(2)}) collective-permute-start(bf16[4,32,768]{2,1,0:T(8,128)(2,1)S(1)} %copy-done.2), channel_id=1, source_target_pairs={{0,1},{1,0},{2,3},{3,2},{4,5},{5,4},{6,7},{7,6},{8,9},{9,8},{10,11... | collective-permute-start | bytes 589832 | tf_op jit(solution)/shard_map/ppermute | solution.py:37
  3.6 6.7 %collective-permute-start.1 = (bf16[48,256]{1,0:T(8,128)(2,1)S(1)}, bf16[48,256]{1,0:T(8,128)(2,1)S(1)}, u32[]{:S(2)}, u32[]{:S(2)}) collective-permute-start(bf16[48,256]{1,0:T(8,128)(2,1)S(1)} %get-tuple-element.25), channel_id=1, source_target_pairs={{0,1},{1,9},{4,5},{5,13},{8,0},{9,8},{12,4},{13,12},{2,3},{3,11},{... | collective-permute-start | bytes 73736 | tf_op jit(solution)/shard_map/ppermute | solution.py:228
  4.0 7.0 %collective-permute-start.2 = (bf16[48,256]{1,0:T(8,128)(2,1)S(1)}, bf16[48,256]{1,0:T(8,128)(2,1)S(1)}, u32[]{:S(2)}, u32[]{:S(2)}) collective-permute-start(bf16[48,256]{1,0:T(8,128)(2,1)S(1)} %get-tuple-element.26), channel_id=1, source_target_pairs={{0,4},{1,13},{4,8},{5,9},{8,12},{9,5},{12,0},{13,1},{2,6},{3,15},{... | collective-permute-start | bytes 73736 | tf_op jit(solution)/shard_map/ppermute | solution.py:228
  6.7 4.3 %collective-permute-start.3 = (bf16[48,256]{1,0:T(8,128)(2,1)S(1)}, bf16[48,256]{1,0:T(8,128)(2,1)S(1)}, u32[]{:S(2)}, u32[]{:S(2)}) collective-permute-start(bf16[48,256]{1,0:T(8,128)(2,1)S(1)} %get-tuple-element.27), channel_id=1, source_target_pairs={{0,12},{1,5},{4,0},{5,1},{8,4},{9,13},{12,8},{13,9},{2,14},{3,7},{... | collective-permute-start | bytes 73736 | tf_op jit(solution)/shard_map/ppermute | solution.py:228
  8.9 2.3 %collective-permute-start.4 = (bf16[48,256]{1,0:T(8,128)(2,1)S(1)}, bf16[48,256]{1,0:T(8,128)(2,1)S(1)}, u32[]{:S(2)}, u32[]{:S(2)}) collective-permute-start(bf16[48,256]{1,0:T(8,128)(2,1)S(1)} %get-tuple-element.28), channel_id=1, source_target_pairs={{0,8},{1,0},{4,12},{5,4},{8,9},{9,1},{12,13},{13,5},{2,10},{3,2},{... | collective-permute-start | bytes 73736 | tf_op jit(solution)/shard_map/ppermute | solution.py:228
  9.7 1.5 %copy-start.3 = (f32[48,768]{1,0:T(8,128)S(1)}, f32[48,768]{1,0:T(8,128)}, u32[]{:S(2)}) copy-start(f32[48,768]{1,0:T(8,128)} %refs_11_.1) | copy-start | bytes 442372
  13.6 5.0 %collective-permute-start.6 = (bf16[1,48,768]{2,1,0:T(8,128)(2,1)S(1)}, bf16[1,48,768]{2,1,0:T(8,128)(2,1)S(1)}, u32[]{:S(2)}, u32[]{:S(2)}) collective-permute-start(bf16[1,48,768]{2,1,0:T(8,128)(2,1)S(1)} %get-tuple-element.36), channel_id=1, source_target_pairs={{0,2},{2,0},{1,3},{3,1},{4,6},{6,4},{5,7},{7,5},{8,10},{10,8},{9,1... | collective-permute-start | bytes 221192 | tf_op jit(solution)/shard_map/ppermute | solution.py:37

commit v6 on v5

--- a/solution.py
+++ b/solution.py
@@ -131,23 +131,23 @@
     kl_col = lax.broadcasted_iota(jnp.int32, kl.shape, 1)
     kept = kl.shape[0] // nf_blocks
 
-    def weight(row, f):
-        hit = (kl_row == row) & (kl_col == here * nfreq + f)
+    def weight(row, column):
+        hit = (kl_row == row) & (kl_col == column)
         return jnp.sum(jnp.where(hit, kl, 0.0), keepdims=True)
 
     lanes_ref[0:1, :] = by_column([step_ref[:, f : f + 1] for f in range(nfreq)])
     for step in range(nf_blocks):
         for j in range(kept):
-            row = partner_of(here, step, nf_blocks)[0] * kept + j
+            source = partner_of(here, step, nf_blocks)[1] * nfreq
             at = 1 + step * kept + j
-            lanes_ref[at : at + 1, :] = by_column([weight(row, f) for f in range(nfreq)])
-
-
-def solve_kernel(plan, nf_blocks, *refs):
+            lanes_ref[at : at + 1, :] = by_column([weight(here * kept + j, source + f) for f in range(nfreq)])
+
+
+def solve_kernel(plan, *refs):
     blocks = len(plan) + 1
     parts = refs[:blocks]
     beam, beam_turned, basis_ref, basis_turned, keep, lanes, gain_ref = refs[blocks : blocks + 7]
-    terms = refs[blocks + 7 :]
+    results = refs[blocks + 7 :]
     modes, degrees = gain_ref.shape
     nfreq = keep.shape[0] // modes
     total = parts[0][...].astype(jnp.float32)
@@ -177,12 +177,39 @@
         e = jnp.dot(coeffs, basis_turned[...], preferred_element_type=jnp.float32)
         again = jnp.dot(scaled(e), beam_turned[...], preferred_element_type=jnp.float32) * keep[...]
         y = y + step * (total - sum(groups(again)))
-    rows = [lanes[row : row + 1, :] for row in range(1, 1 + nf_blocks * terms[0].shape[0])]
-    mixed = jnp.concatenate([(y * row).astype(jnp.bfloat16) for row in rows], axis=0)
-    values = back(mixed)
-    for out_ref in terms:
-        for j in range(out_ref.shape[0]):
-            out_ref[j] = values.pop(0).astype(out_ref.dtype)
+    y_ref, mixed_ref = results
+    y_ref[...] = y.astype(y_ref.dtype)
+    mixed_ref[...] = mixed(y, lanes, 0, mixed_ref.shape[0] // modes)
+
+
+def mixed(y, lanes, source, kept):
+    first = 1 + source * kept
+    return jnp.concatenate([(y * lanes[row : row + 1, :]).astype(jnp.bfloat16) for row in range(first, first + kept)], axis=0)
+
+
+def near_terms_kernel(mixed_ref, beam_ref, *refs):
+    *rows, sum_ref, beams_ref = refs
+    sum_ref[...] = jnp.dot(mixed_ref[...], beam_ref[...], preferred_element_type=jnp.float32)
+    count, width, degrees = beams_ref.shape
+    for k in range(count):
+        for half, ref in enumerate((rows[k], rows[count + k])):
+            at = slice(half * width // 2, (half + 1) * width // 2)
+            beams_ref[k, at, :] = ref[...].reshape(width // 2, degrees)
+
+
+def terms_kernel(sum_ref, beams_ref, lanes_ref, gain_ref, basis_ref, *refs):
+    *others, out_ref = refs
+    kept, modes, degrees = out_ref.shape
+    total = sum_ref[...]
+    for k, y_ref in enumerate(others):
+        part = mixed(y_ref[...].astype(jnp.float32), lanes_ref, k + 1, kept)
+        total = total + jnp.dot(part, beams_ref[k], preferred_element_type=jnp.float32)
+    ids = lax.axis_index("ma") * modes + lax.broadcasted_iota(jnp.int32, (modes, degrees), 0)
+    mask = lax.broadcasted_iota(jnp.int32, (modes, degrees), 1) >= ids
+    rows = [(total[j * modes : (j + 1) * modes] * gain_ref[...]).astype(jnp.bfloat16) for j in range(kept)]
+    values = jnp.dot(jnp.concatenate(rows, axis=0), basis_ref[...], preferred_element_type=jnp.float32)
+    for j in range(kept):
+        out_ref[j] = jnp.where(mask, values[j * modes : (j + 1) * modes], 0.0).astype(out_ref.dtype)
 
 
 def on_device(sizes, visibility, beam_rows, mode_gain, harmonic_basis, step_size, kl_matrix):
@@ -192,7 +219,11 @@
     modes = local_modes * blocks
     n = nfreq * nbase
     shape = jax.ShapeDtypeStruct
+    steps = range(1, nf_blocks)
     far_visibility = exchange(visibility, "pol", 2, 1)
+    peer_rows = []
+    for k in steps:
+        peer_rows.append(exchange(beam_rows, "freq", nf_blocks, k))
     cos, sin = pl.pallas_call(
         functools.partial(table_kernel, ntime),
         out_shape=[shape((modes, ntime), jnp.bfloat16)] * 2,
@@ -242,21 +273,43 @@
         name="prepare",
     )(beam_rows, other_rows, harmonic_basis, step_size[None, :], kl_matrix)
     beam, beam_turned, basis_turned, keep, lanes = tables
+    for k in steps:
+        peer_rows.append(exchange(peer_rows[k - 1], "pol", 2, 1))
     kept = kl_matrix.shape[0] // nf_blocks
-    terms = pl.pallas_call(
-        functools.partial(solve_kernel, plan, nf_blocks),
-        out_shape=[shape((kept, local_modes, degrees), jnp.float32)]
-        + [shape((kept, local_modes, degrees), jnp.bfloat16)] * (nf_blocks - 1),
+    y, near_mixed = pl.pallas_call(
+        functools.partial(solve_kernel, plan),
+        out_shape=[shape((local_modes, 2 * n), jnp.bfloat16), shape((kept * local_modes, 2 * n), jnp.bfloat16)],
         in_specs=[VMEM] * (len(plan) + 8),
-        out_specs=[VMEM] * nf_blocks,
+        out_specs=[VMEM] * 2,
         compiler_params=pltpu.CompilerParams(vmem_limit_bytes=24 << 20),
-        cost_estimate=work(2.5),
+        cost_estimate=work(2.0),
         name="solve",
     )(*parts, beam, beam_turned, harmonic_basis, basis_turned, keep, lanes, mode_gain)
-    total = terms[0]
-    for k in range(1, nf_blocks):
-        total = total + exchange(terms[k], "freq", nf_blocks, k).astype(jnp.float32)
-    return total.astype(jnp.bfloat16).transpose(1, 0, 2)[:, :, None, :]
+    others = []
+    for k in steps:
+        others.append(exchange(y, "freq", nf_blocks, k))
+    near_sum, beams = pl.pallas_call(
+        near_terms_kernel,
+        out_shape=[
+            shape((kept * local_modes, degrees), jnp.float32),
+            shape((nf_blocks - 1, 2 * n, degrees), jnp.bfloat16),
+        ],
+        in_specs=[VMEM] * (2 + len(peer_rows)),
+        out_specs=[VMEM] * 2,
+        compiler_params=pltpu.CompilerParams(vmem_limit_bytes=16 << 20),
+        cost_estimate=work(0.5),
+        name="near_terms",
+    )(near_mixed, beam, *peer_rows)
+    terms = pl.pallas_call(
+        terms_kernel,
+        out_shape=shape((kept, local_modes, degrees), jnp.bfloat16),
+        in_specs=[VMEM] * (5 + len(others)),
+        out_specs=VMEM,
+        compiler_params=pltpu.CompilerParams(vmem_limit_bytes=16 << 20),
+        cost_estimate=work(1.0),
+        name="terms",
+    )(near_sum, beams, lanes, mode_gain, harmonic_basis, *others)
+    return terms.transpose(1, 0, 2)[:, :, None, :]
 
 
 def solution(mesh):

time: 19.4 us -> 23 us (1.19)
  waiting for transfers between devices: 4.41 us -> 6.84 us
  starting transfers between devices: 8.91 us -> 10 us
  Pallas kernels: 4.7 us -> 5.57 us
  other arithmetic: 0.65 us -> 0 us
    ppermute x3 -> x5, waiting for transfers between devices: 3.47 us -> 5.88 us  [exchange(): return lax.ppermute(array, axis, pairs)]
    ppermute x3 -> x5, starting transfers between devices: 2.81 us -> 5.01 us  [exchange(): return lax.ppermute(array, axis, pairs)]
    ppermute x4, starting transfers between devices: 6.1 us -> 5.01 us  [on_device(): lax.ppermute(mine[k + 1], ('ma', 'pol'), list(enumerate(targets)))]
    pallas_call x1 -> x3, Pallas kernels: 2.39 us -> 3.25 us  [the longest x1 1.94 us: on_device(): pl.pallas_call(functools.partial(solve_kernel, plan), out_shape=[shape((l...]
    another operation x1 -> x0, other arithmetic: 0.65 us -> none  [on_device(): return total.astype(jnp.bfloat16).transpose(1, 0, 2)[:, :, None, :]]
  transfers between devices with their start and end apart: 7 -> 9, of which waited for: 4 -> 4; matrix products, arithmetic and copies ran while one was open for 0% -> 0% of each run, Pallas kernels for 12% -> 19%
where the time goes in v6:
time: 23 us; the launch traced here: 22.9 us
  starting transfers between devices  10 us (43%)
  waiting for transfers between devices  6.84 us (30%)
  Pallas kernels  5.57 us (24%)
  local copies, waits for them, and re-layouts  0.36 us (2%)
    ppermute x5, waiting for transfers between devices, exchange(): return lax.ppermute(array, axis, pairs)  5.88 us
    ppermute x4, starting transfers between devices, on_device(): lax.ppermute(mine[k + 1], ('ma', 'pol'), list(enumerate(targets)))  5.01 us
    ppermute x5, starting transfers between devices, exchange(): return lax.ppermute(array, axis, pairs)  5.01 us
    pallas_call x1, Pallas kernels, on_device(): pl.pallas_call(functools.partial(solve_kernel, plan), out_shape=[shape((l...  1.94 us
    pallas_call x1, Pallas kernels, on_device(): pl.pallas_call(terms_kernel, out_shape=shape((kept, local_modes, degrees)...  1.12 us
    ppermute x4, waiting for transfers between devices, on_device(): lax.ppermute(mine[k + 1], ('ma', 'pol'), list(enumerate(targets)))  0.95 us
    pallas_call x1, Pallas kernels, on_device(): pl.pallas_call(functools.partial(table_kernel, ntime), out_shape=[shape((...  0.61 us
    pallas_call x1, Pallas kernels, on_device(): pl.pallas_call(functools.partial(far_kernel, plan), out_shape=[shape((loc...  0.59 us
  transfers between devices with their start and end apart: 9, of which 4 were waited for; matrix products, arithmetic and copies ran while one was open for 0% of the time, Pallas kernels for 19%

profile of v6, /device:TPU:0, one launch (start us, length us, event | category | flops | bytes accessed | tf_op | source)
XLA Modules:
  0.0 22.9 jit_solution(10998897419504445012)
XLA Ops:
  0.0 0.5 %collective-permute-start = (bf16[4,2,32,2048]{3,2,1,0:T(8,128)(2,1)}, bf16[4,2,32,2048]{3,2,1,0:T(8,128)(2,1)S(1)}, u32[]{:S(2)}, u32[]{:S(2)}) collective-permute-start(bf16[4,2,32,2048]{3,2,1,0:T(8,128)(2,1)} %vis_ref.1), channel_id=1, source_target_pairs={{0,1},{1,0},{2,3},{3,2},{4,5},{5,4},{6,7},{7,6},{8,9},{9,8},{10,11... | collective-permute-start | bytes 3145736 | tf_op jit(solution)/shard_map/ppermute | solution.py:37
  0.5 2.5 %collective-permute-start.6 = (bf16[4,32,768]{2,1,0:T(8,128)(2,1)}, bf16[4,32,768]{2,1,0:T(8,128)(2,1)S(1)}, u32[]{:S(2)}, u32[]{:S(2)}) collective-permute-start(bf16[4,32,768]{2,1,0:T(8,128)(2,1)} %rows_own.1), channel_id=1, source_target_pairs={{0,2},{2,0},{1,3},{3,1},{4,6},{6,4},{5,7},{7,5},{8,10},{10,8},{9,1... | collective-permute-start | bytes 589832 | tf_op jit(solution)/shard_map/ppermute | solution.py:37
  3.0 0.6 %tables.1 = (bf16[192,2048]{1,0:T(8,128)(2,1)S(1)}, bf16[192,2048]{1,0:T(8,128)(2,1)S(1)}) custom-call(), custom_call_target="tpu_custom_call" | custom-call | flops 1000000000 | bytes 262144 | tf_op jit(solution)/shard_map/tables/pallas_call | solution.py:227
  3.6 0.0 copy-done
  3.7 0.0 copy-start.2
  3.7 0.6 %near.1.near_ref = bf16[192,128]{1,0:T(8,128)(2,1)S(1)} custom-call(bf16[4,2,32,2048]{3,2,1,0:T(8,128)(2,1)S(1)} %copy-done, bf16[192,2048]{1,0:T(8,128)(2,1)S(1)} %get-tuple-element.23.cos_ref, bf16[192,2048]{1,0:T(8,128)(2,1)S(1)} %get-tuple-element.24.sin_ref), custom_call_target="tpu_custom_call" | custom-call | flops 500000000 | bytes 262144 | tf_op jit(solution)/shard_map/near/pallas_call | solution.py:235
  4.3 0.3 %copy-done.2 = bf16[4,32,768]{2,1,0:T(8,128)(2,1)S(1)} copy-done((bf16[4,32,768]{2,1,0:T(8,128)(2,1)S(1)}, bf16[4,32,768]{2,1,0:T(8,128)(2,1)}, u32[]{:S(2)}) %copy-start.2) | copy-done | bytes 196632
  4.6 0.2 collective-permute-start.5
  4.8 4.0 %collective-permute-done.6.refs_0_ = bf16[4,32,768]{2,1,0:T(8,128)(2,1)S(1)} collective-permute-done((bf16[4,32,768]{2,1,0:T(8,128)(2,1)}, bf16[4,32,768]{2,1,0:T(8,128)(2,1)S(1)}, u32[]{:S(2)}, u32[]{:S(2)}) %collective-permute-start.6) | collective-permute-done | bytes 196640 | tf_op jit(solution)/shard_map/ppermute | solution.py:37
  8.8 0.0 collective-permute-start.7
  8.8 0.0 collective-permute-done.vis_ref
  8.8 0.6 %far.1 = (bf16[48,256]{1,0:T(8,128)(2,1)S(1)}, bf16[48,256]{1,0:T(8,128)(2,1)S(1)}, bf16[48,256]{1,0:T(8,128)(2,1)S(1)}, bf16[48,256]{1,0:T(8,128)(2,1)S(1)}, bf16[48,256]{1,0:T(8,128)(2,1)S(1)}) custom-call(bf16[4,2,32,2048]{3,2,1,0:T(8,128)(2,1)S(1)} %collective-permute-done.vis_ref, bf16[192,2048]{1,0:T(8,128)(2,1)S(1)} %get-tuple-element.23.cos_ref, ...), custom_call_target="tpu_custom_call" | custom-call | flops 500000000 | bytes 262144 | tf_op jit(solution)/shard_map/far/pallas_call | solution.py:247
  9.4 0.6 %collective-permute-start.1 = (bf16[48,256]{1,0:T(8,128)(2,1)S(1)}, bf16[48,256]{1,0:T(8,128)(2,1)S(1)}, u32[]{:S(2)}, u32[]{:S(2)}) collective-permute-start(bf16[48,256]{1,0:T(8,128)(2,1)S(1)} %get-tuple-element.27), channel_id=1, source_target_pairs={{0,1},{1,9},{4,5},{5,13},{8,0},{9,8},{12,4},{13,12},{2,3},{3,11},{... | collective-permute-start | bytes 73736 | tf_op jit(solution)/shard_map/ppermute | solution.py:259
  9.9 1.8 %collective-permute-start.2 = (bf16[48,256]{1,0:T(8,128)(2,1)S(1)}, bf16[48,256]{1,0:T(8,128)(2,1)S(1)}, u32[]{:S(2)}, u32[]{:S(2)}) collective-permute-start(bf16[48,256]{1,0:T(8,128)(2,1)S(1)} %get-tuple-element.28), channel_id=1, source_target_pairs={{0,4},{1,13},{4,8},{5,9},{8,12},{9,5},{12,0},{13,1},{2,6},{3,15},{... | collective-permute-start | bytes 73736 | tf_op jit(solution)/shard_map/ppermute | solution.py:259
  11.8 2.0 %collective-permute-start.3 = (bf16[48,256]{1,0:T(8,128)(2,1)S(1)}, bf16[48,256]{1,0:T(8,128)(2,1)S(1)}, u32[]{:S(2)}, u32[]{:S(2)}) collective-permute-start(bf16[48,256]{1,0:T(8,128)(2,1)S(1)} %get-tuple-element.29), channel_id=1, source_target_pairs={{0,12},{1,5},{4,0},{5,1},{8,4},{9,13},{12,8},{13,9},{2,14},{3,7},{... | collective-permute-start | bytes 73736 | tf_op jit(solution)/shard_map/ppermute | solution.py:259
  13.8 0.0 collective-permute-done.5.rows_other
  13.8 0.6 %collective-permute-start.4 = (bf16[48,256]{1,0:T(8,128)(2,1)S(1)}, bf16[48,256]{1,0:T(8,128)(2,1)S(1)}, u32[]{:S(2)}, u32[]{:S(2)}) collective-permute-start(bf16[48,256]{1,0:T(8,128)(2,1)S(1)} %get-tuple-element.30), channel_id=1, source_target_pairs={{0,8},{1,0},{4,12},{5,4},{8,9},{9,1},{12,13},{13,5},{2,10},{3,2},{... | collective-permute-start | bytes 73736 | tf_op jit(solution)/shard_map/ppermute | solution.py:259
  14.4 0.0 copy-done.1
  14.4 0.0 copy-done.4
  14.4 0.0 copy-done.5
  14.4 0.5 %prepare.1 = (bf16[256,768]{1,0:T(8,128)(2,1)S(1)}, bf16[768,256]{1,0:T(8,128)(2,1)S(1)}, bf16[768,768]{1,0:T(8,128)(2,1)S(1)}, f32[192,256]{1,0:T(8,128)S(1)}, f32[3,256]{1,0:T(4,128)S(1)}) custom-call(bf16[4,32,768]{2,1,0:T(8,128)(2,1)S(1)} %copy-done.2, bf16[4,32,768]{2,1,0:T(8,128)(2,1)S(1)} %collective-permute-done.5.rows_other, ...), custom_call_target="tpu_custom_call" | custom-call | flops 700000000 | bytes 262144 | tf_op jit(solution)/shard_map/prepare/pallas_call | solution.py:260
  14.9 0.0 collective-permute-done.1.refs_1_
  14.9 0.8 %collective-permute-done.2.refs_2_ = bf16[48,256]{1,0:T(8,128)(2,1)S(1)} collective-permute-done((bf16[48,256]{1,0:T(8,128)(2,1)S(1)}, bf16[48,256]{1,0:T(8,128)(2,1)S(1)}, u32[]{:S(2)}, u32[]{:S(2)}) %collective-permute-start.2) | collective-permute-done | bytes 24608 | tf_op jit(solution)/shard_map/ppermute | solution.py:259
  15.8 0.1 collective-permute-done.3.refs_3_
  15.8 0.0 collective-permute-done.4.refs_4_
  15.9 0.0 copy-done.3
  15.9 1.9 %solve.1 = (bf16[48,256]{1,0:T(8,128)(2,1)S(1)}, bf16[48,256]{1,0:T(8,128)(2,1)S(1)}) custom-call(bf16[48,256]{1,0:T(8,128)(2,1)S(1)} %get-tuple-element.26.refs_0_, bf16[48,256]{1,0:T(8,128)(2,1)S(1)} %collective-permute-done.1.refs_1_, bf16[48,256]{1,0:T(8,128)(2,1)S(1)} %collective-permute-done.2.refs_2_, ...), custom_call_target="tpu_custom_call" | custom-call | flops 2000000000 | bytes 262144 | tf_op jit(solution)/shard_map/solve/pallas_call | solution.py:279
  17.8 1.8 %collective-permute-start.8 = (bf16[48,256]{1,0:T(8,128)(2,1)S(1)}, bf16[48,256]{1,0:T(8,128)(2,1)S(1)}, u32[]{:S(2)}, u32[]{:S(2)}) collective-permute-start(bf16[48,256]{1,0:T(8,128)(2,1)S(1)} %get-tuple-element.40), channel_id=1, source_target_pairs={{0,2},{2,0},{1,3},{3,1},{4,6},{6,4},{5,7},{7,5},{8,10},{10,8},{9,1... | collective-permute-start | bytes 73736 | tf_op jit(solution)/shard_map/ppermute | solution.py:37
  19.7 0.0 collective-permute-done.7.refs_1_
  19.7 0.2 near_terms.1
  19.9 1.9 %collective-permute-done.8.refs_0_ = bf16[48,256]{1,0:T(8,128)(2,1)S(1)} collective-permute-done((bf16[48,256]{1,0:T(8,128)(2,1)S(1)}, bf16[48,256]{1,0:T(8,128)(2,1)S(1)}, u32[]{:S(2)}, u32[]{:S(2)}) %collective-permute-start.8) | collective-permute-done | bytes 24608 | tf_op jit(solution)/shard_map/ppermute | solution.py:37
  21.7 1.1 %terms.1 = bf16[1,48,768]{2,1,0:T(8,128)(2,1)} custom-call(f32[48,768]{1,0:T(8,128)S(1)} %get-tuple-element.38.sum_ref, bf16[1,256,768]{2,1,0:T(8,128)(2,1)S(1)} %get-tuple-element.39.beams_ref, f32[3,256]{1,0:T(4,128)S(1)} %get-tuple-element.36.refs_10_.lanes_ref, f32[48,768]{1,0:T(8,128)S(1)} %copy-done.3, bf16[768,768]{1,0:T(8,128)(2,1)S(1)} %copy-done.1, ...), custom_call_target="tpu_custom_call" | custom-call | flops 1000000000 | bytes 262144 | tf_op jit(solution)/shard_map/terms/pallas_call | solution.py:303
  (5 shorter events, 0.0 us)
Async XLA Ops:
  0.0 3.6 %copy-start = (bf16[4,2,32,2048]{3,2,1,0:T(8,128)(2,1)S(1)}, bf16[4,2,32,2048]{3,2,1,0:T(8,128)(2,1)}, u32[]{:S(2)}) copy-start(bf16[4,2,32,2048]{3,2,1,0:T(8,128)(2,1)} %vis_ref.1) | copy-start | bytes 3145732
  0.0 8.8 %collective-permute-start = (bf16[4,2,32,2048]{3,2,1,0:T(8,128)(2,1)}, bf16[4,2,32,2048]{3,2,1,0:T(8,128)(2,1)S(1)}, u32[]{:S(2)}, u32[]{:S(2)}) collective-permute-start(bf16[4,2,32,2048]{3,2,1,0:T(8,128)(2,1)} %vis_ref.1), channel_id=1, source_target_pairs={{0,1},{1,0},{2,3},{3,2},{4,5},{5,4},{6,7},{7,6},{8,9},{9,8},{10,11... | collective-permute-start | bytes 3145736 | tf_op jit(solution)/shard_map/ppermute | solution.py:37
  0.5 8.3 %collective-permute-start.6 = (bf16[4,32,768]{2,1,0:T(8,128)(2,1)}, bf16[4,32,768]{2,1,0:T(8,128)(2,1)S(1)}, u32[]{:S(2)}, u32[]{:S(2)}) collective-permute-start(bf16[4,32,768]{2,1,0:T(8,128)(2,1)} %rows_own.1), channel_id=1, source_target_pairs={{0,2},{2,0},{1,3},{3,1},{4,6},{6,4},{5,7},{7,5},{8,10},{10,8},{9,1... | collective-permute-start | bytes 589832 | tf_op jit(solution)/shard_map/ppermute | solution.py:37
  3.7 0.9 %copy-start.2 = (bf16[4,32,768]{2,1,0:T(8,128)(2,1)S(1)}, bf16[4,32,768]{2,1,0:T(8,128)(2,1)}, u32[]{:S(2)}) copy-start(bf16[4,32,768]{2,1,0:T(8,128)(2,1)} %rows_own.1) | copy-start | bytes 589828
  4.6 9.8 %copy-start.1 = (bf16[768,768]{1,0:T(8,128)(2,1)S(1)}, bf16[768,768]{1,0:T(8,128)(2,1)}, u32[]{:S(2)}) copy-start(bf16[768,768]{1,0:T(8,128)(2,1)} %basis_ref.3) | copy-start | bytes 3538948
  4.6 9.8 %copy-start.4 = (f32[4]{0:T(128)S(1)}, f32[4]{0:T(128)}, u32[]{:S(2)}) copy-start(f32[4]{0:T(128)} %param.10) | copy-start | bytes 52
  4.6 9.8 %copy-start.5 = (bf16[2,8]{1,0:T(2,128)(2,1)S(1)}, bf16[2,8]{1,0:T(2,128)(2,1)}, u32[]{:S(2)}) copy-start(bf16[2,8]{1,0:T(2,128)(2,1)} %kl_ref.1) | copy-start | bytes 100
  4.6 9.2 %collective-permute-start.5 = (bf16[4,32,768]{2,1,0:T(8,128)(2,1)S(1)}, bf16[4,32,768]{2,1,0:T(8,128)(2,1)S(1)}, u32[]{:S(2)}, u32[]{:S(2)}) collective-permute-start(bf16[4,32,768]{2,1,0:T(8,128)(2,1)S(1)} %copy-done.2), channel_id=1, source_target_pairs={{0,1},{1,0},{2,3},{3,2},{4,5},{5,4},{6,7},{7,6},{8,9},{9,8},{10,11... | collective-permute-start | bytes 589832 | tf_op jit(solution)/shard_map/ppermute | solution.py:37
  8.8 10.9 %collective-permute-start.7 = (bf16[4,32,768]{2,1,0:T(8,128)(2,1)S(1)}, bf16[4,32,768]{2,1,0:T(8,128)(2,1)S(1)}, u32[]{:S(2)}, u32[]{:S(2)}) collective-permute-start(bf16[4,32,768]{2,1,0:T(8,128)(2,1)S(1)} %collective-permute-done.6.refs_0_), channel_id=1, source_target_pairs={{0,1},{1,0},{2,3},{3,2},{4,5},{5,4},{6,7},{7,6},{8,9},{9,8},{10,11... | collective-permute-start | bytes 589832 | tf_op jit(solution)/shard_map/ppermute | solution.py:37
  9.4 5.6 %collective-permute-start.1 = (bf16[48,256]{1,0:T(8,128)(2,1)S(1)}, bf16[48,256]{1,0:T(8,128)(2,1)S(1)}, u32[]{:S(2)}, u32[]{:S(2)}) collective-permute-start(bf16[48,256]{1,0:T(8,128)(2,1)S(1)} %get-tuple-element.27), channel_id=1, source_target_pairs={{0,1},{1,9},{4,5},{5,13},{8,0},{9,8},{12,4},{13,12},{2,3},{3,11},{... | collective-permute-start | bytes 73736 | tf_op jit(solution)/shard_map/ppermute | solution.py:259
  9.9 5.8 %collective-permute-start.2 = (bf16[48,256]{1,0:T(8,128)(2,1)S(1)}, bf16[48,256]{1,0:T(8,128)(2,1)S(1)}, u32[]{:S(2)}, u32[]{:S(2)}) collective-permute-start(bf16[48,256]{1,0:T(8,128)(2,1)S(1)} %get-tuple-element.28), channel_id=1, source_target_pairs={{0,4},{1,13},{4,8},{5,9},{8,12},{9,5},{12,0},{13,1},{2,6},{3,15},{... | collective-permute-start | bytes 73736 | tf_op jit(solution)/shard_map/ppermute | solution.py:259
  11.8 4.1 %collective-permute-start.3 = (bf16[48,256]{1,0:T(8,128)(2,1)S(1)}, bf16[48,256]{1,0:T(8,128)(2,1)S(1)}, u32[]{:S(2)}, u32[]{:S(2)}) collective-permute-start(bf16[48,256]{1,0:T(8,128)(2,1)S(1)} %get-tuple-element.29), channel_id=1, source_target_pairs={{0,12},{1,5},{4,0},{5,1},{8,4},{9,13},{12,8},{13,9},{2,14},{3,7},{... | collective-permute-start | bytes 73736 | tf_op jit(solution)/shard_map/ppermute | solution.py:259
  13.8 2.1 %collective-permute-start.4 = (bf16[48,256]{1,0:T(8,128)(2,1)S(1)}, bf16[48,256]{1,0:T(8,128)(2,1)S(1)}, u32[]{:S(2)}, u32[]{:S(2)}) collective-permute-start(bf16[48,256]{1,0:T(8,128)(2,1)S(1)} %get-tuple-element.30), channel_id=1, source_target_pairs={{0,8},{1,0},{4,12},{5,4},{8,9},{9,1},{12,13},{13,5},{2,10},{3,2},{... | collective-permute-start | bytes 73736 | tf_op jit(solution)/shard_map/ppermute | solution.py:259
  14.4 1.5 %copy-start.3 = (f32[48,768]{1,0:T(8,128)S(1)}, f32[48,768]{1,0:T(8,128)}, u32[]{:S(2)}) copy-start(f32[48,768]{1,0:T(8,128)} %gain_ref.1) | copy-start | bytes 442372
  17.8 3.9 %collective-permute-start.8 = (bf16[48,256]{1,0:T(8,128)(2,1)S(1)}, bf16[48,256]{1,0:T(8,128)(2,1)S(1)}, u32[]{:S(2)}, u32[]{:S(2)}) collective-permute-start(bf16[48,256]{1,0:T(8,128)(2,1)S(1)} %get-tuple-element.40), channel_id=1, source_target_pairs={{0,2},{2,0},{1,3},{3,1},{4,6},{6,4},{5,7},{7,5},{8,10},{10,8},{9,1... | collective-permute-start | bytes 73736 | tf_op jit(solution)/shard_map/ppermute | solution.py:37

commit v7 on v6

--- a/solution.py
+++ b/solution.py
@@ -13,10 +13,11 @@
 ITERS = 2
 LANES = 128
 LINE_OF_FOUR = (
-    (1, 5, 3, 7, 0, 4, 2, 6),
-    (2, 7, 4, 5, 6, 3, 0, 1),
-    (6, 3, 0, 1, 2, 7, 4, 5),
-    (4, 0, 6, 2, 5, 1, 7, 3),
+    (1, 5, 3, 2, 0, 4, 7, 6),
+    (2, 7, 3, 5, 6, 4, 0, 1),
+    (4, 3, 0, 7, 5, 1, 2, 6),
+    (6, 0, 4, 1, 2, 3, 7, 5),
+    (1, 0, 6, 2, 5, 7, 4, 3),
 )
 NT_DIMS = (((1,), (1,)), ((), ()))
 VMEM = pl.BlockSpec(memory_space=pltpu.VMEM)
@@ -224,6 +225,7 @@
     peer_rows = []
     for k in steps:
         peer_rows.append(exchange(beam_rows, "freq", nf_blocks, k))
+    other_rows = exchange(beam_rows, "pol", 2, 1)
     cos, sin = pl.pallas_call(
         functools.partial(table_kernel, ntime),
         out_shape=[shape((modes, ntime), jnp.bfloat16)] * 2,
@@ -241,8 +243,6 @@
         cost_estimate=work(0.5),
         name="near",
     )(visibility, cos, sin)
-    near, late_rows = lax.optimization_barrier((near, beam_rows))
-    other_rows = exchange(late_rows, "pol", 2, 1)
     plan = scatter_plan(blocks)
     mine = pl.pallas_call(
         functools.partial(far_kernel, plan),

time: 23 us -> 22.2 us (0.965)
  waiting for transfers between devices: 6.84 us -> 6.23 us
  local copies, waits for them, and re-layouts: 0.36 us -> 0.04 us
    ppermute x5, waiting for transfers between devices: 5.88 us -> 5.51 us  [exchange(): return lax.ppermute(array, axis, pairs)]
    unnamed x12, local copies, waits for them, and re-layouts: 0.36 us -> 0.04 us
    ppermute x4 -> x5, waiting for transfers between devices: 0.95 us -> 0.72 us  [on_device(): lax.ppermute(mine[k + 1], ('ma', 'pol'), list(enumerate(targets)))]
    ppermute x4 -> x5, starting transfers between devices: 5.01 us -> 4.99 us  [on_device(): lax.ppermute(mine[k + 1], ('ma', 'pol'), list(enumerate(targets)))]
  transfers between devices with their start and end apart: 9 -> 10, of which waited for: 4 -> 5; matrix products, arithmetic and copies ran while one was open for 0% -> 0% of each run, Pallas kernels for 19% -> 20%
where the time goes in v7:
time: 22.2 us; the launch traced here: 22 us
  starting transfers between devices  10 us (45%)
  waiting for transfers between devices  6.23 us (28%)
  Pallas kernels  5.61 us (25%)
    ppermute x5, waiting for transfers between devices, exchange(): return lax.ppermute(array, axis, pairs)  5.51 us
    ppermute x5, starting transfers between devices, exchange(): return lax.ppermute(array, axis, pairs)  5.04 us
    ppermute x5, starting transfers between devices, on_device(): lax.ppermute(mine[k + 1], ('ma', 'pol'), list(enumerate(targets)))  4.99 us
    pallas_call x1, Pallas kernels, on_device(): pl.pallas_call(functools.partial(solve_kernel, plan), out_shape=[shape((l...  1.95 us
    pallas_call x1, Pallas kernels, on_device(): pl.pallas_call(terms_kernel, out_shape=shape((kept, local_modes, degrees)...  1.12 us
    ppermute x5, waiting for transfers between devices, on_device(): lax.ppermute(mine[k + 1], ('ma', 'pol'), list(enumerate(targets)))  0.72 us
    pallas_call x1, Pallas kernels, on_device(): pl.pallas_call(functools.partial(table_kernel, ntime), out_shape=[shape((...  0.64 us
    pallas_call x1, Pallas kernels, on_device(): pl.pallas_call(functools.partial(far_kernel, plan), out_shape=[shape((loc...  0.59 us
  transfers between devices with their start and end apart: 10, of which 5 were waited for; matrix products, arithmetic and copies ran while one was open for 0% of the time, Pallas kernels for 20%

profile of v7, /device:TPU:0, one launch (start us, length us, event | category | flops | bytes accessed | tf_op | source)
XLA Modules:
  0.0 22.0 jit_solution(7003415638175025922)
XLA Ops:
  0.0 0.5 %collective-permute-start = (bf16[4,2,32,2048]{3,2,1,0:T(8,128)(2,1)}, bf16[4,2,32,2048]{3,2,1,0:T(8,128)(2,1)S(1)}, u32[]{:S(2)}, u32[]{:S(2)}) collective-permute-start(bf16[4,2,32,2048]{3,2,1,0:T(8,128)(2,1)} %vis_ref.1), channel_id=1, source_target_pairs={{0,1},{1,0},{2,3},{3,2},{4,5},{5,4},{6,7},{7,6},{8,9},{9,8},{10,11... | collective-permute-start | bytes 3145736 | tf_op jit(solution)/shard_map/ppermute | solution.py:38
  0.5 0.1 collective-permute-start.6
  0.6 2.9 %collective-permute-start.7 = (bf16[4,32,768]{2,1,0:T(8,128)(2,1)}, bf16[4,32,768]{2,1,0:T(8,128)(2,1)S(1)}, u32[]{:S(2)}, u32[]{:S(2)}) collective-permute-start(bf16[4,32,768]{2,1,0:T(8,128)(2,1)} %rows_own.1), channel_id=1, source_target_pairs={{0,2},{2,0},{1,3},{3,1},{4,6},{6,4},{5,7},{7,5},{8,10},{10,8},{9,1... | collective-permute-start | bytes 589832 | tf_op jit(solution)/shard_map/ppermute | solution.py:38
  3.5 0.6 %tables.1 = (bf16[192,2048]{1,0:T(8,128)(2,1)S(1)}, bf16[192,2048]{1,0:T(8,128)(2,1)S(1)}) custom-call(), custom_call_target="tpu_custom_call" | custom-call | flops 1000000000 | bytes 262144 | tf_op jit(solution)/shard_map/tables/pallas_call | solution.py:229
  4.1 0.6 %near.1.near_ref = bf16[192,128]{1,0:T(8,128)(2,1)S(1)} custom-call(bf16[4,2,32,2048]{3,2,1,0:T(8,128)(2,1)S(1)} %copy-done, bf16[192,2048]{1,0:T(8,128)(2,1)S(1)} %get-tuple-element.22.cos_ref, bf16[192,2048]{1,0:T(8,128)(2,1)S(1)} %get-tuple-element.23.sin_ref), custom_call_target="tpu_custom_call" | custom-call | flops 500000000 | bytes 262144 | tf_op jit(solution)/shard_map/near/pallas_call | solution.py:237
  4.7 0.0 copy-start.1
  4.7 0.0 copy-start.2
  4.7 0.0 copy-start.4
  4.8 0.0 copy-start.5
  4.8 0.0 collective-permute-done.vis_ref
  4.8 0.6 %far.1 = (bf16[48,256]{1,0:T(8,128)(2,1)S(1)}, bf16[48,256]{1,0:T(8,128)(2,1)S(1)}, bf16[48,256]{1,0:T(8,128)(2,1)S(1)}, bf16[48,256]{1,0:T(8,128)(2,1)S(1)}, bf...) custom-call(bf16[4,2,32,2048]{3,2,1,0:T(8,128)(2,1)S(1)} %collective-permute-done.vis_ref, ...), custom_call_target="tpu_custom_call" | custom-call | flops 500000000 | bytes 262144 | tf_op jit(solution)/shard_map/far/pallas_call | solution.py:247
  5.4 0.1 collective-permute-start.1
  5.4 3.4 %collective-permute-done.7.refs_0_ = bf16[4,32,768]{2,1,0:T(8,128)(2,1)S(1)} collective-permute-done((bf16[4,32,768]{2,1,0:T(8,128)(2,1)}, bf16[4,32,768]{2,1,0:T(8,128)(2,1)S(1)}, u32[]{:S(2)}, u32[]{:S(2)}) %collective-permute-start.7) | collective-permute-done | bytes 196640 | tf_op jit(solution)/shard_map/ppermute | solution.py:38
  8.8 0.0 collective-permute-start.8
  8.8 1.8 %collective-permute-start.2 = (bf16[48,256]{1,0:T(8,128)(2,1)S(1)}, bf16[48,256]{1,0:T(8,128)(2,1)S(1)}, u32[]{:S(2)}, u32[]{:S(2)}) collective-permute-start(bf16[48,256]{1,0:T(8,128)(2,1)S(1)} %get-tuple-element.26), channel_id=1, source_target_pairs={{0,4},{1,13},{4,5},{5,9},{8,12},{9,8},{12,0},{13,1},{2,6},{3,15},{... | collective-permute-start | bytes 73736 | tf_op jit(solution)/shard_map/ppermute | solution.py:259
  10.7 2.6 %collective-permute-start.3 = (bf16[48,256]{1,0:T(8,128)(2,1)S(1)}, bf16[48,256]{1,0:T(8,128)(2,1)S(1)}, u32[]{:S(2)}, u32[]{:S(2)}) collective-permute-start(bf16[48,256]{1,0:T(8,128)(2,1)S(1)} %get-tuple-element.27), channel_id=1, source_target_pairs={{0,8},{1,5},{4,0},{5,13},{8,9},{9,1},{12,4},{13,12},{2,10},{3,7},{... | collective-permute-start | bytes 73736 | tf_op jit(solution)/shard_map/ppermute | solution.py:259
  13.2 0.0 collective-permute-done.6.rows_other
  13.2 0.3 %collective-permute-start.4 = (bf16[48,256]{1,0:T(8,128)(2,1)S(1)}, bf16[48,256]{1,0:T(8,128)(2,1)S(1)}, u32[]{:S(2)}, u32[]{:S(2)}) collective-permute-start(bf16[48,256]{1,0:T(8,128)(2,1)S(1)} %get-tuple-element.28), channel_id=1, source_target_pairs={{0,12},{1,0},{4,8},{5,1},{8,4},{9,5},{12,13},{13,9},{2,14},{3,2},{... | collective-permute-start | bytes 73736 | tf_op jit(solution)/shard_map/ppermute | solution.py:259
  13.5 0.0 collective-permute-done.1.refs_1_
  13.5 0.2 %collective-permute-start.5 = (bf16[48,256]{1,0:T(8,128)(2,1)S(1)}, bf16[48,256]{1,0:T(8,128)(2,1)S(1)}, u32[]{:S(2)}, u32[]{:S(2)}) collective-permute-start(bf16[48,256]{1,0:T(8,128)(2,1)S(1)} %get-tuple-element.29), channel_id=1, source_target_pairs={{0,1},{1,0},{4,12},{5,4},{8,9},{9,13},{12,8},{13,5},{2,3},{3,2},{6... | collective-permute-start | bytes 73736 | tf_op jit(solution)/shard_map/ppermute | solution.py:259
  13.8 0.0 copy-start.3
  13.8 0.5 %prepare.1 = (bf16[256,768]{1,0:T(8,128)(2,1)S(1)}, bf16[768,256]{1,0:T(8,128)(2,1)S(1)}, bf16[768,768]{1,0:T(8,128)(2,1)S(1)}, f32[192,256]{1,0:T(8,128)S(1)}, f32[3,256]{1,0:T(4,128)S(1)}) custom-call(bf16[4,32,768]{2,1,0:T(8,128)(2,1)S(1)} %copy-done.2, bf16[4,32,768]{2,1,0:T(8,128)(2,1)S(1)} %collective-permute-done.6.rows_other, ...), custom_call_target="tpu_custom_call" | custom-call | flops 700000000 | bytes 262144 | tf_op jit(solution)/shard_map/prepare/pallas_call | solution.py:260
  14.3 0.3 %collective-permute-done.2.refs_2_ = bf16[48,256]{1,0:T(8,128)(2,1)S(1)} collective-permute-done((bf16[48,256]{1,0:T(8,128)(2,1)S(1)}, bf16[48,256]{1,0:T(8,128)(2,1)S(1)}, u32[]{:S(2)}, u32[]{:S(2)}) %collective-permute-start.2) | collective-permute-done | bytes 24608 | tf_op jit(solution)/shard_map/ppermute | solution.py:259
  14.6 0.2 %collective-permute-done.3.refs_3_ = bf16[48,256]{1,0:T(8,128)(2,1)S(1)} collective-permute-done((bf16[48,256]{1,0:T(8,128)(2,1)S(1)}, bf16[48,256]{1,0:T(8,128)(2,1)S(1)}, u32[]{:S(2)}, u32[]{:S(2)}) %collective-permute-start.3) | collective-permute-done | bytes 24608 | tf_op jit(solution)/shard_map/ppermute | solution.py:259
  14.8 0.2 %collective-permute-done.4.refs_4_ = bf16[48,256]{1,0:T(8,128)(2,1)S(1)} collective-permute-done((bf16[48,256]{1,0:T(8,128)(2,1)S(1)}, bf16[48,256]{1,0:T(8,128)(2,1)S(1)}, u32[]{:S(2)}, u32[]{:S(2)}) %collective-permute-start.4) | collective-permute-done | bytes 24608 | tf_op jit(solution)/shard_map/ppermute | solution.py:259
  15.0 0.0 collective-permute-done.5.refs_5_
  15.1 2.0 %solve.1 = (bf16[48,256]{1,0:T(8,128)(2,1)S(1)}, bf16[48,256]{1,0:T(8,128)(2,1)S(1)}) custom-call(bf16[48,256]{1,0:T(8,128)(2,1)S(1)} %get-tuple-element.24.refs_0_, bf16[48,256]{1,0:T(8,128)(2,1)S(1)} %collective-permute-done.1.refs_1_, bf16[48,256]{1,0:T(8,128)(2,1)S(1)} %collective-permute-done.2.refs_2_, ...), custom_call_target="tpu_custom_call" | custom-call | flops 2000000000 | bytes 262144 | tf_op jit(solution)/shard_map/solve/pallas_call | solution.py:279
  17.0 1.6 %collective-permute-start.9 = (bf16[48,256]{1,0:T(8,128)(2,1)S(1)}, bf16[48,256]{1,0:T(8,128)(2,1)S(1)}, u32[]{:S(2)}, u32[]{:S(2)}) collective-permute-start(bf16[48,256]{1,0:T(8,128)(2,1)S(1)} %get-tuple-element.38), channel_id=1, source_target_pairs={{0,2},{2,0},{1,3},{3,1},{4,6},{6,4},{5,7},{7,5},{8,10},{10,8},{9,1... | collective-permute-start | bytes 73736 | tf_op jit(solution)/shard_map/ppermute | solution.py:38
  18.6 0.0 collective-permute-done.8.refs_1_
  18.6 0.2 near_terms.1
  18.8 2.1 %collective-permute-done.9.refs_0_ = bf16[48,256]{1,0:T(8,128)(2,1)S(1)} collective-permute-done((bf16[48,256]{1,0:T(8,128)(2,1)S(1)}, bf16[48,256]{1,0:T(8,128)(2,1)S(1)}, u32[]{:S(2)}, u32[]{:S(2)}) %collective-permute-start.9) | collective-permute-done | bytes 24608 | tf_op jit(solution)/shard_map/ppermute | solution.py:38
  20.9 1.1 %terms.1 = bf16[1,48,768]{2,1,0:T(8,128)(2,1)} custom-call(f32[48,768]{1,0:T(8,128)S(1)} %get-tuple-element.36.sum_ref, bf16[1,256,768]{2,1,0:T(8,128)(2,1)S(1)} %get-tuple-element.37.beams_ref, f32[3,256]{1,0:T(4,128)S(1)} %get-tuple-element.34.refs_11_.lanes_ref, f32[48,768]{1,0:T(8,128)S(1)} %copy-done.3, bf16[768,768]{1,0:T(8,128)(2,1)S(1)} %copy-done.1, ...), custom_call_target="tpu_custom_call" | custom-call | flops 1000000000 | bytes 262144 | tf_op jit(solution)/shard_map/terms/pallas_call | solution.py:303
  (7 shorter events, 0.0 us)
Async XLA Ops:
  0.0 4.1 %copy-start = (bf16[4,2,32,2048]{3,2,1,0:T(8,128)(2,1)S(1)}, bf16[4,2,32,2048]{3,2,1,0:T(8,128)(2,1)}, u32[]{:S(2)}) copy-start(bf16[4,2,32,2048]{3,2,1,0:T(8,128)(2,1)} %vis_ref.1) | copy-start | bytes 3145732
  0.0 4.8 %collective-permute-start = (bf16[4,2,32,2048]{3,2,1,0:T(8,128)(2,1)}, bf16[4,2,32,2048]{3,2,1,0:T(8,128)(2,1)S(1)}, u32[]{:S(2)}, u32[]{:S(2)}) collective-permute-start(bf16[4,2,32,2048]{3,2,1,0:T(8,128)(2,1)} %vis_ref.1), channel_id=1, source_target_pairs={{0,1},{1,0},{2,3},{3,2},{4,5},{5,4},{6,7},{7,6},{8,9},{9,8},{10,11... | collective-permute-start | bytes 3145736 | tf_op jit(solution)/shard_map/ppermute | solution.py:38
  0.5 12.7 %collective-permute-start.6 = (bf16[4,32,768]{2,1,0:T(8,128)(2,1)}, bf16[4,32,768]{2,1,0:T(8,128)(2,1)S(1)}, u32[]{:S(2)}, u32[]{:S(2)}) collective-permute-start(bf16[4,32,768]{2,1,0:T(8,128)(2,1)} %rows_own.1), channel_id=1, source_target_pairs={{0,1},{1,0},{2,3},{3,2},{4,5},{5,4},{6,7},{7,6},{8,9},{9,8},{10,11... | collective-permute-start | bytes 589832 | tf_op jit(solution)/shard_map/ppermute | solution.py:38
  0.6 8.3 %collective-permute-start.7 = (bf16[4,32,768]{2,1,0:T(8,128)(2,1)}, bf16[4,32,768]{2,1,0:T(8,128)(2,1)S(1)}, u32[]{:S(2)}, u32[]{:S(2)}) collective-permute-start(bf16[4,32,768]{2,1,0:T(8,128)(2,1)} %rows_own.1), channel_id=1, source_target_pairs={{0,2},{2,0},{1,3},{3,1},{4,6},{6,4},{5,7},{7,5},{8,10},{10,8},{9,1... | collective-permute-start | bytes 589832 | tf_op jit(solution)/shard_map/ppermute | solution.py:38
  4.7 9.0 %copy-start.1 = (bf16[768,768]{1,0:T(8,128)(2,1)S(1)}, bf16[768,768]{1,0:T(8,128)(2,1)}, u32[]{:S(2)}) copy-start(bf16[768,768]{1,0:T(8,128)(2,1)} %basis_ref.3) | copy-start | bytes 3538948
  4.7 9.0 %copy-start.2 = (bf16[4,32,768]{2,1,0:T(8,128)(2,1)S(1)}, bf16[4,32,768]{2,1,0:T(8,128)(2,1)}, u32[]{:S(2)}) copy-start(bf16[4,32,768]{2,1,0:T(8,128)(2,1)} %rows_own.1) | copy-start | bytes 589828
  4.7 9.0 %copy-start.4 = (f32[4]{0:T(128)S(1)}, f32[4]{0:T(128)}, u32[]{:S(2)}) copy-start(f32[4]{0:T(128)} %param.10) | copy-start | bytes 52
  4.8 9.0 %copy-start.5 = (bf16[2,8]{1,0:T(2,128)(2,1)S(1)}, bf16[2,8]{1,0:T(2,128)(2,1)}, u32[]{:S(2)}) copy-start(bf16[2,8]{1,0:T(2,128)(2,1)} %kl_ref.1) | copy-start | bytes 100
  5.4 8.1 %collective-permute-start.1 = (bf16[48,256]{1,0:T(8,128)(2,1)S(1)}, bf16[48,256]{1,0:T(8,128)(2,1)S(1)}, u32[]{:S(2)}, u32[]{:S(2)}) collective-permute-start(bf16[48,256]{1,0:T(8,128)(2,1)S(1)} %get-tuple-element.25), channel_id=1, source_target_pairs={{0,1},{1,9},{4,5},{5,4},{8,0},{9,8},{12,13},{13,12},{2,3},{3,11},{... | collective-permute-start | bytes 73736 | tf_op jit(solution)/shard_map/ppermute | solution.py:259
  8.8 9.8 %collective-permute-start.8 = (bf16[4,32,768]{2,1,0:T(8,128)(2,1)S(1)}, bf16[4,32,768]{2,1,0:T(8,128)(2,1)S(1)}, u32[]{:S(2)}, u32[]{:S(2)}) collective-permute-start(bf16[4,32,768]{2,1,0:T(8,128)(2,1)S(1)} %collective-permute-done.7.refs_0_), channel_id=1, source_target_pairs={{0,1},{1,0},{2,3},{3,2},{4,5},{5,4},{6,7},{7,6},{8,9},{9,8},{10,11... | collective-permute-start | bytes 589832 | tf_op jit(solution)/shard_map/ppermute | solution.py:38
  8.8 5.8 %collective-permute-start.2 = (bf16[48,256]{1,0:T(8,128)(2,1)S(1)}, bf16[48,256]{1,0:T(8,128)(2,1)S(1)}, u32[]{:S(2)}, u32[]{:S(2)}) collective-permute-start(bf16[48,256]{1,0:T(8,128)(2,1)S(1)} %get-tuple-element.26), channel_id=1, source_target_pairs={{0,4},{1,13},{4,5},{5,9},{8,12},{9,8},{12,0},{13,1},{2,6},{3,15},{... | collective-permute-start | bytes 73736 | tf_op jit(solution)/shard_map/ppermute | solution.py:259
  10.7 4.2 %collective-permute-start.3 = (bf16[48,256]{1,0:T(8,128)(2,1)S(1)}, bf16[48,256]{1,0:T(8,128)(2,1)S(1)}, u32[]{:S(2)}, u32[]{:S(2)}) collective-permute-start(bf16[48,256]{1,0:T(8,128)(2,1)S(1)} %get-tuple-element.27), channel_id=1, source_target_pairs={{0,8},{1,5},{4,0},{5,13},{8,9},{9,1},{12,4},{13,12},{2,10},{3,7},{... | collective-permute-start | bytes 73736 | tf_op jit(solution)/shard_map/ppermute | solution.py:259
  13.2 1.8 %collective-permute-start.4 = (bf16[48,256]{1,0:T(8,128)(2,1)S(1)}, bf16[48,256]{1,0:T(8,128)(2,1)S(1)}, u32[]{:S(2)}, u32[]{:S(2)}) collective-permute-start(bf16[48,256]{1,0:T(8,128)(2,1)S(1)} %get-tuple-element.28), channel_id=1, source_target_pairs={{0,12},{1,0},{4,8},{5,1},{8,4},{9,5},{12,13},{13,9},{2,14},{3,2},{... | collective-permute-start | bytes 73736 | tf_op jit(solution)/shard_map/ppermute | solution.py:259
  13.5 1.5 %collective-permute-start.5 = (bf16[48,256]{1,0:T(8,128)(2,1)S(1)}, bf16[48,256]{1,0:T(8,128)(2,1)S(1)}, u32[]{:S(2)}, u32[]{:S(2)}) collective-permute-start(bf16[48,256]{1,0:T(8,128)(2,1)S(1)} %get-tuple-element.29), channel_id=1, source_target_pairs={{0,1},{1,0},{4,12},{5,4},{8,9},{9,13},{12,8},{13,5},{2,3},{3,2},{6... | collective-permute-start | bytes 73736 | tf_op jit(solution)/shard_map/ppermute | solution.py:259
  13.8 1.3 %copy-start.3 = (f32[48,768]{1,0:T(8,128)S(1)}, f32[48,768]{1,0:T(8,128)}, u32[]{:S(2)}) copy-start(f32[48,768]{1,0:T(8,128)} %gain_ref.1) | copy-start | bytes 442372
  17.0 3.9 %collective-permute-start.9 = (bf16[48,256]{1,0:T(8,128)(2,1)S(1)}, bf16[48,256]{1,0:T(8,128)(2,1)S(1)}, u32[]{:S(2)}, u32[]{:S(2)}) collective-permute-start(bf16[48,256]{1,0:T(8,128)(2,1)S(1)} %get-tuple-element.38), channel_id=1, source_target_pairs={{0,2},{2,0},{1,3},{3,1},{4,6},{6,4},{5,7},{7,5},{8,10},{10,8},{9,1... | collective-permute-start | bytes 73736 | tf_op jit(solution)/shard_map/ppermute | solution.py:38

commit v8 on v7

--- a/solution.py
+++ b/solution.py
@@ -100,25 +100,42 @@
 
 def far_kernel(plan, vis_ref, cos_ref, sin_ref, near_ref, *refs):
     out_refs, far_ref = refs[:-1], refs[-1]
-    far_ref[...] = half_of_modes(vis_ref, cos_ref, sin_ref).astype(far_ref.dtype)
     rows, n = out_refs[0].shape[0], near_ref.shape[1]
     me = 2 * lax.axis_index("ma") + lax.axis_index("pol")
+    places = []
     for targets, out_ref in zip(((),) + plan, out_refs):
         to = lookup(me, [target // 2 for target in targets]) if targets else lax.axis_index("ma")
-        at = pl.ds(pl.multiple_of(to * rows, 16), rows)
-        out_ref[:, :n] = near_ref[at, :]
+        places.append(pl.ds(pl.multiple_of(to * rows, 16), rows))
+        out_ref[:, :n] = near_ref[places[-1], :]
+    far_ref[...] = half_of_modes(vis_ref, cos_ref, sin_ref).astype(far_ref.dtype)
+    for at, out_ref in zip(places, out_refs):
         out_ref[:, n:] = far_ref[at, :]
 
 
 def prepare_kernel(nf_blocks, rows_own, rows_other, basis_ref, step_ref, kl_ref, *outs):
-    beam_ref, beam_turned_ref, basis_turned_ref, keep_ref, lanes_ref = outs
+    beam_ref, beam_turned_ref, product_ref, window_ref, keep_ref, lanes_ref = outs
     nfreq, nbase, degrees = rows_own.shape
     n = nfreq * nbase
     beam_ref[:n, :] = rows_own[...].reshape(n, degrees)
     beam_ref[n:, :] = rows_other[...].reshape(n, degrees)
     beam_turned_ref[...] = beam_ref[...].T
-    basis_turned_ref[...] = basis_ref[...].T
     modes = keep_ref.shape[0] // nfreq
+    first = lax.axis_index("ma") * modes
+    above = lax.broadcasted_iota(jnp.int32, basis_ref.shape, 1) >= first + modes
+    shared = jnp.where(above, basis_ref[...], jnp.zeros_like(basis_ref))
+    side = 2 * LANES if degrees % (2 * LANES) == 0 else degrees
+    for left in range(0, degrees, side):
+        columns, below = slice(left, left + side), left + side
+        values = lax.dot_general(shared[:below], basis_ref[columns, :], NT_DIMS, preferred_element_type=jnp.float32)
+        product_ref[:below, columns] = values.astype(jnp.bfloat16)
+        for top in range(0, left, side):
+            product_ref[columns, top : top + side] = values[top : top + side].T.astype(jnp.bfloat16)
+    base = jnp.minimum(first // LANES * LANES, degrees - 2 * LANES)
+    near = basis_ref[:, pl.ds(pl.multiple_of(base, LANES), 2 * LANES)].astype(jnp.float32)
+    near = pltpu.roll(near, (2 * LANES - (first - base)) % (2 * LANES), axis=1)[:, :LANES]
+    near = jnp.where(lax.broadcasted_iota(jnp.int32, near.shape, 1) < modes, near, 0.0)
+    window_ref[...] = near.astype(jnp.bfloat16)
+    product_ref[degrees:, :] = near.T.astype(jnp.bfloat16)
     of_column = (lax.broadcasted_iota(jnp.int32, (modes, 2 * n), 1) % n) // nbase
     for f in range(nfreq):
         keep_ref[f * modes : (f + 1) * modes, :] = jnp.where(of_column == f, 1.0, 0.0)
@@ -147,9 +164,9 @@
 def solve_kernel(plan, *refs):
     blocks = len(plan) + 1
     parts = refs[:blocks]
-    beam, beam_turned, basis_ref, basis_turned, keep, lanes, gain_ref = refs[blocks : blocks + 7]
+    beam, beam_turned, product, window, keep, lanes, gain_ref = refs[blocks : blocks + 7]
     results = refs[blocks + 7 :]
-    modes, degrees = gain_ref.shape
+    modes = gain_ref.shape[0]
     nfreq = keep.shape[0] // modes
     total = parts[0][...].astype(jnp.float32)
     me = 2 * lax.axis_index("ma") + lax.axis_index("pol")
@@ -157,30 +174,27 @@
         real = [int(targets.index(i) // 2 != i // 2) for i in range(len(targets))]
         values = part[...].astype(jnp.float32)
         total = total + (values if all(real) else jnp.where(lookup(me, real) == 1, values, 0.0))
-    ids = lax.axis_index("ma") * modes + lax.broadcasted_iota(jnp.int32, (modes, degrees), 0)
-    mask = lax.broadcasted_iota(jnp.int32, (modes, degrees), 1) >= ids
+    row = lax.broadcasted_iota(jnp.int32, (modes, LANES), 0)
+    inside = lax.broadcasted_iota(jnp.int32, (modes, LANES), 1) >= row
 
     def groups(values):
         return [values[at : at + modes] for at in range(0, values.shape[0], modes)]
 
     def scaled(values):
         return jnp.concatenate([(v * gain_ref[...]).astype(jnp.bfloat16) for v in groups(values)], axis=0)
-
-    def back(signal):
-        h = scaled(jnp.dot(signal, beam[...], preferred_element_type=jnp.float32))
-        return [jnp.where(mask, v, 0.0) for v in groups(jnp.dot(h, basis_ref[...], preferred_element_type=jnp.float32))]
 
     step = lanes[0:1, :]
     y = step * total
     for _ in range(ITERS):
         spread = (jnp.concatenate([y] * nfreq, axis=0) * keep[...]).astype(jnp.bfloat16)
-        coeffs = jnp.concatenate([v.astype(jnp.bfloat16) for v in back(spread)], axis=0)
-        e = jnp.dot(coeffs, basis_turned[...], preferred_element_type=jnp.float32)
+        h = scaled(jnp.dot(spread, beam[...], preferred_element_type=jnp.float32))
+        edge = jnp.dot(h, window[...], preferred_element_type=jnp.float32)
+        edge = jnp.concatenate([jnp.where(inside, v, 0.0).astype(jnp.bfloat16) for v in groups(edge)], axis=0)
+        e = jnp.dot(jnp.concatenate([h, edge], axis=1), product[...], preferred_element_type=jnp.float32)
         again = jnp.dot(scaled(e), beam_turned[...], preferred_element_type=jnp.float32) * keep[...]
         y = y + step * (total - sum(groups(again)))
-    y_ref, mixed_ref = results
+    (y_ref,) = results
     y_ref[...] = y.astype(y_ref.dtype)
-    mixed_ref[...] = mixed(y, lanes, 0, mixed_ref.shape[0] // modes)
 
 
 def mixed(y, lanes, source, kept):
@@ -188,9 +202,10 @@
     return jnp.concatenate([(y * lanes[row : row + 1, :]).astype(jnp.bfloat16) for row in range(first, first + kept)], axis=0)
 
 
-def near_terms_kernel(mixed_ref, beam_ref, *refs):
+def near_terms_kernel(y_ref, lanes_ref, beam_ref, *refs):
     *rows, sum_ref, beams_ref = refs
-    sum_ref[...] = jnp.dot(mixed_ref[...], beam_ref[...], preferred_element_type=jnp.float32)
+    own = mixed(y_ref[...].astype(jnp.float32), lanes_ref, 0, sum_ref.shape[0] // y_ref.shape[0])
+    sum_ref[...] = jnp.dot(own, beam_ref[...], preferred_element_type=jnp.float32)
     count, width, degrees = beams_ref.shape
     for k in range(count):
         for half, ref in enumerate((rows[k], rows[count + k])):
@@ -218,6 +233,7 @@
     nfreq, _, nbase, ntime = visibility.shape
     local_modes, degrees = mode_gain.shape
     modes = local_modes * blocks
+    assert modes <= degrees and local_modes <= LANES
     n = nfreq * nbase
     shape = jax.ShapeDtypeStruct
     steps = range(1, nf_blocks)
@@ -262,29 +278,30 @@
         out_shape=[
             shape((2 * n, degrees), jnp.bfloat16),
             shape((degrees, 2 * n), jnp.bfloat16),
-            shape((degrees, degrees), jnp.bfloat16),
+            shape((degrees + LANES, degrees), jnp.bfloat16),
+            shape((degrees, LANES), jnp.bfloat16),
             shape((nfreq * local_modes, 2 * n), jnp.float32),
             shape((1 + kl_matrix.shape[0], 2 * n), jnp.float32),
         ],
         in_specs=[VMEM] * 5,
-        out_specs=[VMEM] * 5,
-        compiler_params=pltpu.CompilerParams(vmem_limit_bytes=16 << 20),
-        cost_estimate=work(0.7),
+        out_specs=[VMEM] * 6,
+        compiler_params=pltpu.CompilerParams(vmem_limit_bytes=20 << 20),
+        cost_estimate=work(1.5),
         name="prepare",
     )(beam_rows, other_rows, harmonic_basis, step_size[None, :], kl_matrix)
-    beam, beam_turned, basis_turned, keep, lanes = tables
+    beam, beam_turned, product, window, keep, lanes = tables
     for k in steps:
         peer_rows.append(exchange(peer_rows[k - 1], "pol", 2, 1))
     kept = kl_matrix.shape[0] // nf_blocks
-    y, near_mixed = pl.pallas_call(
+    y = pl.pallas_call(
         functools.partial(solve_kernel, plan),
-        out_shape=[shape((local_modes, 2 * n), jnp.bfloat16), shape((kept * local_modes, 2 * n), jnp.bfloat16)],
+        out_shape=[shape((local_modes, 2 * n), jnp.bfloat16)],
         in_specs=[VMEM] * (len(plan) + 8),
-        out_specs=[VMEM] * 2,
+        out_specs=[VMEM],
         compiler_params=pltpu.CompilerParams(vmem_limit_bytes=24 << 20),
         cost_estimate=work(2.0),
         name="solve",
-    )(*parts, beam, beam_turned, harmonic_basis, basis_turned, keep, lanes, mode_gain)
+    )(*parts, beam, beam_turned, product, window, keep, lanes, mode_gain)[0]
     others = []
     for k in steps:
         others.append(exchange(y, "freq", nf_blocks, k))
@@ -294,12 +311,12 @@
             shape((kept * local_modes, degrees), jnp.float32),
             shape((nf_blocks - 1, 2 * n, degrees), jnp.bfloat16),
         ],
-        in_specs=[VMEM] * (2 + len(peer_rows)),
+        in_specs=[VMEM] * (3 + len(peer_rows)),
         out_specs=[VMEM] * 2,
         compiler_params=pltpu.CompilerParams(vmem_limit_bytes=16 << 20),
         cost_estimate=work(0.5),
         name="near_terms",
-    )(near_mixed, beam, *peer_rows)
+    )(y, lanes, beam, *peer_rows)
     terms = pl.pallas_call(
         terms_kernel,
         out_shape=shape((kept, local_modes, degrees), jnp.bfloat16),

time: 22.2 us -> 22 us (level)
  waiting for transfers between devices: 6.23 us -> 5.86 us
    ppermute x5, waiting for transfers between devices: 0.72 us -> 0.35 us  [on_device(): lax.ppermute(mine[k + 1], ('ma', 'pol'), list(enumerate(targets)))]
    pallas_call x1, Pallas kernels: 0.54 us -> 0.91 us  [on_device(): pl.pallas_call(functools.partial(prepare_kernel, nf_blocks), out_shape=[s...]
  transfers between devices with their start and end apart: 10 -> 10, of which waited for: 5 -> 4; matrix products, arithmetic and copies ran while one was open for 0% -> 0% of each run, Pallas kernels for 20% -> 21%
where the time goes in v8:
time: 22 us; the launch traced here: 21.8 us
  starting transfers between devices  10 us (45%)
  waiting for transfers between devices  5.86 us (27%)
  Pallas kernels  5.8 us (26%)
    ppermute x5, waiting for transfers between devices, exchange(): return lax.ppermute(array, axis, pairs)  5.51 us
    ppermute x5, starting transfers between devices, exchange(): return lax.ppermute(array, axis, pairs)  5.03 us
    ppermute x5, starting transfers between devices, on_device(): lax.ppermute(mine[k + 1], ('ma', 'pol'), list(enumerate(targets)))  4.99 us
    pallas_call x1, Pallas kernels, on_device(): pl.pallas_call(functools.partial(solve_kernel, plan), out_shape=[shape((l...  1.76 us
    pallas_call x1, Pallas kernels, on_device(): pl.pallas_call(terms_kernel, out_shape=shape((kept, local_modes, degrees)...  1.12 us
    pallas_call x1, Pallas kernels, on_device(): pl.pallas_call(functools.partial(prepare_kernel, nf_blocks), out_shape=[s...  0.91 us
    pallas_call x1, Pallas kernels, on_device(): pl.pallas_call(functools.partial(table_kernel, ntime), out_shape=[shape((...  0.64 us
    pallas_call x1, Pallas kernels, on_device(): pl.pallas_call(functools.partial(far_kernel, plan), out_shape=[shape((loc...  0.59 us
  transfers between devices with their start and end apart: 10, of which 4 were waited for; matrix products, arithmetic and copies ran while one was open for 0% of the time, Pallas kernels for 21%

profile of v8, /device:TPU:0, one launch (start us, length us, event | category | flops | bytes accessed | tf_op | source)
XLA Modules:
  0.0 21.8 jit_solution(6417771696020963284)
XLA Ops:
  0.0 0.5 %collective-permute-start = (bf16[4,2,32,2048]{3,2,1,0:T(8,128)(2,1)}, bf16[4,2,32,2048]{3,2,1,0:T(8,128)(2,1)S(1)}, u32[]{:S(2)}, u32[]{:S(2)}) collective-permute-start(bf16[4,2,32,2048]{3,2,1,0:T(8,128)(2,1)} %vis_ref.1), channel_id=1, source_target_pairs={{0,1},{1,0},{2,3},{3,2},{4,5},{5,4},{6,7},{7,6},{8,9},{9,8},{10,11... | collective-permute-start | bytes 3145736 | tf_op jit(solution)/shard_map/ppermute | solution.py:38
  0.5 0.1 collective-permute-start.6
  0.6 2.9 %collective-permute-start.7 = (bf16[4,32,768]{2,1,0:T(8,128)(2,1)}, bf16[4,32,768]{2,1,0:T(8,128)(2,1)S(1)}, u32[]{:S(2)}, u32[]{:S(2)}) collective-permute-start(bf16[4,32,768]{2,1,0:T(8,128)(2,1)} %rows_own.1), channel_id=1, source_target_pairs={{0,2},{2,0},{1,3},{3,1},{4,6},{6,4},{5,7},{7,5},{8,10},{10,8},{9,1... | collective-permute-start | bytes 589832 | tf_op jit(solution)/shard_map/ppermute | solution.py:38
  3.5 0.6 %tables.1 = (bf16[192,2048]{1,0:T(8,128)(2,1)S(1)}, bf16[192,2048]{1,0:T(8,128)(2,1)S(1)}) custom-call(), custom_call_target="tpu_custom_call" | custom-call | flops 1000000000 | bytes 262144 | tf_op jit(solution)/shard_map/tables/pallas_call | solution.py:245
  4.1 0.6 %near.1.near_ref = bf16[192,128]{1,0:T(8,128)(2,1)S(1)} custom-call(bf16[4,2,32,2048]{3,2,1,0:T(8,128)(2,1)S(1)} %copy-done, bf16[192,2048]{1,0:T(8,128)(2,1)S(1)} %get-tuple-element.21.cos_ref, bf16[192,2048]{1,0:T(8,128)(2,1)S(1)} %get-tuple-element.22.sin_ref), custom_call_target="tpu_custom_call" | custom-call | flops 500000000 | bytes 262144 | tf_op jit(solution)/shard_map/near/pallas_call | solution.py:253
  4.7 0.0 copy-start.1
  4.7 0.0 copy-start.2
  4.7 0.0 copy-start.4
  4.8 0.0 copy-start.5
  4.8 0.0 collective-permute-done.vis_ref
  4.8 0.6 %far.1 = (bf16[48,256]{1,0:T(8,128)(2,1)S(1)}, bf16[48,256]{1,0:T(8,128)(2,1)S(1)}, bf16[48,256]{1,0:T(8,128)(2,1)S(1)}, bf16[48,256]{1,0:T(8,128)(2,1)S(1)}, bf...) custom-call(bf16[4,2,32,2048]{3,2,1,0:T(8,128)(2,1)S(1)} %collective-permute-done.vis_ref, ...), custom_call_target="tpu_custom_call" | custom-call | flops 500000000 | bytes 262144 | tf_op jit(solution)/shard_map/far/pallas_call | solution.py:263
  5.4 0.1 collective-permute-start.1
  5.4 3.4 %collective-permute-done.7.refs_0_ = bf16[4,32,768]{2,1,0:T(8,128)(2,1)S(1)} collective-permute-done((bf16[4,32,768]{2,1,0:T(8,128)(2,1)}, bf16[4,32,768]{2,1,0:T(8,128)(2,1)S(1)}, u32[]{:S(2)}, u32[]{:S(2)}) %collective-permute-start.7) | collective-permute-done | bytes 196640 | tf_op jit(solution)/shard_map/ppermute | solution.py:38
  8.8 0.0 collective-permute-start.8
  8.8 1.8 %collective-permute-start.2 = (bf16[48,256]{1,0:T(8,128)(2,1)S(1)}, bf16[48,256]{1,0:T(8,128)(2,1)S(1)}, u32[]{:S(2)}, u32[]{:S(2)}) collective-permute-start(bf16[48,256]{1,0:T(8,128)(2,1)S(1)} %get-tuple-element.25), channel_id=1, source_target_pairs={{0,4},{1,13},{4,5},{5,9},{8,12},{9,8},{12,0},{13,1},{2,6},{3,15},{... | collective-permute-start | bytes 73736 | tf_op jit(solution)/shard_map/ppermute | solution.py:275
  10.7 2.6 %collective-permute-start.3 = (bf16[48,256]{1,0:T(8,128)(2,1)S(1)}, bf16[48,256]{1,0:T(8,128)(2,1)S(1)}, u32[]{:S(2)}, u32[]{:S(2)}) collective-permute-start(bf16[48,256]{1,0:T(8,128)(2,1)S(1)} %get-tuple-element.26), channel_id=1, source_target_pairs={{0,8},{1,5},{4,0},{5,13},{8,9},{9,1},{12,4},{13,12},{2,10},{3,7},{... | collective-permute-start | bytes 73736 | tf_op jit(solution)/shard_map/ppermute | solution.py:275
  13.2 0.0 collective-permute-done.6.rows_other
  13.2 0.3 %collective-permute-start.4 = (bf16[48,256]{1,0:T(8,128)(2,1)S(1)}, bf16[48,256]{1,0:T(8,128)(2,1)S(1)}, u32[]{:S(2)}, u32[]{:S(2)}) collective-permute-start(bf16[48,256]{1,0:T(8,128)(2,1)S(1)} %get-tuple-element.27), channel_id=1, source_target_pairs={{0,12},{1,0},{4,8},{5,1},{8,4},{9,5},{12,13},{13,9},{2,14},{3,2},{... | collective-permute-start | bytes 73736 | tf_op jit(solution)/shard_map/ppermute | solution.py:275
  13.5 0.0 collective-permute-done.1.refs_1_
  13.5 0.2 %collective-permute-start.5 = (bf16[48,256]{1,0:T(8,128)(2,1)S(1)}, bf16[48,256]{1,0:T(8,128)(2,1)S(1)}, u32[]{:S(2)}, u32[]{:S(2)}) collective-permute-start(bf16[48,256]{1,0:T(8,128)(2,1)S(1)} %get-tuple-element.28), channel_id=1, source_target_pairs={{0,1},{1,0},{4,12},{5,4},{8,9},{9,13},{12,8},{13,5},{2,3},{3,2},{6... | collective-permute-start | bytes 73736 | tf_op jit(solution)/shard_map/ppermute | solution.py:275
  13.8 0.0 copy-start.3
  13.8 0.9 %prepare.1 = (bf16[256,768]{1,0:T(8,128)(2,1)S(1)}, bf16[768,256]{1,0:T(8,128)(2,1)S(1)}, bf16[896,768]{1,0:T(8,128)(2,1)S(1)}, bf16[768,128]{1,0:T(8,128)(2,1)S...) custom-call(bf16[4,32,768]{2,1,0:T(8,128)(2,1)S(1)} %copy-done.2, ...), custom_call_target="tpu_custom_call" | custom-call | flops 1500000000 | bytes 262144 | tf_op jit(solution)/shard_map/prepare/pallas_call | solution.py:276
  14.7 0.0 collective-permute-done.2.refs_2_
  14.7 0.1 collective-permute-done.3.refs_3_
  14.8 0.2 %collective-permute-done.4.refs_4_ = bf16[48,256]{1,0:T(8,128)(2,1)S(1)} collective-permute-done((bf16[48,256]{1,0:T(8,128)(2,1)S(1)}, bf16[48,256]{1,0:T(8,128)(2,1)S(1)}, u32[]{:S(2)}, u32[]{:S(2)}) %collective-permute-start.4) | collective-permute-done | bytes 24608 | tf_op jit(solution)/shard_map/ppermute | solution.py:275
  15.0 0.0 collective-permute-done.5.refs_5_
  15.1 1.8 %solve.1.y_ref = bf16[48,256]{1,0:T(8,128)(2,1)S(1)} custom-call(bf16[48,256]{1,0:T(8,128)(2,1)S(1)} %get-tuple-element.23.refs_0_, bf16[48,256]{1,0:T(8,128)(2,1)S(1)} %collective-permute-done.1.refs_1_, bf16[48,256]{1,0:T(8,128)(2,1)S(1)} %collective-permute-done.2.refs_2_, bf16[48,256]{1,0:T(8,128)(2,1)S(1)} %collective-permute-done.3.refs_3_, ...), custom_call_target="tpu_custom_call" | custom-call | flops 2000000000 | bytes 262144 | tf_op jit(solution)/shard_map/solve/pallas_call | solution.py:296
  16.8 1.6 %collective-permute-start.9 = (bf16[48,256]{1,0:T(8,128)(2,1)S(1)}, bf16[48,256]{1,0:T(8,128)(2,1)S(1)}, u32[]{:S(2)}, u32[]{:S(2)}) collective-permute-start(bf16[48,256]{1,0:T(8,128)(2,1)S(1)} %solve.1.y_ref), channel_id=1, source_target_pairs={{0,2},{2,0},{1,3},{3,1},{4,6},{6,4},{5,7},{7,5},{8,10},{10,8},{9,1... | collective-permute-start | bytes 73736 | tf_op jit(solution)/shard_map/ppermute | solution.py:38
  18.4 0.0 collective-permute-done.8.refs_1_
  18.4 0.2 near_terms.1
  18.6 2.1 %collective-permute-done.9.refs_0_ = bf16[48,256]{1,0:T(8,128)(2,1)S(1)} collective-permute-done((bf16[48,256]{1,0:T(8,128)(2,1)S(1)}, bf16[48,256]{1,0:T(8,128)(2,1)S(1)}, u32[]{:S(2)}, u32[]{:S(2)}) %collective-permute-start.9) | collective-permute-done | bytes 24608 | tf_op jit(solution)/shard_map/ppermute | solution.py:38
  20.7 1.1 %terms.1 = bf16[1,48,768]{2,1,0:T(8,128)(2,1)} custom-call(f32[48,768]{1,0:T(8,128)S(1)} %get-tuple-element.35.sum_ref, bf16[1,256,768]{2,1,0:T(8,128)(2,1)S(1)} %get-tuple-element.36.beams_ref, f32[3,256]{1,0:T(4,128)S(1)} %get-tuple-element.34.refs_11_.lanes_ref, f32[48,768]{1,0:T(8,128)S(1)} %copy-done.3, bf16[768,768]{1,0:T(8,128)(2,1)S(1)} %copy-done.1, ...), custom_call_target="tpu_custom_call" | custom-call | flops 1000000000 | bytes 262144 | tf_op jit(solution)/shard_map/terms/pallas_call | solution.py:320
  (7 shorter events, 0.0 us)
Async XLA Ops:
  0.0 4.1 %copy-start = (bf16[4,2,32,2048]{3,2,1,0:T(8,128)(2,1)S(1)}, bf16[4,2,32,2048]{3,2,1,0:T(8,128)(2,1)}, u32[]{:S(2)}) copy-start(bf16[4,2,32,2048]{3,2,1,0:T(8,128)(2,1)} %vis_ref.1) | copy-start | bytes 3145732
  0.0 4.8 %collective-permute-start = (bf16[4,2,32,2048]{3,2,1,0:T(8,128)(2,1)}, bf16[4,2,32,2048]{3,2,1,0:T(8,128)(2,1)S(1)}, u32[]{:S(2)}, u32[]{:S(2)}) collective-permute-start(bf16[4,2,32,2048]{3,2,1,0:T(8,128)(2,1)} %vis_ref.1), channel_id=1, source_target_pairs={{0,1},{1,0},{2,3},{3,2},{4,5},{5,4},{6,7},{7,6},{8,9},{9,8},{10,11... | collective-permute-start | bytes 3145736 | tf_op jit(solution)/shard_map/ppermute | solution.py:38
  0.5 12.7 %collective-permute-start.6 = (bf16[4,32,768]{2,1,0:T(8,128)(2,1)}, bf16[4,32,768]{2,1,0:T(8,128)(2,1)S(1)}, u32[]{:S(2)}, u32[]{:S(2)}) collective-permute-start(bf16[4,32,768]{2,1,0:T(8,128)(2,1)} %rows_own.1), channel_id=1, source_target_pairs={{0,1},{1,0},{2,3},{3,2},{4,5},{5,4},{6,7},{7,6},{8,9},{9,8},{10,11... | collective-permute-start | bytes 589832 | tf_op jit(solution)/shard_map/ppermute | solution.py:38
  0.6 8.3 %collective-permute-start.7 = (bf16[4,32,768]{2,1,0:T(8,128)(2,1)}, bf16[4,32,768]{2,1,0:T(8,128)(2,1)S(1)}, u32[]{:S(2)}, u32[]{:S(2)}) collective-permute-start(bf16[4,32,768]{2,1,0:T(8,128)(2,1)} %rows_own.1), channel_id=1, source_target_pairs={{0,2},{2,0},{1,3},{3,1},{4,6},{6,4},{5,7},{7,5},{8,10},{10,8},{9,1... | collective-permute-start | bytes 589832 | tf_op jit(solution)/shard_map/ppermute | solution.py:38
  4.7 9.0 %copy-start.1 = (bf16[768,768]{1,0:T(8,128)(2,1)S(1)}, bf16[768,768]{1,0:T(8,128)(2,1)}, u32[]{:S(2)}) copy-start(bf16[768,768]{1,0:T(8,128)(2,1)} %basis_ref.3) | copy-start | bytes 3538948
  4.7 9.0 %copy-start.2 = (bf16[4,32,768]{2,1,0:T(8,128)(2,1)S(1)}, bf16[4,32,768]{2,1,0:T(8,128)(2,1)}, u32[]{:S(2)}) copy-start(bf16[4,32,768]{2,1,0:T(8,128)(2,1)} %rows_own.1) | copy-start | bytes 589828
  4.7 9.0 %copy-start.4 = (f32[4]{0:T(128)S(1)}, f32[4]{0:T(128)}, u32[]{:S(2)}) copy-start(f32[4]{0:T(128)} %param.10) | copy-start | bytes 52
  4.8 9.0 %copy-start.5 = (bf16[2,8]{1,0:T(2,128)(2,1)S(1)}, bf16[2,8]{1,0:T(2,128)(2,1)}, u32[]{:S(2)}) copy-start(bf16[2,8]{1,0:T(2,128)(2,1)} %kl_ref.1) | copy-start | bytes 100
  5.4 8.1 %collective-permute-start.1 = (bf16[48,256]{1,0:T(8,128)(2,1)S(1)}, bf16[48,256]{1,0:T(8,128)(2,1)S(1)}, u32[]{:S(2)}, u32[]{:S(2)}) collective-permute-start(bf16[48,256]{1,0:T(8,128)(2,1)S(1)} %get-tuple-element.24), channel_id=1, source_target_pairs={{0,1},{1,9},{4,5},{5,4},{8,0},{9,8},{12,13},{13,12},{2,3},{3,11},{... | collective-permute-start | bytes 73736 | tf_op jit(solution)/shard_map/ppermute | solution.py:275
  8.8 9.6 %collective-permute-start.8 = (bf16[4,32,768]{2,1,0:T(8,128)(2,1)S(1)}, bf16[4,32,768]{2,1,0:T(8,128)(2,1)S(1)}, u32[]{:S(2)}, u32[]{:S(2)}) collective-permute-start(bf16[4,32,768]{2,1,0:T(8,128)(2,1)S(1)} %collective-permute-done.7.refs_0_), channel_id=1, source_target_pairs={{0,1},{1,0},{2,3},{3,2},{4,5},{5,4},{6,7},{7,6},{8,9},{9,8},{10,11... | collective-permute-start | bytes 589832 | tf_op jit(solution)/shard_map/ppermute | solution.py:38
  8.8 5.9 %collective-permute-start.2 = (bf16[48,256]{1,0:T(8,128)(2,1)S(1)}, bf16[48,256]{1,0:T(8,128)(2,1)S(1)}, u32[]{:S(2)}, u32[]{:S(2)}) collective-permute-start(bf16[48,256]{1,0:T(8,128)(2,1)S(1)} %get-tuple-element.25), channel_id=1, source_target_pairs={{0,4},{1,13},{4,5},{5,9},{8,12},{9,8},{12,0},{13,1},{2,6},{3,15},{... | collective-permute-start | bytes 73736 | tf_op jit(solution)/shard_map/ppermute | solution.py:275
  10.7 4.2 %collective-permute-start.3 = (bf16[48,256]{1,0:T(8,128)(2,1)S(1)}, bf16[48,256]{1,0:T(8,128)(2,1)S(1)}, u32[]{:S(2)}, u32[]{:S(2)}) collective-permute-start(bf16[48,256]{1,0:T(8,128)(2,1)S(1)} %get-tuple-element.26), channel_id=1, source_target_pairs={{0,8},{1,5},{4,0},{5,13},{8,9},{9,1},{12,4},{13,12},{2,10},{3,7},{... | collective-permute-start | bytes 73736 | tf_op jit(solution)/shard_map/ppermute | solution.py:275
  13.2 1.8 %collective-permute-start.4 = (bf16[48,256]{1,0:T(8,128)(2,1)S(1)}, bf16[48,256]{1,0:T(8,128)(2,1)S(1)}, u32[]{:S(2)}, u32[]{:S(2)}) collective-permute-start(bf16[48,256]{1,0:T(8,128)(2,1)S(1)} %get-tuple-element.27), channel_id=1, source_target_pairs={{0,12},{1,0},{4,8},{5,1},{8,4},{9,5},{12,13},{13,9},{2,14},{3,2},{... | collective-permute-start | bytes 73736 | tf_op jit(solution)/shard_map/ppermute | solution.py:275
  13.5 1.5 %collective-permute-start.5 = (bf16[48,256]{1,0:T(8,128)(2,1)S(1)}, bf16[48,256]{1,0:T(8,128)(2,1)S(1)}, u32[]{:S(2)}, u32[]{:S(2)}) collective-permute-start(bf16[48,256]{1,0:T(8,128)(2,1)S(1)} %get-tuple-element.28), channel_id=1, source_target_pairs={{0,1},{1,0},{4,12},{5,4},{8,9},{9,13},{12,8},{13,5},{2,3},{3,2},{6... | collective-permute-start | bytes 73736 | tf_op jit(solution)/shard_map/ppermute | solution.py:275
  13.8 1.3 %copy-start.3 = (f32[48,768]{1,0:T(8,128)S(1)}, f32[48,768]{1,0:T(8,128)}, u32[]{:S(2)}) copy-start(f32[48,768]{1,0:T(8,128)} %gain_ref.1) | copy-start | bytes 442372
  16.8 3.9 %collective-permute-start.9 = (bf16[48,256]{1,0:T(8,128)(2,1)S(1)}, bf16[48,256]{1,0:T(8,128)(2,1)S(1)}, u32[]{:S(2)}, u32[]{:S(2)}) collective-permute-start(bf16[48,256]{1,0:T(8,128)(2,1)S(1)} %solve.1.y_ref), channel_id=1, source_target_pairs={{0,2},{2,0},{1,3},{3,1},{4,6},{6,4},{5,7},{7,5},{8,10},{10,8},{9,1... | collective-permute-start | bytes 73736 | tf_op jit(solution)/shard_map/ppermute | solution.py:38

commit v9 on v8

--- a/solution.py
+++ b/solution.py
@@ -15,9 +15,9 @@
 LINE_OF_FOUR = (
     (1, 5, 3, 2, 0, 4, 7, 6),
     (2, 7, 3, 5, 6, 4, 0, 1),
-    (4, 3, 0, 7, 5, 1, 2, 6),
-    (6, 0, 4, 1, 2, 3, 7, 5),
-    (1, 0, 6, 2, 5, 7, 4, 3),
+    (6, 3, 0, 1, 2, 7, 4, 5),
+    (4, 0, 6, 7, 5, 1, 2, 3),
+    (1, 0, 4, 2, 5, 3, 7, 6),
 )
 NT_DIMS = (((1,), (1,)), ((), ()))
 VMEM = pl.BlockSpec(memory_space=pltpu.VMEM)

time: 22 us -> 21.8 us (level)
  starting transfers between devices: 10 us -> 9.53 us
  waiting for transfers between devices: 5.86 us -> 6.12 us
    ppermute x5, starting transfers between devices: 4.99 us -> 4.48 us  [on_device(): lax.ppermute(mine[k + 1], ('ma', 'pol'), list(enumerate(targets)))]
    ppermute x5, waiting for transfers between devices: 0.35 us -> 0.62 us  [on_device(): lax.ppermute(mine[k + 1], ('ma', 'pol'), list(enumerate(targets)))]
  transfers between devices with their start and end apart: 10 -> 10, of which waited for: 4 -> 4; matrix products, arithmetic and copies ran while one was open for 0% -> 0% of each run, Pallas kernels for 21% -> 22%
where the time goes in v9:
time: 21.8 us; the launch traced here: 21.6 us
  starting transfers between devices  9.53 us (44%)
  waiting for transfers between devices  6.12 us (28%)
  Pallas kernels  5.79 us (27%)
    ppermute x5, waiting for transfers between devices, exchange(): return lax.ppermute(array, axis, pairs)  5.5 us
    ppermute x5, starting transfers between devices, exchange(): return lax.ppermute(array, axis, pairs)  5.04 us
    ppermute x5, starting transfers between devices, on_device(): lax.ppermute(mine[k + 1], ('ma', 'pol'), list(enumerate(targets)))  4.48 us
    pallas_call x1, Pallas kernels, on_device(): pl.pallas_call(functools.partial(solve_kernel, plan), out_shape=[shape((l...  1.75 us
    pallas_call x1, Pallas kernels, on_device(): pl.pallas_call(terms_kernel, out_shape=shape((kept, local_modes, degrees)...  1.12 us
    pallas_call x1, Pallas kernels, on_device(): pl.pallas_call(functools.partial(prepare_kernel, nf_blocks), out_shape=[s...  0.91 us
    pallas_call x1, Pallas kernels, on_device(): pl.pallas_call(functools.partial(table_kernel, ntime), out_shape=[shape((...  0.64 us
    ppermute x5, waiting for transfers between devices, on_device(): lax.ppermute(mine[k + 1], ('ma', 'pol'), list(enumerate(targets)))  0.62 us
  transfers between devices with their start and end apart: 10, of which 4 were waited for; matrix products, arithmetic and copies ran while one was open for 0% of the time, Pallas kernels for 22%

profile of v9, /device:TPU:0, one launch (start us, length us, event | category | flops | bytes accessed | tf_op | source)
XLA Modules:
  0.0 21.6 jit_solution(248666230308465807)
XLA Ops:
  0.0 0.5 %collective-permute-start = (bf16[4,2,32,2048]{3,2,1,0:T(8,128)(2,1)}, bf16[4,2,32,2048]{3,2,1,0:T(8,128)(2,1)S(1)}, u32[]{:S(2)}, u32[]{:S(2)}) collective-permute-start(bf16[4,2,32,2048]{3,2,1,0:T(8,128)(2,1)} %vis_ref.1), channel_id=1, source_target_pairs={{0,1},{1,0},{2,3},{3,2},{4,5},{5,4},{6,7},{7,6},{8,9},{9,8},{10,11... | collective-permute-start | bytes 3145736 | tf_op jit(solution)/shard_map/ppermute | solution.py:38
  0.5 0.1 collective-permute-start.6
  0.6 2.9 %collective-permute-start.7 = (bf16[4,32,768]{2,1,0:T(8,128)(2,1)}, bf16[4,32,768]{2,1,0:T(8,128)(2,1)S(1)}, u32[]{:S(2)}, u32[]{:S(2)}) collective-permute-start(bf16[4,32,768]{2,1,0:T(8,128)(2,1)} %rows_own.1), channel_id=1, source_target_pairs={{0,2},{2,0},{1,3},{3,1},{4,6},{6,4},{5,7},{7,5},{8,10},{10,8},{9,1... | collective-permute-start | bytes 589832 | tf_op jit(solution)/shard_map/ppermute | solution.py:38
  3.5 0.6 %tables.1 = (bf16[192,2048]{1,0:T(8,128)(2,1)S(1)}, bf16[192,2048]{1,0:T(8,128)(2,1)S(1)}) custom-call(), custom_call_target="tpu_custom_call" | custom-call | flops 1000000000 | bytes 262144 | tf_op jit(solution)/shard_map/tables/pallas_call | solution.py:245
  4.1 0.6 %near.1.near_ref = bf16[192,128]{1,0:T(8,128)(2,1)S(1)} custom-call(bf16[4,2,32,2048]{3,2,1,0:T(8,128)(2,1)S(1)} %copy-done, bf16[192,2048]{1,0:T(8,128)(2,1)S(1)} %get-tuple-element.21.cos_ref, bf16[192,2048]{1,0:T(8,128)(2,1)S(1)} %get-tuple-element.22.sin_ref), custom_call_target="tpu_custom_call" | custom-call | flops 500000000 | bytes 262144 | tf_op jit(solution)/shard_map/near/pallas_call | solution.py:253
  4.7 0.0 copy-start.1
  4.7 0.0 copy-start.2
  4.7 0.0 copy-start.4
  4.8 0.0 copy-start.5
  4.8 0.0 collective-permute-done.vis_ref
  4.8 0.6 %far.1 = (bf16[48,256]{1,0:T(8,128)(2,1)S(1)}, bf16[48,256]{1,0:T(8,128)(2,1)S(1)}, bf16[48,256]{1,0:T(8,128)(2,1)S(1)}, bf16[48,256]{1,0:T(8,128)(2,1)S(1)}, bf...) custom-call(bf16[4,2,32,2048]{3,2,1,0:T(8,128)(2,1)S(1)} %collective-permute-done.vis_ref, ...), custom_call_target="tpu_custom_call" | custom-call | flops 500000000 | bytes 262144 | tf_op jit(solution)/shard_map/far/pallas_call | solution.py:263
  5.4 0.1 collective-permute-start.1
  5.5 3.4 %collective-permute-done.7.refs_0_ = bf16[4,32,768]{2,1,0:T(8,128)(2,1)S(1)} collective-permute-done((bf16[4,32,768]{2,1,0:T(8,128)(2,1)}, bf16[4,32,768]{2,1,0:T(8,128)(2,1)S(1)}, u32[]{:S(2)}, u32[]{:S(2)}) %collective-permute-start.7) | collective-permute-done | bytes 196640 | tf_op jit(solution)/shard_map/ppermute | solution.py:38
  8.8 0.0 collective-permute-start.8
  8.8 1.8 %collective-permute-start.2 = (bf16[48,256]{1,0:T(8,128)(2,1)S(1)}, bf16[48,256]{1,0:T(8,128)(2,1)S(1)}, u32[]{:S(2)}, u32[]{:S(2)}) collective-permute-start(bf16[48,256]{1,0:T(8,128)(2,1)S(1)} %get-tuple-element.25), channel_id=1, source_target_pairs={{0,4},{1,13},{4,5},{5,9},{8,12},{9,8},{12,0},{13,1},{2,6},{3,15},{... | collective-permute-start | bytes 73736 | tf_op jit(solution)/shard_map/ppermute | solution.py:275
  10.7 2.0 %collective-permute-start.3 = (bf16[48,256]{1,0:T(8,128)(2,1)S(1)}, bf16[48,256]{1,0:T(8,128)(2,1)S(1)}, u32[]{:S(2)}, u32[]{:S(2)}) collective-permute-start(bf16[48,256]{1,0:T(8,128)(2,1)S(1)} %get-tuple-element.26), channel_id=1, source_target_pairs={{0,12},{1,5},{4,0},{5,1},{8,4},{9,13},{12,8},{13,9},{2,14},{3,7},{... | collective-permute-start | bytes 73736 | tf_op jit(solution)/shard_map/ppermute | solution.py:275
  12.7 0.0 collective-permute-done.6.rows_other
  12.7 0.6 %collective-permute-start.4 = (bf16[48,256]{1,0:T(8,128)(2,1)S(1)}, bf16[48,256]{1,0:T(8,128)(2,1)S(1)}, u32[]{:S(2)}, u32[]{:S(2)}) collective-permute-start(bf16[48,256]{1,0:T(8,128)(2,1)S(1)} %get-tuple-element.27), channel_id=1, source_target_pairs={{0,8},{1,0},{4,12},{5,13},{8,9},{9,1},{12,4},{13,5},{2,10},{3,2},{... | collective-permute-start | bytes 73736 | tf_op jit(solution)/shard_map/ppermute | solution.py:275
  13.2 0.0 collective-permute-done.1.refs_1_
  13.3 0.0 collective-permute-start.5
  13.3 0.0 copy-start.3
  13.3 0.9 %prepare.1 = (bf16[256,768]{1,0:T(8,128)(2,1)S(1)}, bf16[768,256]{1,0:T(8,128)(2,1)S(1)}, bf16[896,768]{1,0:T(8,128)(2,1)S(1)}, bf16[768,128]{1,0:T(8,128)(2,1)S...) custom-call(bf16[4,32,768]{2,1,0:T(8,128)(2,1)S(1)} %copy-done.2, ...), custom_call_target="tpu_custom_call" | custom-call | flops 1500000000 | bytes 262144 | tf_op jit(solution)/shard_map/prepare/pallas_call | solution.py:276
  14.2 0.5 %collective-permute-done.2.refs_2_ = bf16[48,256]{1,0:T(8,128)(2,1)S(1)} collective-permute-done((bf16[48,256]{1,0:T(8,128)(2,1)S(1)}, bf16[48,256]{1,0:T(8,128)(2,1)S(1)}, u32[]{:S(2)}, u32[]{:S(2)}) %collective-permute-start.2) | collective-permute-done | bytes 24608 | tf_op jit(solution)/shard_map/ppermute | solution.py:275
  14.7 0.1 collective-permute-done.3.refs_3_
  14.8 0.0 collective-permute-done.4.refs_4_
  14.8 0.0 collective-permute-done.5.refs_5_
  14.8 1.8 %solve.1.y_ref = bf16[48,256]{1,0:T(8,128)(2,1)S(1)} custom-call(bf16[48,256]{1,0:T(8,128)(2,1)S(1)} %get-tuple-element.23.refs_0_, bf16[48,256]{1,0:T(8,128)(2,1)S(1)} %collective-permute-done.1.refs_1_, bf16[48,256]{1,0:T(8,128)(2,1)S(1)} %collective-permute-done.2.refs_2_, bf16[48,256]{1,0:T(8,128)(2,1)S(1)} %collective-permute-done.3.refs_3_, ...), custom_call_target="tpu_custom_call" | custom-call | flops 2000000000 | bytes 262144 | tf_op jit(solution)/shard_map/solve/pallas_call | solution.py:296
  16.6 1.6 %collective-permute-start.9 = (bf16[48,256]{1,0:T(8,128)(2,1)S(1)}, bf16[48,256]{1,0:T(8,128)(2,1)S(1)}, u32[]{:S(2)}, u32[]{:S(2)}) collective-permute-start(bf16[48,256]{1,0:T(8,128)(2,1)S(1)} %solve.1.y_ref), channel_id=1, source_target_pairs={{0,2},{2,0},{1,3},{3,1},{4,6},{6,4},{5,7},{7,5},{8,10},{10,8},{9,1... | collective-permute-start | bytes 73736 | tf_op jit(solution)/shard_map/ppermute | solution.py:38
  18.2 0.0 collective-permute-done.8.refs_1_
  18.2 0.2 near_terms.1
  18.4 2.1 %collective-permute-done.9.refs_0_ = bf16[48,256]{1,0:T(8,128)(2,1)S(1)} collective-permute-done((bf16[48,256]{1,0:T(8,128)(2,1)S(1)}, bf16[48,256]{1,0:T(8,128)(2,1)S(1)}, u32[]{:S(2)}, u32[]{:S(2)}) %collective-permute-start.9) | collective-permute-done | bytes 24608 | tf_op jit(solution)/shard_map/ppermute | solution.py:38
  20.5 1.1 %terms.1 = bf16[1,48,768]{2,1,0:T(8,128)(2,1)} custom-call(f32[48,768]{1,0:T(8,128)S(1)} %get-tuple-element.35.sum_ref, bf16[1,256,768]{2,1,0:T(8,128)(2,1)S(1)} %get-tuple-element.36.beams_ref, f32[3,256]{1,0:T(4,128)S(1)} %get-tuple-element.34.refs_11_.lanes_ref, f32[48,768]{1,0:T(8,128)S(1)} %copy-done.3, bf16[768,768]{1,0:T(8,128)(2,1)S(1)} %copy-done.1, ...), custom_call_target="tpu_custom_call" | custom-call | flops 1000000000 | bytes 262144 | tf_op jit(solution)/shard_map/terms/pallas_call | solution.py:320
  (7 shorter events, 0.0 us)
Async XLA Ops:
  0.0 4.1 %copy-start = (bf16[4,2,32,2048]{3,2,1,0:T(8,128)(2,1)S(1)}, bf16[4,2,32,2048]{3,2,1,0:T(8,128)(2,1)}, u32[]{:S(2)}) copy-start(bf16[4,2,32,2048]{3,2,1,0:T(8,128)(2,1)} %vis_ref.1) | copy-start | bytes 3145732
  0.0 4.8 %collective-permute-start = (bf16[4,2,32,2048]{3,2,1,0:T(8,128)(2,1)}, bf16[4,2,32,2048]{3,2,1,0:T(8,128)(2,1)S(1)}, u32[]{:S(2)}, u32[]{:S(2)}) collective-permute-start(bf16[4,2,32,2048]{3,2,1,0:T(8,128)(2,1)} %vis_ref.1), channel_id=1, source_target_pairs={{0,1},{1,0},{2,3},{3,2},{4,5},{5,4},{6,7},{7,6},{8,9},{9,8},{10,11... | collective-permute-start | bytes 3145736 | tf_op jit(solution)/shard_map/ppermute | solution.py:38
  0.5 12.2 %collective-permute-start.6 = (bf16[4,32,768]{2,1,0:T(8,128)(2,1)}, bf16[4,32,768]{2,1,0:T(8,128)(2,1)S(1)}, u32[]{:S(2)}, u32[]{:S(2)}) collective-permute-start(bf16[4,32,768]{2,1,0:T(8,128)(2,1)} %rows_own.1), channel_id=1, source_target_pairs={{0,1},{1,0},{2,3},{3,2},{4,5},{5,4},{6,7},{7,6},{8,9},{9,8},{10,11... | collective-permute-start | bytes 589832 | tf_op jit(solution)/shard_map/ppermute | solution.py:38
  0.6 8.3 %collective-permute-start.7 = (bf16[4,32,768]{2,1,0:T(8,128)(2,1)}, bf16[4,32,768]{2,1,0:T(8,128)(2,1)S(1)}, u32[]{:S(2)}, u32[]{:S(2)}) collective-permute-start(bf16[4,32,768]{2,1,0:T(8,128)(2,1)} %rows_own.1), channel_id=1, source_target_pairs={{0,2},{2,0},{1,3},{3,1},{4,6},{6,4},{5,7},{7,5},{8,10},{10,8},{9,1... | collective-permute-start | bytes 589832 | tf_op jit(solution)/shard_map/ppermute | solution.py:38
  4.7 8.5 %copy-start.1 = (bf16[768,768]{1,0:T(8,128)(2,1)S(1)}, bf16[768,768]{1,0:T(8,128)(2,1)}, u32[]{:S(2)}) copy-start(bf16[768,768]{1,0:T(8,128)(2,1)} %basis_ref.3) | copy-start | bytes 3538948
  4.7 8.5 %copy-start.2 = (bf16[4,32,768]{2,1,0:T(8,128)(2,1)S(1)}, bf16[4,32,768]{2,1,0:T(8,128)(2,1)}, u32[]{:S(2)}) copy-start(bf16[4,32,768]{2,1,0:T(8,128)(2,1)} %rows_own.1) | copy-start | bytes 589828
  4.7 8.5 %copy-start.4 = (f32[4]{0:T(128)S(1)}, f32[4]{0:T(128)}, u32[]{:S(2)}) copy-start(f32[4]{0:T(128)} %param.10) | copy-start | bytes 52
  4.8 8.5 %copy-start.5 = (bf16[2,8]{1,0:T(2,128)(2,1)S(1)}, bf16[2,8]{1,0:T(2,128)(2,1)}, u32[]{:S(2)}) copy-start(bf16[2,8]{1,0:T(2,128)(2,1)} %kl_ref.1) | copy-start | bytes 100
  5.4 7.9 %collective-permute-start.1 = (bf16[48,256]{1,0:T(8,128)(2,1)S(1)}, bf16[48,256]{1,0:T(8,128)(2,1)S(1)}, u32[]{:S(2)}, u32[]{:S(2)}) collective-permute-start(bf16[48,256]{1,0:T(8,128)(2,1)S(1)} %get-tuple-element.24), channel_id=1, source_target_pairs={{0,1},{1,9},{4,5},{5,4},{8,0},{9,8},{12,13},{13,12},{2,3},{3,11},{... | collective-permute-start | bytes 73736 | tf_op jit(solution)/shard_map/ppermute | solution.py:275
  8.8 9.3 %collective-permute-start.8 = (bf16[4,32,768]{2,1,0:T(8,128)(2,1)S(1)}, bf16[4,32,768]{2,1,0:T(8,128)(2,1)S(1)}, u32[]{:S(2)}, u32[]{:S(2)}) collective-permute-start(bf16[4,32,768]{2,1,0:T(8,128)(2,1)S(1)} %collective-permute-done.7.refs_0_), channel_id=1, source_target_pairs={{0,1},{1,0},{2,3},{3,2},{4,5},{5,4},{6,7},{7,6},{8,9},{9,8},{10,11... | collective-permute-start | bytes 589832 | tf_op jit(solution)/shard_map/ppermute | solution.py:38
  8.8 5.9 %collective-permute-start.2 = (bf16[48,256]{1,0:T(8,128)(2,1)S(1)}, bf16[48,256]{1,0:T(8,128)(2,1)S(1)}, u32[]{:S(2)}, u32[]{:S(2)}) collective-permute-start(bf16[48,256]{1,0:T(8,128)(2,1)S(1)} %get-tuple-element.25), channel_id=1, source_target_pairs={{0,4},{1,13},{4,5},{5,9},{8,12},{9,8},{12,0},{13,1},{2,6},{3,15},{... | collective-permute-start | bytes 73736 | tf_op jit(solution)/shard_map/ppermute | solution.py:275
  10.7 4.2 %collective-permute-start.3 = (bf16[48,256]{1,0:T(8,128)(2,1)S(1)}, bf16[48,256]{1,0:T(8,128)(2,1)S(1)}, u32[]{:S(2)}, u32[]{:S(2)}) collective-permute-start(bf16[48,256]{1,0:T(8,128)(2,1)S(1)} %get-tuple-element.26), channel_id=1, source_target_pairs={{0,12},{1,5},{4,0},{5,1},{8,4},{9,13},{12,8},{13,9},{2,14},{3,7},{... | collective-permute-start | bytes 73736 | tf_op jit(solution)/shard_map/ppermute | solution.py:275
  12.7 2.1 %collective-permute-start.4 = (bf16[48,256]{1,0:T(8,128)(2,1)S(1)}, bf16[48,256]{1,0:T(8,128)(2,1)S(1)}, u32[]{:S(2)}, u32[]{:S(2)}) collective-permute-start(bf16[48,256]{1,0:T(8,128)(2,1)S(1)} %get-tuple-element.27), channel_id=1, source_target_pairs={{0,8},{1,0},{4,12},{5,13},{8,9},{9,1},{12,4},{13,5},{2,10},{3,2},{... | collective-permute-start | bytes 73736 | tf_op jit(solution)/shard_map/ppermute | solution.py:275
  13.3 1.6 %collective-permute-start.5 = (bf16[48,256]{1,0:T(8,128)(2,1)S(1)}, bf16[48,256]{1,0:T(8,128)(2,1)S(1)}, u32[]{:S(2)}, u32[]{:S(2)}) collective-permute-start(bf16[48,256]{1,0:T(8,128)(2,1)S(1)} %get-tuple-element.28), channel_id=1, source_target_pairs={{0,1},{1,0},{4,8},{5,4},{8,9},{9,5},{12,13},{13,12},{2,3},{3,2},{6... | collective-permute-start | bytes 73736 | tf_op jit(solution)/shard_map/ppermute | solution.py:275
  13.3 1.5 %copy-start.3 = (f32[48,768]{1,0:T(8,128)S(1)}, f32[48,768]{1,0:T(8,128)}, u32[]{:S(2)}) copy-start(f32[48,768]{1,0:T(8,128)} %gain_ref.1) | copy-start | bytes 442372
  16.6 3.9 %collective-permute-start.9 = (bf16[48,256]{1,0:T(8,128)(2,1)S(1)}, bf16[48,256]{1,0:T(8,128)(2,1)S(1)}, u32[]{:S(2)}, u32[]{:S(2)}) collective-permute-start(bf16[48,256]{1,0:T(8,128)(2,1)S(1)} %solve.1.y_ref), channel_id=1, source_target_pairs={{0,2},{2,0},{1,3},{3,1},{4,6},{6,4},{5,7},{7,5},{8,10},{10,8},{9,1... | collective-permute-start | bytes 73736 | tf_op jit(solution)/shard_map/ppermute | solution.py:38
